TPU v7x, 32 devices: a whole 2x2x4 slice. The times are simulated.
32 devices in a mesh: dp: 4 (over y, x), row: 4 (over z), col: 2 (over core).
Axes of the slice: x: 2, y: 2, z: 4, core: 2. Of those that a mesh axis runs over, the one named last changes fastest.
Arguments:
- layer_input: bfloat16 [8192, 768], P(('dp', 'row'), 'col'), may hold values from -6 to 6
- cotangent: bfloat16 [8192, 768], P(('dp', 'row'), 'col'), may hold values from -6 to 6
- labels: int32 [4], P('dp'), may hold values from 0 to 2
- block_ids: int32 [8192], P('dp'), may hold values from 0 to 63, never falling along the last dimension, each value on 1 to 256 neighbouring positions
- w_query: bfloat16 [768, 768], P('row', 'col'), may hold values from -0.21875 to 0.21875
- b_query: bfloat16 [768], P('col'), may hold values from -1.75 to 1.75
- w_key: bfloat16 [768, 768], P('row', 'col'), may hold values from -0.21875 to 0.21875
- w_value: bfloat16 [768, 768], P('row', 'col'), may hold values from -0.21875 to 0.21875
- b_value: bfloat16 [768], P('col'), may hold values from -0.125 to 0.125
- w_output: bfloat16 [768, 768], P('col', 'row'), may hold values from -6 to 6
- b_output: bfloat16 [768], P('col'), may hold values from -1.75 to 1.75
- ln1_gain: bfloat16 [768], P('col'), may hold values from 0.5 to 1.5
- ln1_bias: bfloat16 [768], P('col'), may hold values from -1.75 to 1.75
- w_inner: bfloat16 [768, 3072], P('row', 'col'), may hold values from -0.21875 to 0.21875
- b_inner: bfloat16 [3072], P('col'), may hold values from -1.75 to 1.75
- w_outer: bfloat16 [3072, 768], P('col', 'row'), may hold values from -0.109375 to 0.109375
- b_outer: bfloat16 [768], P('col'), may hold values from -1.75 to 1.75
- ln2_gain: bfloat16 [768], P('col'), may hold values from 0.5 to 1.5
- ln2_bias: bfloat16 [768], P('col'), may hold values from -1.75 to 1.75
- w_pooler: bfloat16 [768, 768], replicated, may hold values from -0.21875 to 0.21875
- b_pooler: bfloat16 [768], replicated, may hold values from -1.75 to 1.75
- w_classes: bfloat16 [768, 3], replicated, may hold values from -0.4375 to 0.4375
- b_classes: bfloat16 [3], replicated, may hold values from -3 to 3
Outputs:
- output: bfloat16 [8192, 768], P(('dp', 'row'), 'col')
- logits: float32 [4, 3], P('dp')
- grad_input: bfloat16 [8192, 768], P(('dp', 'row'), 'col')
- grad_w_query: float32 [768, 768], P('row', 'col')
- grad_b_query: float32 [768], P('col')
- grad_w_key: float32 [768, 768], P('row', 'col')
- grad_w_value: float32 [768, 768], P('row', 'col')
- grad_b_value: float32 [768], P('col')
- grad_w_output: float32 [768, 768], P('col', 'row')
- grad_b_output: float32 [768], P('col')
- grad_ln1_gain: float32 [768], P('col')
- grad_ln1_bias: float32 [768], P('col')
- grad_w_inner: float32 [768, 3072], P('row', 'col')
- grad_b_inner: float32 [3072], P('col')
- grad_w_outer: float32 [3072, 768], P('col', 'row')
- grad_b_outer: float32 [768], P('col')
- grad_ln2_gain: float32 [768], P('col')
- grad_ln2_bias: float32 [768], P('col')
- grad_w_pooler: float32 [768, 768], replicated
- grad_b_pooler: float32 [768], replicated
- grad_w_classes: float32 [768, 3], replicated
- grad_b_classes: float32 [3], replicated
Inputs may be any that keep to these rules, and one draw needn't show every extreme that they name: `block_ids`: block numbers never fall along the tokens; a block holds 1 to 256 tokens and some block holds exactly 256.
All inputs are finite; a program needn't handle non-finite values.
Results may differ from a plain program's by a relative error of at most 0.02.
Values may be sent and summed in bfloat16 or wider, within the bound.
A program may use at most 192 MiB of HBM per device.

v0:
```python
import jax
import jax.numpy as jnp
from jax import lax
from jax.sharding import PartitionSpec as P

HEAD = 64


highest = lax.Precision.HIGHEST
epsilon = 1e-05
root_half = 0.7071067811865476
inv_root_tau = 0.3989422804014327
masked_score = -1e30


def gelu_exact(values):
    return values * 0.5 * (1.0 + lax.erf(values * root_half))


def gelu_slope(values):
    return 0.5 * (1.0 + lax.erf(values * root_half)) + values * inv_root_tau * jnp.exp(
        -0.5 * values * values
    )


def project(left, right):
    return jnp.dot(left, right, preferred_element_type=jnp.float32)


def contract_first(left, right):
    return lax.dot_general(
        left, right, (((0,), (0,)), ((), ())), preferred_element_type=jnp.float32
    )


def contract_last(left, right):
    return lax.dot_general(
        left, right, (((1,), (1,)), ((), ())), preferred_element_type=jnp.float32
    )


def gather_features(values):
    return lax.all_gather(values, "col", axis=1, tiled=True)


def sum_features(values):
    return lax.psum_scatter(
        values.astype(jnp.bfloat16), "col", scatter_dimension=1, tiled=True
    ).astype(jnp.float32)


def feature_totals(first_part, second_part):
    return lax.psum((jnp.sum(first_part, axis=1), jnp.sum(second_part, axis=1)), "col")


def norm_forward(hidden, gain, shift, features):
    row_total, square_total = feature_totals(hidden, hidden * hidden)
    row_mean = row_total / features
    row_var = square_total / features - row_mean * row_mean
    inv_scale = lax.rsqrt(row_var + epsilon)
    normed = (hidden - row_mean[:, None]) * inv_scale[:, None]
    return (normed * gain + shift, normed, inv_scale)


def norm_backward(grad, normed, inv_scale, gain, features):
    scaled = grad * gain
    first_total, second_total = feature_totals(scaled, scaled * normed)
    return inv_scale[:, None] * (
        scaled - (first_total / features)[:, None] - normed * (second_total / features)[:, None]
    )


def key_split(piece_rows, rows_dev):
    return (piece_rows // rows_dev, rows_dev)


def body(
    layer_input,
    cotangent,
    labels,
    block_ids,
    w_query,
    b_query,
    w_key,
    w_value,
    b_value,
    w_output,
    b_output,
    ln1_gain,
    ln1_bias,
    w_inner,
    b_inner,
    w_outer,
    b_outer,
    ln2_gain,
    ln2_bias,
    w_pooler,
    b_pooler,
    w_classes,
    b_classes,
):
    f32 = jnp.float32
    bf16 = jnp.bfloat16
    rows_dev, feat_col = layer_input.shape
    heads_col = feat_col // HEAD
    features = feat_col * lax.axis_size("col")
    row_index = lax.axis_index("row")
    col_index = lax.axis_index("col")
    seq_index = lax.axis_index("dp")
    seq_count = lax.axis_size("dp")
    score_scale = HEAD ** (-0.5)
    query_ids = lax.dynamic_slice_in_dim(block_ids, row_index * rows_dev, rows_dev)
    last_query = query_ids[rows_dev - 1]
    wq_full, wk_full, wv_full, w1_full = (
        lax.all_gather(w_query, "row", axis=0, tiled=True),
        lax.all_gather(w_key, "row", axis=0, tiled=True),
        lax.all_gather(w_value, "row", axis=0, tiled=True),
        lax.all_gather(w_inner, "row", axis=0, tiled=True),
    )
    wo_full, w2_full = (
        lax.all_gather(w_output, "row", axis=1, tiled=True),
        lax.all_gather(w_outer, "row", axis=1, tiled=True),
    )
    input_whole = gather_features(layer_input)
    queries = (project(input_whole, wq_full) + b_query.astype(f32)).astype(bf16)
    keys_local = project(input_whole, wk_full).astype(bf16)
    values_local = (project(input_whole, wv_full) + b_value.astype(f32)).astype(bf16)
    queries3 = queries.reshape(rows_dev, heads_col, HEAD)
    start_state = (
        jnp.full((heads_col, rows_dev), masked_score, f32),
        jnp.zeros((heads_col, rows_dev), f32),
        jnp.zeros((heads_col, rows_dev, HEAD), f32),
    )
    running = start_state
    keys_piece = lax.all_gather(keys_local, "row", axis=0, tiled=True)
    values_piece = lax.all_gather(values_local, "row", axis=0, tiled=True)
    piece_rows = keys_piece.shape[0]
    number, block_rows = key_split(piece_rows, rows_dev)
    keys4 = keys_piece.reshape(number, block_rows, heads_col, HEAD)
    values4 = values_piece.reshape(number, block_rows, heads_col, HEAD)
    piece_ids = block_ids.reshape(number, block_rows)

    def attend_block_work(state, block_item):
        peak_score, row_mass, accum = state
        keys3, values3, key_ids = block_item
        scores = (
            jnp.einsum("qhd,khd->hqk", queries3, keys3, preferred_element_type=f32) * score_scale
        )
        allowed = (key_ids[None, :] <= query_ids[:, None])[None]
        block_top = jnp.max(jnp.where(allowed, scores, masked_score), axis=2)
        new_peak = jnp.maximum(peak_score, block_top)
        weights = jnp.where(allowed, jnp.exp(scores - new_peak[:, :, None]), 0.0)
        factor = jnp.exp(peak_score - new_peak)
        row_mass = row_mass * factor + jnp.sum(weights, axis=2)
        accum = accum * factor[:, :, None] + jnp.einsum(
            "hqk,khd->hqd", weights.astype(bf16), values3, preferred_element_type=f32
        )
        return (new_peak, row_mass, accum)

    def attend_block_step(state, block_item):
        state = lax.cond(
            block_item[2][0] > last_query, lambda st, item: st, attend_block_work, state, block_item
        )
        return (state, None)

    running, unused = lax.scan(attend_block_step, running, (keys4, values4, piece_ids))
    peak_score, row_mass, accum = running
    mixed = accum / row_mass[:, :, None]
    log_mass = peak_score + jnp.log(row_mass)
    context_low = mixed.transpose(1, 0, 2).reshape(rows_dev, feat_col).astype(bf16)
    attn_branch = sum_features(project(context_low, wo_full))
    hidden_one = layer_input.astype(f32) + attn_branch + b_output.astype(f32)
    gain_one = ln1_gain.astype(f32)
    stream, normed_one, inv_one = norm_forward(hidden_one, gain_one, ln1_bias.astype(f32), features)
    stream_whole = gather_features(stream.astype(bf16))
    pre_act = project(stream_whole, w1_full) + b_inner.astype(f32)
    activ = gelu_exact(pre_act).astype(bf16)
    ffn_branch = sum_features(project(activ, w2_full))
    hidden_two = stream + ffn_branch + b_outer.astype(f32)
    gain_two = ln2_gain.astype(f32)
    result, normed_two, inv_two = norm_forward(hidden_two, gain_two, ln2_bias.astype(f32), features)
    output = result.astype(bf16)
    row_zero = (row_index == 0).astype(f32)
    pool_input = gather_features(output[0:1])
    pooled = jnp.tanh(project(pool_input, w_pooler) + b_pooler.astype(f32))
    classes_f32 = w_classes.astype(f32)
    logits_own = jnp.dot(pooled, classes_f32, precision=highest) + b_classes.astype(f32)
    onehot = (jnp.arange(w_classes.shape[1]) == labels[0]).astype(f32)
    grad_logits = jax.nn.softmax(logits_own, axis=-1) - onehot[None, :]
    g_w_classes = jnp.dot(pooled.T, grad_logits, precision=highest)
    g_b_classes = grad_logits[0]
    grad_pre_pool = jnp.dot(grad_logits, classes_f32.T, precision=highest) * (1.0 - pooled * pooled)
    g_b_pooler = grad_pre_pool[0]
    g_w_pooler = jnp.dot(pool_input.astype(f32).T, grad_pre_pool, precision=highest)
    grad_first = jnp.dot(grad_pre_pool, w_pooler.astype(f32).T, precision=highest)
    first_col = lax.dynamic_slice_in_dim(grad_first[0], col_index * feat_col, feat_col)
    grad_result = cotangent.astype(f32).at[0].add(first_col * row_zero)
    logits_table = lax.dynamic_update_slice_in_dim(
        jnp.zeros((seq_count, w_classes.shape[1]), f32), logits_own * row_zero, seq_index, 0
    )
    g_ln2_gain = jnp.sum(grad_result * normed_two, axis=0)
    g_ln2_bias = jnp.sum(grad_result, axis=0)
    grad_hidden_two = norm_backward(grad_result, normed_two, inv_two, gain_two, features)
    g_b_outer = jnp.sum(grad_hidden_two, axis=0)
    branch_two_whole = gather_features(grad_hidden_two.astype(bf16))
    g_w_outer_full = contract_first(activ, branch_two_whole)
    grad_act = contract_last(branch_two_whole, w2_full)
    grad_pre = (grad_act * gelu_slope(pre_act)).astype(bf16)
    g_b_inner = jnp.sum(grad_pre.astype(f32), axis=0)
    g_w_inner_full = contract_first(stream_whole, grad_pre)
    grad_stream = grad_hidden_two + sum_features(contract_last(grad_pre, w1_full))
    g_ln1_gain = jnp.sum(grad_stream * normed_one, axis=0)
    g_ln1_bias = jnp.sum(grad_stream, axis=0)
    grad_hidden_one = norm_backward(grad_stream, normed_one, inv_one, gain_one, features)
    g_b_output = jnp.sum(grad_hidden_one, axis=0)
    branch_one_whole = gather_features(grad_hidden_one.astype(bf16))
    g_w_output_full = contract_first(context_low, branch_one_whole)
    grad_context = contract_last(branch_one_whole, wo_full).astype(bf16)
    grad_ctx3 = grad_context.reshape(rows_dev, heads_col, HEAD)
    delta = jnp.sum(grad_ctx3.astype(f32).transpose(1, 0, 2) * mixed, axis=2)

    def score_grads(queries_blk, grad_ctx_blk, keys3, values3, allowed, lse_blk, delta_blk):
        scores = (
            jnp.einsum("qhd,khd->hqk", queries_blk, keys3, preferred_element_type=f32) * score_scale
        )
        probs = jnp.where(allowed, jnp.exp(scores - lse_blk[:, :, None]), 0.0)
        grad_probs = jnp.einsum("qhd,khd->hqk", grad_ctx_blk, values3, preferred_element_type=f32)
        grad_scores = (probs * (grad_probs - delta_blk[:, :, None])).astype(bf16)
        return (probs, grad_scores)

    zero_q = jnp.zeros((rows_dev, heads_col, HEAD), f32)
    keys_piece = lax.all_gather(keys_local, "row", axis=0, tiled=True)
    values_piece = lax.all_gather(values_local, "row", axis=0, tiled=True)
    piece_rows = keys_piece.shape[0]
    number, block_rows = key_split(piece_rows, rows_dev)
    keys4 = keys_piece.reshape(number, block_rows, heads_col, HEAD)
    values4 = values_piece.reshape(number, block_rows, heads_col, HEAD)
    piece_ids = block_ids.reshape(number, block_rows)

    def make_block_work(accum_q, block_item):
        keys3, values3, key_ids = block_item
        allowed = (key_ids[None, :] <= query_ids[:, None])[None]
        probs, grad_scores = score_grads(
            queries3, grad_ctx3, keys3, values3, allowed, log_mass, delta
        )
        accum_q = (
            accum_q
            + jnp.einsum("hqk,khd->qhd", grad_scores, keys3, preferred_element_type=f32)
            * score_scale
        )
        part_k = (
            jnp.einsum("hqk,qhd->khd", grad_scores, queries3, preferred_element_type=f32)
            * score_scale
        )
        part_v = jnp.einsum(
            "hqk,qhd->khd", probs.astype(bf16), grad_ctx3, preferred_element_type=f32
        )
        return (accum_q, (part_k, part_v))

    def block_skip(accum_q, block_item):
        empty = jnp.zeros((block_rows, heads_col, HEAD), f32)
        return (accum_q, (empty, empty))

    def make_block_step(accum_q, block_item):
        return lax.cond(
            block_item[2][0] > last_query, block_skip, make_block_work, accum_q, block_item
        )

    grad_q = zero_q
    grad_q, (parts_k, parts_v) = lax.scan(make_block_step, grad_q, (keys4, values4, piece_ids))
    parts_k = parts_k.reshape(piece_rows, feat_col)
    parts_v = parts_v.reshape(piece_rows, feat_col)
    grad_k_all = parts_k
    grad_v_all = parts_v
    back_result = (grad_q, grad_k_all, grad_v_all)
    grad_q3, grad_k_all, grad_v_all = back_result
    grad_keys, grad_values = (
        lax.psum_scatter(
            grad_k_all.astype(jnp.bfloat16), "row", scatter_dimension=0, tiled=True
        ).astype(jnp.float32),
        lax.psum_scatter(
            grad_v_all.astype(jnp.bfloat16), "row", scatter_dimension=0, tiled=True
        ).astype(jnp.float32),
    )
    queries_grad = grad_q3.reshape(rows_dev, feat_col).astype(bf16)
    keys_grad = grad_keys.astype(bf16)
    values_grad = grad_values.astype(bf16)
    g_b_query = jnp.sum(queries_grad.astype(f32), axis=0)
    g_b_value = jnp.sum(values_grad.astype(f32), axis=0)
    g_w_query_full = contract_first(input_whole, queries_grad)
    g_w_key_full = contract_first(input_whole, keys_grad)
    g_w_value_full = contract_first(input_whole, values_grad)
    grad_input_whole = (
        contract_last(queries_grad, wq_full)
        + contract_last(keys_grad, wk_full)
        + contract_last(values_grad, wv_full)
    )
    grad_input = (grad_hidden_one + sum_features(grad_input_whole)).astype(bf16)
    in_rows = w_query.shape[0]
    out_cols = w_output.shape[1]
    (
        sum_wq,
        sum_wk,
        sum_wv,
        sum_w1,
        sum_wo,
        sum_w2,
        g_w_pooler,
        g_b_pooler,
        g_w_classes,
        g_b_classes,
        g_b_query,
        g_b_value,
        g_b_output,
        g_ln1_gain,
        g_ln1_bias,
        g_b_inner,
        g_b_outer,
        g_ln2_gain,
        g_ln2_bias,
        logits_all,
    ) = lax.psum(
        (
            g_w_query_full,
            g_w_key_full,
            g_w_value_full,
            g_w_inner_full,
            g_w_output_full,
            g_w_outer_full,
            g_w_pooler * row_zero,
            g_b_pooler * row_zero,
            g_w_classes * row_zero,
            g_b_classes * row_zero,
            g_b_query,
            g_b_value,
            g_b_output,
            g_ln1_gain,
            g_ln1_bias,
            g_b_inner,
            g_b_outer,
            g_ln2_gain,
            g_ln2_bias,
            logits_table,
        ),
        ("dp", "row"),
    )
    row_start = row_index * in_rows
    col_start = row_index * out_cols
    g_w_query = lax.dynamic_slice_in_dim(sum_wq, row_start, in_rows, 0)
    g_w_key = lax.dynamic_slice_in_dim(sum_wk, row_start, in_rows, 0)
    g_w_value = lax.dynamic_slice_in_dim(sum_wv, row_start, in_rows, 0)
    g_w_inner = lax.dynamic_slice_in_dim(sum_w1, row_start, in_rows, 0)
    g_w_output = lax.dynamic_slice_in_dim(sum_wo, col_start, out_cols, 1)
    g_w_outer = lax.dynamic_slice_in_dim(sum_w2, col_start, out_cols, 1)
    logits = lax.dynamic_slice_in_dim(logits_all, seq_index, 1, 0)
    return (
        output,
        logits,
        grad_input,
        g_w_query,
        g_b_query,
        g_w_key,
        g_w_value,
        g_b_value,
        g_w_output,
        g_b_output,
        g_ln1_gain,
        g_ln1_bias,
        g_w_inner,
        g_b_inner,
        g_w_outer,
        g_b_outer,
        g_ln2_gain,
        g_ln2_bias,
        g_w_pooler,
        g_b_pooler,
        g_w_classes,
        g_b_classes,
    )


def solution(mesh):
    placed = (
        P(("dp", "row"), "col"),
        P(("dp", "row"), "col"),
        P("dp"),
        P("dp"),
        P("row", "col"),
        P("col"),
        P("row", "col"),
        P("row", "col"),
        P("col"),
        P("col", "row"),
        P("col"),
        P("col"),
        P("col"),
        P("row", "col"),
        P("col"),
        P("col", "row"),
        P("col"),
        P("col"),
        P("col"),
        P(),
        P(),
        P(),
        P(),
    )
    return jax.shard_map(
        body,
        mesh=mesh,
        in_specs=placed,
        out_specs=(
            P(("dp", "row"), "col"),
            P("dp", None),
            P(("dp", "row"), "col"),
            P("row", "col"),
            P("col"),
            P("row", "col"),
            P("row", "col"),
            P("col"),
            P("col", "row"),
            P("col"),
            P("col"),
            P("col"),
            P("row", "col"),
            P("col"),
            P("col", "row"),
            P("col"),
            P("col"),
            P("col"),
            P(),
            P(),
            P(),
            P(),
        ),
        check_vma=False,
    )
```

profile of v0, /device:TPU:0, one launch (start us, length us, event | category | flops | bytes accessed | tf_op | source)
XLA Modules:
  0.0 996.6 jit_solution(11116804711149378010)
XLA Ops:
  8.1 18.4 %all_gather.45 = bf16[768,384]{1,0:T(8,128)(2,1)S(1)} all-gather(bf16[192,384]{1,0:T(8,128)(2,1)} %param.40), channel_id=1, replica_groups=mesh['dp'=4,'row'=4,'col'=2] {'row'}, dimensions={0}, use_global_device_ids=true | all-gather | bytes 737280 | tf_op jit(solution)/shard_map/all_gather | solution.py:117
  26.4 2.6 all_gather.41
  30.4 21.4 %all_gather.42 = bf16[768,384]{1,0:T(8,128)(2,1)S(1)} all-gather(bf16[192,384]{1,0:T(8,128)(2,1)S(1)} %copy-done.32), channel_id=1, replica_groups=mesh['dp'=4,'row'=4,'col'=2] {'row'}, dimensions={0}, use_global_device_ids=true | all-gather | bytes 737280 | tf_op jit(solution)/shard_map/all_gather | solution.py:116
  54.7 22.8 %all_gather.44 = bf16[768,384]{1,0:T(8,128)(2,1)S(1)} all-gather(bf16[192,384]{1,0:T(8,128)(2,1)S(1)} %copy-done.33), channel_id=1, replica_groups=mesh['dp'=4,'row'=4,'col'=2] {'row'}, dimensions={0}, use_global_device_ids=true | all-gather | bytes 737280 | tf_op jit(solution)/shard_map/all_gather | solution.py:115
  77.6 17.2 %all_gather.47 = bf16[384,768]{0,1:T(8,128)(2,1)} all-gather(bf16[384,192]{0,1:T(8,128)(2,1)S(1)} %copy-done.34), channel_id=1, replica_groups=mesh['dp'=4,'row'=4,'col'=2] {'row'}, dimensions={1}, use_global_device_ids=true | all-gather | bytes 737280 | tf_op jit(solution)/shard_map/all_gather | solution.py:121
  99.5 3.0 copy.78
  102.5 19.6 %all-gather.5.cloned.1.call-done = bf16[2048,384]{1,0:T(8,128)(2,1)} async-done(((bf16[512,384]{1,0:T(8,128)(2,1)}), bf16[2048,384]{1,0:T(8,128)(2,1)}) %all-gather.5.cloned.1.call-update) | async-done | bytes 1572880 | tf_op jit(solution)/shard_map/all_gather | solution.py:135
  123.8 2.4 reshape.236
  129.0 20.0 %while.32 = (s32[]{:T(128)}, f32[6,512]{1,0:T(8,128)S(1)}, f32[6,512]{1,0:T(8,128)S(1)}, f32[6,512,64]{1,2,0:T(8,128)}, s32[4,512]{1,0:T(4,128)S(1)}, /*index=5*...) while((s32[]{:T(128)}, f32[6,512]{1,0:T(8,128)S(1)}, ...), condition=%wide.region_5.6_spmd, body=%wide.region_0.5_spmd.sunk | while | flops 420616192 | bytes 29172552 | solution.py:166
  130.8 6.3 conditional.4
  133.6 2.6 fusion.8
  138.9 6.3 conditional.4
  141.7 2.6 fusion.8
  151.0 2.6 convolution_convert_fusion.2
  162.2 13.4 %reduce-scatter.19.cloned.1.call-done = bf16[384,512]{1,0:T(8,128)(2,1)} async-done(((bf16[768,512]{1,0:T(8,128)(2,1)}), bf16[384,512]{1,0:T(8,128)(2,1)}) %reduce-scatter.19.cloned.1.call-update) | async-done | bytes 393232
  179.3 3.1 all-reduce.5
  185.1 2.7 all_gather.48
  187.8 40.9 %all-gather.9.cloned.1.call-done = bf16[768,1536]{1,0:T(8,128)(2,1)} async-done(((bf16[192,1536]{1,0:T(8,128)(2,1)}), bf16[768,1536]{1,0:T(8,128)(2,1)}) %all-gather.9.cloned.1.call-update) | async-done | bytes 2359312 | tf_op jit(solution)/shard_map/all_gather | solution.py:118
  228.7 5.6 multiply_convert_fusion
  234.3 45.3 %all-gather.11.cloned.1.call-done = bf16[1536,768]{0,1:T(8,128)(2,1)} async-done(((bf16[1536,192]{0,1:T(8,128)(2,1)}), bf16[1536,768]{0,1:T(8,128)(2,1)}) %all-gather.11.cloned.1.call-update) | async-done | bytes 2359312 | tf_op jit(solution)/shard_map/all_gather | solution.py:122
  279.6 4.4 convolution_convert_fusion.1
  295.4 3.0 fusion.58
  298.5 3.1 all-reduce.4
  316.2 2.4 multiply_reduce_fusion
  318.6 2.4 all-reduce.3
  322.9 2.4 all_gather.52
  325.3 4.6 convert_reduce_fusion
  337.1 8.2 reduce-scatter.23.cloned.1.call-done
  349.4 3.1 all-reduce.2
  356.0 2.7 all_gather.53
  361.9 34.5 %while.33 = (s32[]{:T(128)}, f32[512,6,64]{0,2,1:T(8,128)S(1)}, bf16[4,512,6,64]{1,3,2,0:T(8,128)(2,1)}, bf16[4,512,6,64]{1,3,2,0:T(8,128)(2,1)}, s32[4,512]{1,0...) while((s32[]{:T(128)}, f32[512,6,64]{0,2,1:T(8,128)S(1)}, ...), condition=%wide.region_32.33_spmd, body=%wide.region_29.32_spmd.sunk | while | flops 1023410176 | bytes 35837208 | solution.py:270
  365.1 8.8 conditional.5
  366.4 2.4 fusion.25
  368.8 3.4 fusion.20
  378.1 8.8 conditional.5
  379.4 2.4 fusion.25
  381.8 3.4 fusion.20
  396.4 2.6 copy.81
  400.8 2.6 copy.82
  405.4 5.0 fusion.66
  411.2 43.7 %reduce-scatter.15.cloned.1.call-done = bf16[512,384]{0,1:T(8,128)(2,1)} async-done(((bf16[2048,384]{0,1:T(8,128)(2,1)}), bf16[512,384]{0,1:T(8,128)(2,1)}) %reduce-scatter.15.cloned.1.call-update) | async-done | bytes 393232 | tf_op jit(solution)/shard_map/reduce_scatter | solution.py:278
  456.6 34.9 %reduce-scatter.17.cloned.1.call-done = bf16[512,384]{0,1:T(8,128)(2,1)} async-done(((bf16[2048,384]{0,1:T(8,128)(2,1)}), bf16[512,384]{0,1:T(8,128)(2,1)}) %reduce-scatter.17.cloned.1.call-update) | async-done | bytes 393232 | tf_op jit(solution)/shard_map/reduce_scatter | solution.py:281
  491.5 2.7 add_convert_fusion
  494.2 2.4 copy.96
  498.4 5.1 fusion.65
  510.7 80.1 %all-reduce = (f32[4,3]{1,0:T(4,128)S(1)}, f32[384]{0:T(512)}, f32[384]{0:T(512)}, f32[384]{0:T(512)}, f32[384]{0:T(512)}, /*index=5*/f32[384]{0:T(512)}, f32[15...) all-reduce(f32[4,3]{1,0:T(4,128)S(1)} %dynamic_update_slice.10, ...), channel_id=1, replica_groups=mesh['dp'=4,'row'=4,'col'=2] {'dp','row'}, use_global_device_ids=true, to_apply=%region_16.17 | all-reduce | flops 7695 | bytes 61560 | tf_op jit(solution)/shard_map/psum | solution.py:322
  593.4 381.3 %all-reduce.8.cloned.1.call-done = (f32[768,384]{0,1:T(8,128)}, f32[768,384]{0,1:T(8,128)}, f32[768,384]{0,1:T(8,128)}, f32[384,768]{0,1:T(8,128)}, f32[768,1536...) async-done(((f32[768,384]{0,1:T(8,128)}, f32[768,384]{0,1:T(8,128)}, f32[768,384]{0,1:T(8,128)}, f32[384,768]{0,1:T(8,128)}, f32[768,1536]{1,0:T(8,128)}, ...) | async-done | bytes 16515088 | tf_op jit(solution)/shard_map/psum | solution.py:322
  982.6 2.5 constant_dynamic-slice_fusion.5
  (312 shorter events, 133.2 us)
Async XLA Ops:
  7.2 299.7 %copy-start = (bf16[768,768]{1,0:T(8,128)(2,1)S(1)}, bf16[768,768]{1,0:T(8,128)(2,1)}, u32[]{:S(2)}) copy-start(bf16[768,768]{1,0:T(8,128)(2,1)} %param.52) | copy-start | bytes 3538948
  7.2 23.2 %copy-start.32 = (bf16[192,384]{1,0:T(8,128)(2,1)S(1)}, bf16[192,384]{1,0:T(8,128)(2,1)}, u32[]{:S(2)}) copy-start(bf16[192,384]{1,0:T(8,128)(2,1)} %param.39) | copy-start | bytes 442372
  7.2 88.2 %all-gather.7.cloned.1.call-start = ((), (), s32[]{:S(2)}) async-start(), calls=%async_computation.7 | async-start | bytes 1966080 | tf_op jit(solution)/shard_map/all_gather | solution.py:136
  26.4 27.5 %copy-start.19 = (bf16[768,384]{1,0:T(8,128)(2,1)}, bf16[768,384]{1,0:T(8,128)(2,1)S(1)}, u32[]{:S(2)}) copy-start(bf16[768,384]{1,0:T(8,128)(2,1)S(1)} %all_gather.45) | copy-start | bytes 1769476
  29.0 65.8 %copy-start.4 = (bf16[512,768]{1,0:T(8,128)(2,1)}, bf16[512,768]{1,0:T(8,128)(2,1)S(1)}, u32[]{:S(2)}) copy-start(bf16[512,768]{1,0:T(8,128)(2,1)S(1)} %all_gather.41) | copy-start | bytes 2359300
  29.0 25.0 %copy-start.51 = (s32[2048]{0:T(1024)S(1)}, s32[2048]{0:T(1024)}, u32[]{:S(2)}) copy-start(s32[2048]{0:T(1024)} %param.36) | copy-start | bytes 24580
  29.0 25.7 %copy-start.64 = (bf16[384]{0:T(512)(128)(2,1)S(1)}, bf16[384]{0:T(512)(128)(2,1)}, u32[]{:S(2)}) copy-start(bf16[384]{0:T(512)(128)(2,1)} %param.38) | copy-start | bytes 2308
  29.0 25.7 %copy-start.33 = (bf16[192,384]{1,0:T(8,128)(2,1)S(1)}, bf16[192,384]{1,0:T(8,128)(2,1)}, u32[]{:S(2)}) copy-start(bf16[192,384]{1,0:T(8,128)(2,1)} %param.37) | copy-start | bytes 442372
  30.3 47.2 %copy-start.34 = (bf16[384,192]{0,1:T(8,128)(2,1)S(1)}, bf16[384,192]{0,1:T(8,128)(2,1)}, u32[]{:S(2)}) copy-start(bf16[384,192]{0,1:T(8,128)(2,1)} %param.42) | copy-start | bytes 442372
  30.4 91.7 %all-gather.5.cloned.1.call-start = ((), (), s32[]{:S(2)}) async-start(), calls=%async_computation.6 | async-start | bytes 1966080 | tf_op jit(solution)/shard_map/all_gather | solution.py:135
  54.0 121.6 %reduce-scatter.19.cloned.1.call-start = ((), (), s32[]{:S(2)}) async-start(), calls=%async_computation.12 | async-start | bytes 1179648
  77.6 17.8 %copy-start.21 = (bf16[768,384]{1,0:T(8,128)(2,1)}, bf16[768,384]{1,0:T(8,128)(2,1)S(1)}, u32[]{:S(2)}) copy-start(bf16[768,384]{1,0:T(8,128)(2,1)S(1)} %all_gather.44) | copy-start | bytes 1769476
  153.6 23.9 %copy-start.2 = (bf16[512,384]{1,0:T(8,128)(2,1)S(1)}, bf16[512,384]{1,0:T(8,128)(2,1)}, u32[]{:S(2)}) copy-start(bf16[512,384]{1,0:T(8,128)(2,1)} %param.33) | copy-start | bytes 1179652
  155.9 72.8 %all-gather.9.cloned.1.call-start = ((), (), s32[]{:S(2)}) async-start(), calls=%async_computation.8 | async-start | bytes 2949120 | tf_op jit(solution)/shard_map/all_gather | solution.py:118
  156.5 123.1 %all-gather.11.cloned.1.call-start = ((), (), s32[]{:S(2)}) async-start(), calls=%async_computation.9 | async-start | bytes 2949120 | tf_op jit(solution)/shard_map/all_gather | solution.py:122
  157.1 136.4 %reduce-scatter.21.cloned.1.call-start = ((), (), s32[]{:S(2)}) async-start(), calls=%async_computation.13 | async-start | bytes 1179648
  286.3 59.0 %reduce-scatter.23.cloned.1.call-start = ((), (), s32[]{:S(2)}) async-start(), calls=%async_computation.14 | async-start | bytes 1179648
  301.6 5.5 copy-start.60
  301.6 5.6 copy-start.67
  301.6 5.6 copy-start.68
  302.4 10.6 %copy-start.46 = (f32[512]{0:T(512)}, f32[512]{0:T(512)S(1)}, u32[]{:S(2)}) copy-start(f32[512]{0:T(512)S(1)} %get-tuple-element.574) | copy-start | bytes 6148
  302.4 11.7 %copy-start.47 = (f32[512]{0:T(512)}, f32[512]{0:T(512)S(1)}, u32[]{:S(2)}) copy-start(f32[512]{0:T(512)S(1)} %get-tuple-element.575) | copy-start | bytes 6148
  307.2 4.6 copy-start.37
  321.0 4.3 copy-start.66
  325.3 4.6 copy-start.17
  325.3 5.7 copy-start.65
  333.3 13.9 %copy-start.3 = (bf16[512,384]{1,0:T(8,128)(2,1)S(1)}, bf16[512,384]{1,0:T(8,128)(2,1)}, u32[]{:S(2)}) copy-start(bf16[512,384]{1,0:T(8,128)(2,1)} %copy.91) | copy-start | bytes 1179652
  335.7 119.1 %reduce-scatter.15.cloned.1.call-start = ((), (), s32[]{:S(2)}) async-start(), calls=%async_computation.10 | async-start | bytes 1966080 | tf_op jit(solution)/shard_map/reduce_scatter | solution.py:278
  337.1 16.8 %copy-start.36 = (f32[384]{0:T(512)S(1)}, f32[384]{0:T(512)}, u32[]{:S(2)}) copy-start(f32[384]{0:T(512)} %convert_element_type.180) | copy-start | bytes 4612
  337.1 16.8 %copy-start.39 = (f32[384]{0:T(512)S(1)}, f32[384]{0:T(512)}, u32[]{:S(2)}) copy-start(f32[384]{0:T(512)} %convert_element_type.181) | copy-start | bytes 4612
  337.1 16.8 %copy-start.41 = (f32[512]{0:T(512)S(1)}, f32[512]{0:T(512)}, u32[]{:S(2)}) copy-start(f32[512]{0:T(512)} %copy-done.40) | copy-start | bytes 6148
  337.1 16.8 %copy-start.43 = (f32[512]{0:T(512)S(1)}, f32[512]{0:T(512)}, u32[]{:S(2)}) copy-start(f32[512]{0:T(512)} %copy-done.42) | copy-start | bytes 6148
  353.9 4.8 copy-start.23
  356.0 5.8 copy-start.9
  356.0 4.0 copy-start.8
  356.0 4.0 copy-start.28
  356.0 5.9 copy-start.31
  358.8 3.1 copy-start.15
  400.7 90.8 %reduce-scatter.17.cloned.1.call-start = ((), (), s32[]{:S(2)}) async-start(), calls=%async_computation.11 | async-start | bytes 1966080 | tf_op jit(solution)/shard_map/reduce_scatter | solution.py:281
  405.0 186.3 %reduce-scatter.25.cloned.1.call-start = ((), (), s32[]{:S(2)}) async-start(), calls=%async_computation.15 | async-start | bytes 1179648
  405.4 5.2 copy-start.22
  494.2 4.2 copy-start.14
  496.6 478.0 %all-reduce.8.cloned.1.call-start = ((), (), s32[]{:S(2)}) async-start(), calls=%async_computation.16 | async-start | bytes 33030144 | tf_op jit(solution)/shard_map/psum | solution.py:322
  498.4 5.1 copy-start.13
  498.4 5.1 copy-start.16
  503.5 3.2 copy-start.11
  509.7 82.8 %copy-start.10 = (f32[512,384]{1,0:T(8,128)S(1)}, f32[512,384]{1,0:T(8,128)}, u32[]{:S(2)}) copy-start(f32[512,384]{1,0:T(8,128)} %copy-done.9) | copy-start | bytes 2359300
  982.6 4.9 copy-start.24
  (34 other events, 39.9 us)
Sparse Core Ops, SparseCore 0:
  30.5 53.0 all-gather.6
  85.8 36.3 all-gather.4
  156.0 19.4 reduce-scatter.18
  177.1 51.6 all-gather.8
  230.2 49.2 all-gather.10
  286.4 7.0 reduce-scatter.20
  335.8 9.4 reduce-scatter.22
  400.8 53.9 reduce-scatter.14
  457.3 34.2 reduce-scatter.16
  496.8 7.2 reduce-scatter.24
  511.6 462.9 all-reduce.7
where the time goes:
time: 1010 us; the launch traced here: 997 us
  waiting for transfers between devices  589 us (58%)
  blocking collectives  184 us (18%)
  local copies, waits for them, and re-layouts  78.4 us (8%)
  matrix products  72.1 us (7%)
  other arithmetic  45.8 us (5%)
  between operations  15.7 us (2%)
  loops' own time  10.9 us (1%)
    psum x1, waiting for transfers between devices, body(): lax.psum((g_w_query_full, g_w_key_full, g_w_value_full, g_w_inner_full, g...  381 us
    psum x1, blocking collectives, body(): lax.psum((g_w_query_full, g_w_key_full, g_w_value_full, g_w_inner_full, g...  80.1 us
    all_gather x1, waiting for transfers between devices, body(): lax.all_gather(w_outer, 'row', axis=1, tiled=True)  45.3 us
    reduce_scatter x1, waiting for transfers between devices, body(): lax.psum_scatter(grad_k_all.astype(jnp.bfloat16), 'row', scatter_dimensio...  43.7 us
    all_gather x1, waiting for transfers between devices, body(): lax.all_gather(w_inner, 'row', axis=0, tiled=True)  40.9 us
    reduce_scatter x1, waiting for transfers between devices, body(): lax.psum_scatter(grad_v_all.astype(jnp.bfloat16), 'row', scatter_dimensio...  34.9 us
    unnamed x148, local copies, waits for them, and re-layouts  30.7 us
    unnamed x15, waiting for transfers between devices  23.5 us
  transfers between devices with their start and end apart: 11, of which 9 were waited for; matrix products, arithmetic and copies ran while one was open for 6% of the time, Pallas kernels for 0%

commit v1 on v0

--- a/solution.py
+++ b/solution.py
@@ -1,6 +1,10 @@
+import functools
+
 import jax
 import jax.numpy as jnp
 from jax import lax
+from jax.experimental import pallas as pl
+from jax.experimental.pallas import tpu as pltpu
 from jax.sharding import PartitionSpec as P
 
 HEAD = 64
@@ -379,6 +383,881 @@
     )
 
 
+MESH_IDS = pl.DeviceIdType.MESH
+ROWS = 4
+VMEM_BYTES = 64000 * 1024
+
+
+def place():
+    return lax.axis_index("dp"), lax.axis_index("row"), lax.axis_index("col")
+
+
+class Links:
+    def __init__(self, send, recv):
+        self.send, self.recv = send, recv
+        self.sends, self.recvs, self.open = 0, 0, []
+
+    def slots(self, count):
+        base = self.recvs
+        self.recvs += count
+        return base
+
+    def push(self, source, target, slot, device, when=None):
+        copy = pltpu.make_async_remote_copy(
+            src_ref=source,
+            dst_ref=target,
+            send_sem=self.send.at[self.sends],
+            recv_sem=self.recv.at[slot],
+            device_id=device,
+            device_id_type=MESH_IDS,
+        )
+        self.sends += 1
+        if when is None:
+            copy.start()
+        else:
+            pl.when(when)(lambda: copy.start())
+        self.open.append((copy, when))
+
+    def arrive(self, target, slot, device, when=None):
+        copy = pltpu.make_async_remote_copy(
+            src_ref=target,
+            dst_ref=target,
+            send_sem=self.send.at[0],
+            recv_sem=self.recv.at[slot],
+            device_id=device,
+            device_id_type=MESH_IDS,
+        )
+        if when is None:
+            copy.wait_recv()
+        else:
+            pl.when(when)(lambda: copy.wait_recv())
+
+    def drain(self):
+        for copy, when in self.open:
+            if when is None:
+                copy.wait_send()
+            else:
+                pl.when(when)(lambda copy=copy: copy.wait_send())
+        self.open = []
+
+
+def meet(devices):
+    barrier = pltpu.get_barrier_semaphore()
+    for device in devices:
+        pl.semaphore_signal(barrier, inc=1, device_id=device, device_id_type=MESH_IDS)
+    pl.semaphore_wait(barrier, len(devices))
+
+
+def within(value):
+    return (value >= 0) & (value < ROWS)
+
+
+def steps_of_line(row):
+    for step in (1, 2, 3):
+        for way in (1, -1):
+            source = row - way * step
+            yield step, way, (3 - step if way == 1 else step - 1), source, within(source)
+
+
+def columns(col, width):
+    return pl.ds(pl.multiple_of(col * width, 128), width)
+
+
+def gather_kernel(widths, x, cot, vec, *refs):
+    count = len(widths)
+    shards, refs = refs[:count], refs[count:]
+    x_all, cot_own, vec_all = refs[:3]
+    fulls = refs[3 : 3 + count]
+    send, recv, local = refs[3 + count :]
+    dp, row, col = place()
+    links = Links(send, recv)
+    feat = x.shape[1]
+    mate = (dp, row, 1 - col)
+    at_row = lambda other: (dp, other, col)
+    at_dp = lambda flip: (dp ^ flip, row, col)
+    meet([at_row(lax.rem(row + k, ROWS)) for k in (1, 2, 3)] + [at_dp(1), at_dp(2), mate])
+
+    half = x.shape[0] // 2
+    mine = lax.rem(row + col, 2)
+    x_at = lambda k: x_all.at[k, :, columns(col, feat)]
+    w_at = lambda i, k, q: fulls[i].at[k, q, :, columns(col, widths[i])]
+    row_at = lambda i, k: fulls[i].at[k, :, :, columns(col, widths[i])]
+    x_mate_at = lambda k: x_all.at[k, :, columns(1 - col, feat)]
+    row_mate_at = lambda i, k: fulls[i].at[k, :, :, columns(1 - col, widths[i])]
+
+    line_x = links.slots(3)
+    line_w = [links.slots(3) for _ in widths]
+    first_w = [links.slots(3) for _ in widths]
+    second_w = [links.slots(6) for _ in widths]
+    mate_x = links.slots(4)
+    mate_w = [links.slots(4) for _ in widths]
+    mate_cot, mate_vec = links.slots(1), links.slots(1)
+
+    copies = [pltpu.make_async_copy(x, x_at(row), local.at[0])]
+    copies += [
+        pltpu.make_async_copy(shards[i], row_at(i, row), local.at[1 + i]) for i in range(count)
+    ]
+    copies += [
+        pltpu.make_async_copy(
+            cot.at[pl.ds(pl.multiple_of(mine * half, 128), half)],
+            cot_own.at[:, columns(col, feat)],
+            local.at[1 + count],
+        ),
+        pltpu.make_async_copy(vec, vec_all.at[col], local.at[2 + count]),
+    ]
+
+    def relay(step):
+        for way in (1, -1):
+            held, onward = row - way * (step - 1), row + way
+            ok = within(held) & within(onward)
+            slot = 3 - step if way == 1 else step - 1
+            links.push(x if step == 1 else x_at(held), x_at(held), line_x + slot, at_row(onward), ok)
+            for i in range(count):
+                source = shards[i].at[dp] if step == 1 else w_at(i, held, dp)
+                links.push(source, w_at(i, held, dp), line_w[i] + slot, at_row(onward), ok)
+
+    relay(1)
+    links.push(x, x_at(row), mate_x, mate)
+    links.push(
+        cot.at[pl.ds(pl.multiple_of((1 - mine) * half, 128), half)],
+        cot_own.at[:, columns(col, feat)],
+        mate_cot,
+        mate,
+    )
+    links.push(vec, vec_all.at[col], mate_vec, mate)
+    for i in range(count):
+        links.push(shards[i], row_at(i, row), mate_w[i], mate)
+    for copy in copies:
+        copy.start()
+    steps = list(steps_of_line(row))
+    turn = lambda i, slot: (1, 2) if (i + slot) % 2 == 0 else (2, 1)
+    for step in (1, 2, 3):
+        for at_step, way, slot, k, ok in steps:
+            if at_step != step:
+                continue
+            links.arrive(x_at(k), line_x + slot, mate, ok)
+            for i in range(count):
+                links.arrive(w_at(i, k, dp), line_w[i] + slot, mate, ok)
+        if step < 3:
+            relay(step + 1)
+        for at_step, way, slot, k, ok in steps:
+            if at_step != step:
+                continue
+            links.push(x_at(k), x_at(k), mate_x + 1 + slot, mate, ok)
+            for i in range(count):
+                one, two = turn(i, slot)
+                links.push(w_at(i, k, dp), w_at(i, k, dp), first_w[i] + slot, at_dp(one), ok)
+    for slot in range(3):
+        k = lax.rem(row + slot + 1, ROWS)
+        for i in range(count):
+            one, two = turn(i, slot)
+            links.arrive(w_at(i, k, dp ^ one), first_w[i] + slot, mate)
+            links.push(w_at(i, k, dp), w_at(i, k, dp), second_w[i] + 2 * slot, at_dp(two))
+            links.push(
+                w_at(i, k, dp ^ one), w_at(i, k, dp ^ one), second_w[i] + 2 * slot + 1, at_dp(two)
+            )
+    for slot in range(3):
+        k = lax.rem(row + slot + 1, ROWS)
+        for i in range(count):
+            one, two = turn(i, slot)
+            links.arrive(w_at(i, k, dp ^ two), second_w[i] + 2 * slot, mate)
+            links.arrive(w_at(i, k, dp ^ 3), second_w[i] + 2 * slot + 1, mate)
+            links.push(row_at(i, k), row_at(i, k), mate_w[i] + 1 + slot, mate)
+    links.arrive(x_mate_at(row), mate_x, mate)
+    links.arrive(cot_own.at[:, columns(1 - col, feat)], mate_cot, mate)
+    links.arrive(vec_all.at[1 - col], mate_vec, mate)
+    for i in range(count):
+        links.arrive(row_mate_at(i, row), mate_w[i], mate)
+    for slot in range(3):
+        k = lax.rem(row + slot + 1, ROWS)
+        links.arrive(x_mate_at(k), mate_x + 1 + slot, mate)
+        for i in range(count):
+            links.arrive(row_mate_at(i, k), mate_w[i] + 1 + slot, mate)
+    for copy in copies:
+        copy.wait()
+    links.drain()
+
+
+IN_VMEM = pl.BlockSpec(memory_space=pltpu.VMEM)
+IN_PLACE = pl.BlockSpec(memory_space=pl.ANY)
+
+
+def comm_params(number):
+    return pltpu.CompilerParams(
+        collective_id=number, has_side_effects=True, vmem_limit_bytes=VMEM_BYTES
+    )
+
+
+def gather_all(x, cot, vec, shards):
+    widths = [shard.shape[1] for shard in shards]
+    rows, feat = x.shape
+    low = x.dtype
+    part = shards[0].shape[0] // 4
+    shapes = [
+        jax.ShapeDtypeStruct((ROWS, rows, 2 * feat), low),
+        jax.ShapeDtypeStruct((rows // 2, 2 * feat), low),
+        jax.ShapeDtypeStruct((2,) + vec.shape, vec.dtype),
+    ] + [jax.ShapeDtypeStruct((ROWS, 4, part, 2 * width), low) for width in widths]
+    return pl.pallas_call(
+        functools.partial(gather_kernel, widths),
+        out_shape=shapes,
+        in_specs=[IN_VMEM] * (3 + len(shards)),
+        out_specs=[IN_PLACE] * len(shapes),
+        scratch_shapes=[
+            pltpu.SemaphoreType.DMA((160,)),
+            pltpu.SemaphoreType.DMA((96,)),
+            pltpu.SemaphoreType.DMA((16,)),
+        ],
+        compiler_params=comm_params(1),
+        name="gather_all",
+    )(x, cot, vec, *[shard.reshape(4, part, -1) for shard in shards])
+
+
+def swap_kernel(split, *refs):
+    blocks, out_blocks = refs[0], refs[1 + split]
+    send, recv, local = refs[-3:]
+    dp, row, col = place()
+    links = Links(send, recv)
+    mate = (dp, row, 1 - col)
+    peers = [lax.rem(row + k, ROWS) for k in (1, 2, 3)]
+    meet([(dp, peer, col) for peer in peers] + ([mate] if split else []))
+    base = links.slots(4)
+    for number, peer in enumerate(peers):
+        links.push(blocks.at[peer], out_blocks.at[row], base + 2 - number, (dp, peer, col))
+    keep = [pltpu.make_async_copy(blocks.at[row], out_blocks.at[row], local.at[0])]
+    if split:
+        whole, halves = refs[1], refs[3]
+        half, feat = whole.shape[0], whole.shape[1] // 2
+        mine = lax.rem(row + col, 2)
+        own_rows = pl.ds(pl.multiple_of(mine * half, 128), half)
+        keep.append(
+            pltpu.make_async_copy(
+                whole.at[:, columns(col, feat)], halves.at[own_rows], local.at[1]
+            )
+        )
+        links.push(whole.at[:, columns(1 - col, feat)], halves.at[own_rows], base + 3, mate)
+        other_rows = pl.ds(pl.multiple_of((1 - mine) * half, 128), half)
+    for copy in keep:
+        copy.start()
+    for number, peer in enumerate(peers):
+        links.arrive(out_blocks.at[peer], base + number, mate)
+    if split:
+        links.arrive(halves.at[other_rows], base + 3, mate)
+    for copy in keep:
+        copy.wait()
+    links.drain()
+
+
+def swap_blocks(blocks, number, whole=None):
+    split = 0 if whole is None else 1
+    shapes = [jax.ShapeDtypeStruct(blocks.shape, blocks.dtype)]
+    if split:
+        shapes.append(
+            jax.ShapeDtypeStruct((2 * whole.shape[0], whole.shape[1] // 2), whole.dtype)
+        )
+    return pl.pallas_call(
+        functools.partial(swap_kernel, split),
+        out_shape=shapes,
+        in_specs=[IN_VMEM] * (1 + split),
+        out_specs=[IN_VMEM] * (1 + split),
+        scratch_shapes=[
+            pltpu.SemaphoreType.DMA((4,)),
+            pltpu.SemaphoreType.DMA((4,)),
+            pltpu.SemaphoreType.DMA((2,)),
+        ],
+        compiler_params=comm_params(number),
+        name="swap_blocks",
+    )(blocks, *([whole] if split else []))
+
+
+def add_into(total, *others):
+    def one(step, carry):
+        value = total[step].astype(jnp.float32)
+        for other in others:
+            value = value + other[step].astype(jnp.float32)
+        total[step] = value.astype(total.dtype)
+        return carry
+
+    lax.fori_loop(0, total.shape[0], one, 0)
+
+
+def reduce_kernel(count, *refs):
+    grads, refs = refs[:count], refs[count:]
+    gq, dx, vec = refs[:3]
+    outs, refs = refs[3 : 3 + count], refs[3 + count :]
+    out_q, out_x, out_vec = refs[:3]
+    refs = refs[3:]
+    sums, refs = refs[:count], refs[count:]
+    first, refs = refs[: count + 1], refs[count + 1 :]
+    second, refs = refs[: count + 1], refs[count + 1 :]
+    lines, refs = refs[:count], refs[count:]
+    sum_q, all_q, sum_x, line_x, vec_mate, vec_line, vec_flat, send, recv = refs
+    dp, row, col = place()
+    links = Links(send, recv)
+    mate = (dp, row, 1 - col)
+    peers = [lax.rem(row + k, ROWS) for k in (1, 2, 3)]
+    at_row = lambda other: (dp, other, col)
+    at_dp = lambda flip: (dp ^ flip, row, col)
+    owner = row // 2
+    meet(
+        [at_row(peer) for peer in peers]
+        + [at_dp(1), at_dp(2), mate]
+        + [(dp, peer, 1 - col) for peer in peers]
+    )
+    widths = [grad.shape[3] // 2 for grad in grads]
+    feat = dx.shape[2] // 2
+    turns = [(1, 2) if i % 2 == 0 else (2, 1) for i in range(count + 1)]
+
+    slot_x, slot_q, slot_v = links.slots(1), links.slots(1), links.slots(1)
+    slot_g = [links.slots(1) for _ in grads]
+    links.push(vec, vec_mate, slot_v, mate)
+    links.push(dx.at[:, :, columns(1 - col, feat)], sum_x, slot_x, mate)
+    links.push(gq.at[:, 1 - col], sum_q, slot_q, mate)
+    for i in range(count):
+        links.push(grads[i].at[:, :, :, columns(1 - col, widths[i])], sums[i], slot_g[i], mate)
+
+    links.arrive(vec_mate, slot_v, mate)
+    out_vec[...] = vec[...] + vec_mate[...]
+    slot_vl = links.slots(3)
+    for n, peer in enumerate(peers):
+        links.push(out_vec, vec_line.at[2 - n], slot_vl + 2 - n, at_row(peer))
+
+    links.arrive(sum_x, slot_x, mate)
+    tile = dx.shape[1] // 4
+
+    def add_x(step, carry):
+        rows = pl.ds(pl.multiple_of((step % 4) * tile, 128), tile)
+        sum_x[step // 4, rows] = (
+            sum_x[step // 4, rows].astype(jnp.float32)
+            + dx[step // 4, rows, columns(col, feat)].astype(jnp.float32)
+        ).astype(sum_x.dtype)
+        return carry
+
+    lax.fori_loop(0, 16, add_x, 0)
+    slot_xl = links.slots(3)
+    for n, peer in enumerate(peers):
+        links.push(sum_x.at[peer], line_x.at[2 - n], slot_xl + 2 - n, at_row(peer))
+
+    links.arrive(sum_q, slot_q, mate)
+
+    def add_q(step, carry):
+        sum_q[step] = (
+            sum_q[step].astype(jnp.float32) + gq[step, col].astype(jnp.float32)
+        ).astype(sum_q.dtype)
+        return carry
+
+    lax.fori_loop(0, 4, add_q, 0)
+    slot_ql = links.slots(4)
+    side = lax.rem(row, 2)
+    own_part = all_q.at[side, pl.ds(2 * col, 2)]
+    at_home = owner == col
+
+    def keep_own():
+        own_part[...] = sum_q[row]
+
+    pl.when(at_home)(keep_own)
+    links.push(sum_q.at[row], own_part, slot_ql + 2 * side + col, mate, jnp.logical_not(at_home))
+    for peer in peers:
+        links.push(sum_q.at[peer], own_part, slot_ql + 2 * side + col, (dp, peer, owner))
+
+    def send_first(i, total):
+        one, two = turns[i]
+        base = links.slots(2)
+        links.push(total.at[:, dp ^ one], first[i].at[0], base, at_dp(one))
+        links.push(total.at[:, dp ^ 3], first[i].at[1], base + 1, at_dp(one))
+        return base
+
+    def send_second(i, total, base):
+        one, two = turns[i]
+        links.arrive(first[i].at[1], base + 1, mate)
+        add_into(total.at[:, dp ^ two], first[i].at[1])
+        slot = links.slots(1)
+        links.push(total.at[:, dp ^ two], second[i], slot, at_dp(two))
+        links.arrive(first[i].at[0], base, mate)
+        add_into(total.at[:, dp], first[i].at[0])
+        return slot
+
+    def share(i, out):
+        one, two = turns[i]
+        base = links.slots(3)
+        links.push(out.at[dp], out.at[dp], base, at_dp(two))
+        links.push(out.at[dp], out.at[dp], base + 1, at_dp(one))
+        links.arrive(out.at[dp ^ two], base, mate)
+        links.push(out.at[dp ^ two], out.at[dp ^ two], base + 2, at_dp(one))
+        return base
+
+    def shared(i, out, base):
+        one, two = turns[i]
+        links.arrive(out.at[dp ^ one], base + 1, mate)
+        links.arrive(out.at[dp ^ 3], base + 2, mate)
+
+    started = []
+    for i in range(count):
+        links.arrive(sums[i], slot_g[i], mate)
+        width = widths[i]
+
+        def add_g(step, carry, i=i, width=width):
+            k, q = step // 4, step % 4
+            sums[i][k, q] = (
+                sums[i][k, q].astype(jnp.float32)
+                + grads[i][k, q, :, columns(col, width)].astype(jnp.float32)
+            ).astype(sums[i].dtype)
+            return carry
+
+        lax.fori_loop(0, 16, add_g, 0)
+        started.append(send_first(i, sums[i]))
+    for j in range(2):
+        for e in range(2):
+            here = (row == 2 * col + j) & (col == e)
+            links.arrive(
+                all_q.at[j, pl.ds(2 * e, 2)], slot_ql + 2 * j + e, mate, jnp.logical_not(here)
+            )
+    started.append(send_first(count, all_q))
+
+    for n in range(3):
+        links.arrive(vec_line.at[n], slot_vl + n, mate)
+    vec_sum = out_vec[...] + vec_line[0] + vec_line[1] + vec_line[2]
+    vec_mate[...] = vec_sum
+    slot_v1 = links.slots(2)
+    links.push(vec_mate, vec_flat.at[0], slot_v1, at_dp(1))
+
+    totals = list(sums) + [all_q]
+    started = [send_second(i, totals[i], started[i]) for i in range(count + 1)]
+    slot_z = []
+    for i in range(count + 1):
+        links.arrive(second[i], started[i], mate)
+        add_into(totals[i].at[:, dp], second[i])
+        if i < count:
+            base = links.slots(3)
+            for n, peer in enumerate(peers):
+                links.push(
+                    sums[i].at[peer, dp], lines[i].at[2 - n], base + 2 - n, at_row(peer)
+                )
+            slot_z.append(base)
+        else:
+            for j in range(2):
+                out_q[dp, j] = all_q[j, dp]
+            slot_share_q = share(count, out_q)
+
+    links.arrive(vec_flat.at[0], slot_v1, mate)
+    vec_line[0] = vec_mate[...] + vec_flat[0]
+    links.push(vec_line.at[0], vec_flat.at[1], slot_v1 + 1, at_dp(2))
+
+    for n in range(3):
+        links.arrive(line_x.at[n], slot_xl + n, mate)
+
+    def finish_x(step, carry):
+        rows = pl.ds(pl.multiple_of(step * tile, 128), tile)
+        value = sum_x[row, rows].astype(jnp.float32)
+        for n in range(3):
+            value = value + line_x[n, rows].astype(jnp.float32)
+        out_x[rows] = value.astype(out_x.dtype)
+        return carry
+
+    lax.fori_loop(0, 4, finish_x, 0)
+    shares = []
+    for i in range(count):
+        for n in range(3):
+            links.arrive(lines[i].at[n], slot_z[i] + n, mate)
+        value = sums[i][row, dp].astype(jnp.float32)
+        for n in range(3):
+            value = value + lines[i][n].astype(jnp.float32)
+        outs[i][dp] = value.astype(outs[i].dtype)
+        shares.append(share(i, outs[i]))
+    links.arrive(vec_flat.at[1], slot_v1 + 1, mate)
+    vec_total = vec_line[0] + vec_flat[1]
+    for i in range(count):
+        shared(i, outs[i], shares[i])
+    shared(count, out_q, slot_share_q)
+    links.drain()
+    out_vec[...] = vec_total
+
+
+def reduce_all(grads, gq, dx, vec):
+    count = len(grads)
+    low = dx.dtype
+    depth = grads[0].shape[0]
+    part = depth // ROWS // 4
+    widths = [grad.shape[1] // 2 for grad in grads]
+    wide = gq.shape[1]
+    rows, feat = dx.shape[0] // ROWS, dx.shape[1] // 2
+    blocks = lambda lead, width: (lead, 4, part, width)
+    outs = [jax.ShapeDtypeStruct((4, part, width), low) for width in widths] + [
+        jax.ShapeDtypeStruct((4, 2, part, wide), low),
+        jax.ShapeDtypeStruct((rows, feat), low),
+        jax.ShapeDtypeStruct(vec.shape, vec.dtype),
+    ]
+    every = [(ROWS, width) for width in widths] + [(2, wide)]
+    return pl.pallas_call(
+        functools.partial(reduce_kernel, count),
+        out_shape=outs,
+        in_specs=[IN_VMEM] * (count + 3),
+        out_specs=[IN_VMEM] * len(outs),
+        scratch_shapes=[pltpu.VMEM(blocks(ROWS, width), low) for width in widths]
+        + [pltpu.VMEM((2, lead, part, width), low) for lead, width in every]
+        + [pltpu.VMEM((lead, part, width), low) for lead, width in every]
+        + [pltpu.VMEM((3, part, width), low) for width in widths]
+        + [
+            pltpu.VMEM((ROWS, 2, part, wide), low),
+            pltpu.VMEM((2, 4, part, wide), low),
+            pltpu.VMEM((ROWS, rows, feat), low),
+            pltpu.VMEM((3, rows, feat), low),
+            pltpu.VMEM(vec.shape, vec.dtype),
+            pltpu.VMEM((3,) + vec.shape, vec.dtype),
+            pltpu.VMEM((2,) + vec.shape, vec.dtype),
+            pltpu.SemaphoreType.DMA((96,)),
+            pltpu.SemaphoreType.DMA((96,)),
+        ],
+        compiler_params=comm_params(4),
+        name="reduce_all",
+    )(
+        *[grad.reshape(ROWS, 4, part, 2 * width) for grad, width in zip(grads, widths)],
+        gq.reshape(ROWS, 2, 2, part, wide),
+        dx.reshape(ROWS, rows, 2 * feat),
+        vec,
+    )
+
+
+TILE = 256
+NEAR = 3
+
+
+def nt(left, right):
+    return lax.dot_general(
+        left, right, (((1,), (1,)), ((), ())), preferred_element_type=jnp.float32
+    )
+
+
+def nn(left, right):
+    return jnp.dot(left, right, preferred_element_type=jnp.float32)
+
+
+def attend_kernel(
+    heads, x, weights, bias_q, bias_v, ids_col, ids_row,
+    q_out, k_out, kt_out, v_out, vt_out, mixed_out, low_out, lse_out,
+):
+    width = heads * HEAD
+    row_tiles = x.shape[0] // TILE
+    col = lax.axis_index("col")
+    low = x.dtype
+
+    def project_keys(step, carry):
+        rows = pl.ds(pl.multiple_of(step * TILE, TILE), TILE)
+        both = nn(x[rows], weights[:, width:])
+        keys = both[:, :width]
+        values = both[:, width:] + bias_v[...]
+        keys_t = keys.T
+        values_t = values.T
+        for h in range(heads):
+            part = slice(h * HEAD, (h + 1) * HEAD)
+            k_out[h, rows] = keys[:, part].astype(low)
+            v_out[h, rows] = values[:, part].astype(low)
+            kt_out[h, :, rows] = keys_t[part].astype(low)
+            vt_out[h, :, rows] = values_t[part].astype(low)
+        return carry
+
+    lax.fori_loop(0, row_tiles, project_keys, 0)
+    for j in range(row_tiles // 2):
+        block = 2 * j + lax.rem(j + col, 2)
+        rows = pl.ds(pl.multiple_of(block * TILE, TILE), TILE)
+        query = nn(x[rows], weights[:, :width]) + bias_q[...]
+        query = query.astype(low) * jnp.asarray(HEAD**-0.5, low)
+        for h in range(heads):
+            q_out[h, j] = query[:, h * HEAD : (h + 1) * HEAD]
+    for j in range(row_tiles // 2):
+        block = 2 * j + lax.rem(j + col, 2)
+        rows = pl.ds(pl.multiple_of(block * TILE, TILE), TILE)
+        query_ids = ids_row[:, rows]
+        tiles = min(2 * j + NEAR, row_tiles)
+        length = tiles * TILE
+        clear = 2 * j * TILE
+
+        def one_head(h, carry, j=j, query_ids=query_ids, length=length, clear=clear):
+            scores = nt(k_out[h, :length], q_out[h, j])
+            near = jnp.where(
+                ids_col[clear:length] <= query_ids, scores[clear:], masked_score
+            )
+            top = jnp.max(near, axis=0, keepdims=True)
+            if clear:
+                top = jnp.maximum(top, jnp.max(scores[:clear], axis=0, keepdims=True))
+                weights_far = jnp.exp(scores[:clear] - top)
+            weights_near = jnp.exp(near - top)
+            mass = jnp.sum(weights_near, axis=0, keepdims=True)
+            value = nn(vt_out[h, :, clear:length], weights_near.astype(low))
+            if clear:
+                mass = mass + jnp.sum(weights_far, axis=0, keepdims=True)
+                value = value + nn(vt_out[h, :, :clear], weights_far.astype(low))
+            mixed_out[j, h] = value / mass
+            lse_out[j, h] = top + jnp.log(mass)
+            return carry
+
+        lax.fori_loop(0, heads, one_head, 0)
+        low_out[j] = (
+            jnp.concatenate([mixed_out[j, h] for h in range(heads)], axis=0).T.astype(low)
+        )
+
+
+def attend(x, weights, bias_q, bias_v, ids, heads):
+    length = x.shape[0]
+    blocks = length // TILE // 2
+    low, f32 = x.dtype, jnp.float32
+    shape = jax.ShapeDtypeStruct
+    return pl.pallas_call(
+        functools.partial(attend_kernel, heads),
+        out_shape=[
+            shape((heads, blocks, TILE, HEAD), low),
+            shape((heads, length, HEAD), low),
+            shape((heads, HEAD, length), low),
+            shape((heads, length, HEAD), low),
+            shape((heads, HEAD, length), low),
+            shape((blocks, heads, HEAD, TILE), f32),
+            shape((blocks, TILE, heads * HEAD), low),
+            shape((blocks, heads, 1, TILE), f32),
+        ],
+        in_specs=[IN_VMEM] * 6,
+        out_specs=[IN_VMEM] * 8,
+        compiler_params=pltpu.CompilerParams(vmem_limit_bytes=VMEM_BYTES),
+        name="attend",
+    )(x, weights, bias_q, bias_v, ids.reshape(-1, 1), ids.reshape(1, -1))
+
+
+def attend_back_kernel(
+    heads, grad_ctx, q, k, kt, v, mixed, lse, ids_col, ids_row, grads, dk, dv
+):
+    length = k.shape[1]
+    row_tiles = length // TILE
+    width = heads * HEAD
+    low = q.dtype
+    col = lax.axis_index("col")
+    dk[...] = jnp.zeros_like(dk)
+    dv[...] = jnp.zeros_like(dv)
+    for j in range(row_tiles // 2):
+        block = 2 * j + lax.rem(j + col, 2)
+        rows = pl.ds(pl.multiple_of(block * TILE, TILE), TILE)
+        other = pl.ds(pl.multiple_of((4 * j + 1 - block) * TILE, TILE), TILE)
+        query_ids = ids_row[:, rows]
+        tiles = min(2 * j + NEAR, row_tiles)
+        length_j = tiles * TILE
+        clear = 2 * j * TILE
+        grad_t = grad_ctx[j].astype(jnp.float32).T
+        parts = []
+        for h in range(heads):
+            part = slice(h * HEAD, (h + 1) * HEAD)
+            grad_h = grad_ctx[j, :, part]
+            delta = jnp.sum(grad_t[part] * mixed[j, h], axis=0, keepdims=True)
+            query = q[h, j]
+            dq = jnp.zeros((HEAD, TILE), jnp.float32)
+            spans = ([(0, clear)] if clear else []) + [(clear, length_j)]
+            for low_end, high_end in spans:
+                probs = jnp.exp(nt(k[h, low_end:high_end], query) - lse[j, h])
+                if low_end == clear:
+                    probs = jnp.where(ids_col[low_end:high_end] <= query_ids, probs, 0.0)
+                slope = nt(v[h, low_end:high_end], grad_h) - delta
+                grad_scores = (probs * slope).astype(low)
+                dv[h, low_end:high_end] += nn(probs.astype(low), grad_h)
+                dk[h, low_end:high_end] += nn(grad_scores, query)
+                dq = dq + nn(kt[h, :, low_end:high_end], grad_scores)
+            parts.append(dq * HEAD**-0.5)
+        grads[rows, :width] = jnp.concatenate(parts, axis=0).T.astype(low)
+        grads[other, :width] = jnp.zeros((TILE, width), low)
+
+    def write(step, carry):
+        rows = pl.ds(pl.multiple_of(step * TILE, TILE), TILE)
+        grads[rows, width:] = jnp.concatenate(
+            [dk[h, rows] for h in range(heads)] + [dv[h, rows] for h in range(heads)], axis=1
+        ).astype(low)
+        return carry
+
+    lax.fori_loop(0, row_tiles, write, 0)
+
+
+def attend_back(grad_ctx, q, k, kt, v, mixed, lse, ids, heads):
+    length = k.shape[1]
+    low, f32 = q.dtype, jnp.float32
+    return pl.pallas_call(
+        functools.partial(attend_back_kernel, heads),
+        out_shape=jax.ShapeDtypeStruct((length, 3 * heads * HEAD), low),
+        in_specs=[IN_VMEM] * 9,
+        out_specs=IN_VMEM,
+        scratch_shapes=[pltpu.VMEM((heads, length, HEAD), f32)] * 2,
+        compiler_params=pltpu.CompilerParams(vmem_limit_bytes=VMEM_BYTES),
+        name="attend_back",
+    )(grad_ctx, q, k, kt, v, mixed, lse, ids.reshape(-1, 1), ids.reshape(1, -1))
+
+
+def norm_rows(hidden, gain, shift):
+    row_mean = jnp.mean(hidden, axis=1, keepdims=True)
+    row_var = jnp.mean(hidden * hidden, axis=1, keepdims=True) - row_mean * row_mean
+    inv_scale = lax.rsqrt(row_var + epsilon)
+    normed = (hidden - row_mean) * inv_scale
+    return normed * gain + shift, normed, inv_scale
+
+
+def norm_rows_back(grad, normed, inv_scale, gain):
+    scaled = grad * gain
+    first = jnp.mean(scaled, axis=1, keepdims=True)
+    second = jnp.mean(scaled * normed, axis=1, keepdims=True)
+    return inv_scale * (scaled - first - normed * second)
+
+
+def fast_body(
+    layer_input, cotangent, labels, block_ids, w_query, b_query, w_key, w_value, b_value,
+    w_output, b_output, ln1_gain, ln1_bias, w_inner, b_inner, w_outer, b_outer,
+    ln2_gain, ln2_bias, w_pooler, b_pooler, w_classes, b_classes,
+):
+    f32, bf16 = jnp.float32, jnp.bfloat16
+    dp, row, col = place()
+    rows, feat = layer_input.shape
+    features = 2 * feat
+    hidden = b_inner.shape[0]
+    own = rows // 2
+    heads = features // HEAD // ROWS
+    wide = heads * HEAD
+    vectors = jnp.concatenate(
+        [b_query, b_value, b_output, ln1_gain, ln1_bias, b_outer, ln2_gain, ln2_bias, b_inner]
+    )
+    count = vectors.shape[0] // feat
+    vectors = jnp.pad(vectors.reshape(count, feat), ((0, -count % 16), (0, 0)))
+    shards = [
+        jnp.concatenate([w_query, w_key, w_value], axis=1),
+        w_output.T,
+        w_inner,
+        w_outer.T,
+    ]
+    x_all, cot, vec_all, w_qkv, w_o, w_1, w_2 = gather_all(
+        layer_input, cotangent, vectors, shards
+    )
+    x_all = x_all.reshape(ROWS * rows, features)
+    w_qkv = w_qkv.reshape(features, 2, 3, 2, wide)
+    home, side = row // 2, lax.rem(row, 2)
+    w_heads = lax.dynamic_slice(
+        w_qkv, (0, home, 0, side, 0), (features, 1, 3, 1, wide)
+    ).reshape(features, 3 * wide)
+    w_o = w_o.reshape(features, features)
+    w_1 = w_1.reshape(features, 2 * hidden)
+    w_2 = w_2.reshape(features, 2 * hidden)
+    vec_all = vec_all.astype(f32)
+    take = lambda start, number=1: vec_all[:, start : start + number].reshape(1, -1)
+    bias_q = lax.dynamic_slice(take(0), (0, row * wide), (1, wide))
+    bias_v = lax.dynamic_slice(take(1), (0, row * wide), (1, wide))
+    bias_o, gain_one, shift_one, bias_2, gain_two, shift_two = [take(i) for i in range(2, 8)]
+    bias_1 = take(8, count - 8)
+
+    q, k, kt, v, vt, mixed, context_own, lse = attend(
+        x_all, w_heads, bias_q, bias_v, block_ids, heads
+    )
+    (context,) = swap_blocks(context_own, 2)
+    context = context.transpose(1, 0, 2).reshape(own, features)
+    start = row * rows + lax.rem(row + col, 2) * own
+    x_own = lax.dynamic_slice_in_dim(x_all, start, own, 0).astype(f32)
+
+    hidden_one = x_own + contract_last(context, w_o) + bias_o
+    stream, normed_one, inv_one = norm_rows(hidden_one, gain_one, shift_one)
+    stream_low = stream.astype(bf16)
+    pre_act = project(stream_low, w_1) + bias_1
+    activ = gelu_exact(pre_act).astype(bf16)
+    hidden_two = stream + contract_last(activ, w_2) + bias_2
+    result, normed_two, inv_two = norm_rows(hidden_two, gain_two, shift_two)
+    output = result.astype(bf16)
+
+    holder = ((row == 0) & (col == 0)).astype(f32)
+    first = output[0:1]
+    pooled = jnp.tanh(project(first, w_pooler) + b_pooler.astype(f32))
+    classes = w_classes.astype(f32)
+    logits_own = jnp.dot(pooled, classes, precision=highest) + b_classes.astype(f32)
+    onehot = (jnp.arange(w_classes.shape[1]) == labels[0]).astype(f32)
+    grad_logits = jax.nn.softmax(logits_own, axis=-1) - onehot[None, :]
+    grad_pre_pool = jnp.dot(grad_logits, classes.T, precision=highest) * (1.0 - pooled * pooled)
+    grad_first = jnp.dot(grad_pre_pool, w_pooler.astype(f32).T, precision=highest)
+    grad_result = cot.astype(f32).at[0].add(grad_first[0] * holder)
+
+    total = lambda values: jnp.sum(values, axis=0)
+    g_ln2_gain, g_ln2_bias = total(grad_result * normed_two), total(grad_result)
+    grad_hidden_two = norm_rows_back(grad_result, normed_two, inv_two, gain_two)
+    g_b_outer = total(grad_hidden_two)
+    branch_two = grad_hidden_two.astype(bf16)
+    g_w2 = contract_first(branch_two, activ)
+    grad_pre = (project(branch_two, w_2) * gelu_slope(pre_act)).astype(bf16)
+    g_b_inner = total(grad_pre.astype(f32))
+    g_w1 = contract_first(stream_low, grad_pre)
+    grad_stream = grad_hidden_two + contract_last(grad_pre, w_1)
+    g_ln1_gain, g_ln1_bias = total(grad_stream * normed_one), total(grad_stream)
+    grad_hidden_one = norm_rows_back(grad_stream, normed_one, inv_one, gain_one)
+    g_b_output = total(grad_hidden_one)
+    branch_one = grad_hidden_one.astype(bf16)
+    g_wo = contract_first(branch_one, context)
+    grad_context = project(branch_one, w_o).astype(bf16)
+    grad_blocks = grad_context.reshape(own, ROWS, wide).transpose(1, 0, 2)
+    grad_ctx, output = swap_blocks(grad_blocks, 3, output)
+
+    grads_low = attend_back(grad_ctx, q, k, kt, v, mixed, lse, block_ids, heads)
+    g_qkv = contract_first(x_all, grads_low).astype(bf16)
+    grad_x = contract_last(grads_low, w_heads)
+    tokens = grad_x.shape[0]
+    grad_x = lax.dynamic_update_slice_in_dim(
+        grad_x, lax.dynamic_slice_in_dim(grad_x, start, own, 0) + grad_hidden_one, start, 0
+    ).astype(bf16)
+    bias_sums = total(grads_low.astype(f32))
+    spread = lambda part: lax.dynamic_update_slice(
+        jnp.zeros((features,), f32), part, (row * wide,)
+    )
+    classes_count = w_classes.shape[1]
+    tail = jnp.pad(
+        jnp.concatenate([logits_own[0], grad_logits[0]]) * holder, (0, 128 - 2 * classes_count)
+    )
+    table = jnp.concatenate(
+        [first[0].astype(f32) * holder, grad_pre_pool[0] * holder, pooled[0] * holder, tail]
+    )
+    sequences = lax.axis_size("dp")
+    table = lax.dynamic_update_slice(
+        jnp.zeros((sequences, table.shape[0]), f32), table[None], (dp, 0)
+    )
+    pieces = [
+        spread(bias_sums[:wide]), spread(bias_sums[2 * wide :]), g_b_output, g_ln1_gain,
+        g_ln1_bias, g_b_outer, g_ln2_gain, g_ln2_bias, g_b_inner, table.reshape(-1),
+    ]
+    packed = jnp.concatenate(pieces)
+    packed = jnp.pad(packed, (0, -packed.shape[0] % 1024)).reshape(-1, 128)
+    s_w1, s_w2, s_wo, s_q, grad_input, sums = reduce_all(
+        [g.astype(bf16) for g in (g_w1, g_w2, g_wo)], g_qkv, grad_x, packed
+    )
+    depth = w_query.shape[0]
+    s_q = s_q.transpose(0, 2, 1, 3).reshape(depth, 2, 3, wide).transpose(2, 0, 1, 3)
+    s_q = s_q.reshape(3, depth, feat).astype(f32)
+    sums = sums.reshape(-1)
+    found, at = [], 0
+    for piece in pieces:
+        found.append(sums[at : at + piece.shape[0]])
+        at += piece.shape[0]
+    own_part = lambda full: lax.dynamic_slice_in_dim(
+        full, col * (full.shape[0] // 2), full.shape[0] // 2
+    )
+    (
+        g_b_query, g_b_value, g_b_output, g_ln1_gain, g_ln1_bias, g_b_outer, g_ln2_gain,
+        g_ln2_bias, g_b_inner,
+    ) = [own_part(full) for full in found[:-1]]
+    table = found[-1].reshape(sequences, -1)
+    firsts, pre_pools, pools = [
+        table[:, i * features : (i + 1) * features] for i in range(3)
+    ]
+    ends = table[:, 3 * features :]
+    all_grads = ends[:, classes_count : 2 * classes_count]
+    logits = lax.dynamic_slice_in_dim(ends[:, :classes_count], dp, 1, 0)
+    outer = lambda left, right: jnp.sum(left[:, :, None] * right[:, None, :], axis=0)
+    return (
+        output, logits, grad_input, s_q[0], g_b_query, s_q[1], s_q[2], g_b_value,
+        s_wo.reshape(depth, feat).astype(f32).T, g_b_output, g_ln1_gain, g_ln1_bias,
+        s_w1.reshape(depth, hidden).astype(f32), g_b_inner,
+        s_w2.reshape(depth, hidden).astype(f32).T, g_b_outer, g_ln2_gain, g_ln2_bias,
+        outer(firsts, pre_pools), total(pre_pools), outer(pools, all_grads), total(all_grads),
+    )
+
+
+def is_fast(mesh):
+    sizes = mesh.shape
+    return sizes["dp"] == 4 and sizes["row"] == ROWS and sizes["col"] == 2
+
+
 def solution(mesh):
     placed = (
         P(("dp", "row"), "col"),
@@ -406,7 +1285,7 @@
         P(),
     )
     return jax.shard_map(
-        body,
+        fast_body if is_fast(mesh) else body,
         mesh=mesh,
         in_specs=placed,
         out_specs=(

time: 1010 us -> 425 us (0.42)
  waiting for transfers between devices: 589 us -> 0 us
  Pallas kernels: 0 us -> 286 us
  blocking collectives: 184 us -> 0 us
  matrix products: 72.1 us -> 44.4 us
  other arithmetic: 45.8 us -> 25.2 us
  local copies, waits for them, and re-layouts: 78.4 us -> 62 us
  between operations: 15.7 us -> 2.43 us
  loops' own time: 10.9 us -> 0 us
    psum x1 -> x0, waiting for transfers between devices: 381 us -> none  [body(): lax.psum((g_w_query_full, g_w_key_full, g_w_value_full, g_w_inner_full, g...]
    pallas_call x0 -> x6, Pallas kernels: none -> 286 us  [the longest x1 109 us: reduce_all(): pl.pallas_call(functools.partial(reduce_kernel, count), out_shape=outs, i...]
    all_gather x4 -> x0, waiting for transfers between devices: 106 us -> none  [the longest x1 45.3 us: body(): lax.all_gather(w_outer, 'row', axis=1, tiled=True)]
    psum x5 -> x0, blocking collectives: 92 us -> none  [the longest x1 80.1 us: body(): lax.psum((g_w_query_full, g_w_key_full, g_w_value_full, g_w_inner_full, g...]
    all_gather x9 -> x0, blocking collectives: 91.9 us -> none  [the longest x1 22.8 us: body(): lax.all_gather(w_query, 'row', axis=0, tiled=True)]
    reduce_scatter x2 -> x0, waiting for transfers between devices: 78.6 us -> none  [the longest x1 43.7 us: body(): lax.psum_scatter(grad_k_all.astype(jnp.bfloat16), 'row', scatter_dimensio...]
    unnamed x15 -> x0, waiting for transfers between devices: 23.5 us -> none
    dot_general x17 -> x3, matrix products: 26.6 us -> 3.34 us  [the longest x1 1.44 us: fast_body(): jnp.dot(pooled, classes, precision=highest) + b_classes.astype(f32)]
  transfers between devices with their start and end apart: 11 -> 0, of which waited for: 9 -> 0; matrix products, arithmetic and copies ran while one was open for 6% -> 0% of each run, Pallas kernels for 0% -> 0%
where the time goes in v1:
time: 425 us; the launch traced here: 420 us
  Pallas kernels  286 us (67%)
  local copies, waits for them, and re-layouts  62 us (15%)
  matrix products  44.4 us (10%)
  other arithmetic  25.2 us (6%)
    pallas_call x1, Pallas kernels, reduce_all(): pl.pallas_call(functools.partial(reduce_kernel, count), out_shape=outs, i...  109 us
    pallas_call x1, Pallas kernels, gather_all(): pl.pallas_call(functools.partial(gather_kernel, widths), out_shape=shapes...  103 us
    pallas_call x2, Pallas kernels, swap_blocks(): pl.pallas_call(functools.partial(swap_kernel, split), out_shape=shapes, i...  32.8 us
    pallas_call x1, Pallas kernels, attend(): pl.pallas_call(functools.partial(attend_kernel, heads), out_shape=[shape(...  23 us
    pallas_call x1, Pallas kernels, attend_back(): pl.pallas_call(functools.partial(attend_back_kernel, heads), out_shape=ja...  18.7 us
    dot_general x4, matrix products, contract_first(): lax.dot_general(left, right, (((0,), (0,)), ((), ())), preferred_element_...  15.4 us
    dot_general x4, matrix products, contract_last(): lax.dot_general(left, right, (((1,), (1,)), ((), ())), preferred_element_...  13.3 us
    reshape x1, local copies, waits for them, and re-layouts, fast_body(): w_qkv = w_qkv.reshape(features, 2, 3, 2, wide)  12.7 us

profile of v1, /device:TPU:0, one launch (start us, length us, event | category | flops | bytes accessed | tf_op | source)
XLA Modules:
  0.0 419.9 jit_solution(798584417400762197)
XLA Ops:
  0.7 1.0 dynamic-update-slice.13
  3.4 0.9 dynamic-update-slice.16
  5.9 0.9 dynamic-update-slice.19
  9.0 1.9 pad_maximum_fusion
  10.8 102.8 %gather_all.1 = (bf16[4,512,768]{2,1,0:T(8,128)(2,1)}, bf16[256,768]{1,0:T(8,128)(2,1)}, bf16[2,16,384]{2,1,0:T(8,128)(2,1)}, bf16[4,4,48,2304]{3,2,1,0:T(8,128)...) custom-call(bf16[512,384]{1,0:T(8,128)(2,1)} %x.7, ...), custom_call_target="tpu_custom_call" | custom-call | tf_op jit(solution)/shard_map/gather_all/pallas_call | solution.py:601
  115.0 12.7 %reshape.294 = bf16[768,2,3,2,192]{4,3,2,1,0:T(2,128)(2,1)} reshape(bf16[4,4,48,2304]{3,2,1,0:T(8,128)(2,1)} %get-tuple-element.57) | data formatting | bytes 7077888 | tf_op jit(solution)/shard_map/reshape | solution.py:1131
  127.7 4.1 constant_dynamic-slice_fusion.3
  131.8 4.4 %copy.68 = bf16[768,1,3,1,192]{0,4,2,3,1:T(8,128)(2,1)} copy(bf16[768,1,3,1,192]{4,3,2,1,0:T(2,128)(2,1)S(1)} %constant_dynamic-slice_fusion.3) | data formatting | bytes 1769472 | tf_op jit(solution)/shard_map/dynamic_slice | solution.py:1133
  136.2 2.2 copy.69.weights
  139.8 1.3 copy.70.ids_col
  141.2 23.0 %attend.1 = (bf16[3,4,256,64]{3,2,1,0:T(8,128)(2,1)}, bf16[3,2048,64]{2,1,0:T(8,128)(2,1)}, bf16[3,64,2048]{2,1,0:T(8,128)(2,1)}, bf16[3,2048,64]{2,1,0:T(8,128)...) custom-call(bf16[2048,768]{1,0:T(8,128)(2,1)} %bitcast.110, ...), custom_call_target="tpu_custom_call" | custom-call | tf_op jit(solution)/shard_map/attend/pallas_call | solution.py:1005
  164.2 15.4 %swap_blocks.2 = bf16[4,256,192]{2,1,0:T(8,128)(2,1)} custom-call(bf16[4,256,192]{2,1,0:T(8,128)(2,1)} %get-tuple-element.59.refs_0_), custom_call_target="tpu_custom_call" | custom-call | tf_op jit(solution)/shard_map/swap_blocks/pallas_call | solution.py:658
  179.6 1.3 copy.71
  181.0 2.1 multiply_reduce_fusion.6
  184.6 6.0 %multiply_convert_fusion = (bf16[256,3072]{1,0:T(8,128)(2,1)S(1)}, f32[256,3072]{1,0:T(8,128)}) fusion(f32[3072]{0:T(1024)S(1)} %add.161, bf16[768,3072]{1,0:T(8,128)(2,1)} %bitcast.129, f32[256,768]{1,0:T(8,128)S(1)} %get-tuple-element.128, f32[768]{0:T(1024)S(1)} %add.158, f32[768]{0:T(1024)S(1)} %mul.234, f32[256]{0:T(256)S(1)} %get-tuple-element.127, ...), kind=kOutput, calls=%fused_computation.12 | convolution fusion | flops 1213661184 | bytes 10244096 | tf_op jit(solution)/shard_map/dot_general | solution.py:31
  190.7 5.1 %multiply_reduce_fusion.5 = (f32[256]{0:T(256)}, f32[256]{0:T(256)}, f32[256,768]{1,0:T(8,128)S(1)}) fusion(f32[768]{0:T(1024)S(1)} %copy-done.33, bf16[256,3072]{1,0:T(8,128)(2,1)S(1)} %get-tuple-element.129, bf16[768,3072]{1,0:T(8,128)(2,1)} %bitcast.133, f32[768]{0:T(1024)S(1)} %add.158, f32[768]{0:T(1024)S(1)} %mul.234, f32[256]{0:T(256)S(1)} %get-tuple-element.126, ...), kind=kOutput, calls=%fused_computation.38 | convolution fusion | flops 1209728512 | bytes 7877632 | tf_op jit(solution)/shard_map/dot_general | solution.py:41
  195.7 1.3 add.170
  198.4 0.9 add_convert_fusion.refs_1_
  199.6 1.3 broadcast_multiply_fusion
  200.9 1.4 fusion.23
  202.4 1.3 fusion.15
  203.6 1.3 divide_subtract_fusion
  206.9 1.1 convolution_reduce_fusion
  208.1 1.8 multiply_reduce_fusion.1
  209.9 1.7 fusion.18
  211.7 5.6 %convert_reduce_fusion.1 = (f32[3072]{0:T(1024)S(1)}, bf16[256,3072]{1,0:T(8,128)(2,1)S(1)}) fusion(f32[256,3072]{1,0:T(8,128)S(1)} %copy-done.38, bf16[768,3072]{1,0:T(8,128)(2,1)} %bitcast.134, f32[256,768]{1,0:T(8,128)S(1)} %get-tuple-element.101), kind=kOutput, calls=%fused_computation.11 | convolution fusion | flops 1217590272 | bytes 10235904 | tf_op jit(solution)/shard_map/dot_general | solution.py:31
  217.4 1.7 multiply_reduce_fusion.2
  220.1 1.0 copy.73
  221.1 17.4 %swap_blocks.3 = (bf16[4,256,192]{2,1,0:T(8,128)(2,1)}, bf16[512,384]{1,0:T(8,128)(2,1)}) custom-call(bf16[4,256,192]{2,1,0:T(8,128)(2,1)} %bitcast.113, bf16[256,768]{1,0:T(8,128)(2,1)} %copy-done.6), custom_call_target="tpu_custom_call" | custom-call | tf_op jit(solution)/shard_map/swap_blocks/pallas_call | solution.py:658
  238.5 5.5 %convolution_convert_fusion.1 = bf16[768,3072]{1,0:T(8,128)(2,1)} fusion(bf16[256,3072]{1,0:T(8,128)(2,1)} %copy-done.11, f32[256,768]{1,0:T(8,128)} %copy-done.4, f32[768]{0:T(1024)S(1)} %add.158, f32[768]{0:T(1024)S(1)} %mul.234, f32[256]{0:T(256)S(1)} %copy-done.30, f32[256]{0:T(256)S(1)} %copy-done.28), kind=kOutput, calls=%fused_computation.3 | convolution fusion | flops 1211301888 | bytes 7086080 | tf_op jit(solution)/shard_map/dot_general | solution.py:35
  244.1 3.5 convolution_convert_fusion
  247.6 1.5 convolution_convert_fusion.2
  249.1 18.7 %attend_back.1 = bf16[2048,576]{1,0:T(8,128)(2,1)} custom-call(bf16[4,256,192]{2,1,0:T(8,128)(2,1)} %get-tuple-element.65.grad_ctx, bf16[3,4,256,64]{3,2,1,0:T(8,128)(2,1)} %get-tuple-element.66.q, bf16[3,2048,64]{2,1,0:T(8,128)(2,1)} %get-tuple-element.67.k, bf16[3,64,2048]{2,1,0:T(8,128)(2,1)} %get-tuple-element.68.kt, ...), custom_call_target="tpu_custom_call" | custom-call | tf_op jit(solution)/shard_map/attend_back/pallas_call | solution.py:1077
  267.9 4.8 %convolution_convert_fusion.3 = bf16[768,576]{0,1:T(8,128)(2,1)S(1)} fusion(bf16[2048,768]{1,0:T(8,128)(2,1)} %bitcast.112, bf16[2048,576]{1,0:T(8,128)(2,1)} %attend_back.1), kind=kOutput, calls=%fused_computation.15 | convolution fusion | flops 1812381696 | bytes 6389760 | tf_op jit(solution)/shard_map/dot_general | solution.py:35
  272.7 1.3 copy.75
  274.0 4.4 %fusion.24 = f32[2048,768]{1,0:T(8,128)S(1)} fusion(bf16[2048,576]{1,0:T(8,128)(2,1)} %attend_back.1, bf16[768,576]{0,1:T(8,128)(2,1)S(1)} %bitcast.109), kind=kOutput, calls=%fused_computation.120 | convolution fusion | flops 1811939328 | bytes 9535488 | tf_op jit(solution)/shard_map/dot_general | solution.py:41
  278.7 2.0 convert_element_type.119
  280.6 2.2 convert_reduce_fusion
  285.0 108.6 %reduce_all.1 = (bf16[4,48,1536]{2,1,0:T(8,128)(2,1)}, bf16[4,48,1536]{2,1,0:T(8,128)(2,1)}, bf16[4,48,384]{2,1,0:T(8,128)(2,1)}, bf16[4,2,48,576]{3,2,1,0:T(8,1...) custom-call(bf16[4,4,48,3072]{3,2,1,0:T(8,128)(2,1)} %bitcast.102, bf16[4,4,48,3072]{3,2,1,0:T(8,128)(2,1)} %bitcast.103, ...), custom_call_target="tpu_custom_call" | custom-call | tf_op jit(solution)/shard_map/reduce_all/pallas_call | solution.py:891
  395.5 1.1 convert_bitcast_fusion.1
  396.6 1.0 copy.76
  397.6 1.8 reshape.316
  400.6 1.0 squeeze.9
  403.4 1.0 squeeze.20
  404.7 1.0 squeeze.21
  409.0 1.2 bitcast_convert_fusion
  411.6 1.2 convert_bitcast_fusion
  415.4 2.1 multiply_reduce_fusion
  (171 shorter events, 30.7 us)
Async XLA Ops:
  0.7 198.7 %copy-start = (bf16[768,768]{1,0:T(8,128)(2,1)S(1)}, bf16[768,768]{1,0:T(8,128)(2,1)}, u32[]{:S(2)}) copy-start(bf16[768,768]{1,0:T(8,128)(2,1)} %param.44) | copy-start | bytes 3538948
  131.8 8.0 %copy-start.20 = (s32[2048]{0:T(1024)S(1)}, s32[2048]{0:T(1024)}, u32[]{:S(2)}) copy-start(s32[2048]{0:T(1024)} %param.28) | copy-start | bytes 24580
  164.2 19.0 %copy-start.32 = (f32[2,384]{1,0:T(2,128)S(1)}, f32[2,384]{1,0:T(2,128)}, u32[]{:S(2)}) copy-start(f32[2,384]{1,0:T(2,128)} %get-tuple-element.94) | copy-start | bytes 9220
  164.2 20.4 %copy-start.19 = (bf16[2,16,384]{2,1,0:T(8,128)(2,1)S(1)}, bf16[2,16,384]{2,1,0:T(8,128)(2,1)}, u32[]{:S(2)}) copy-start(bf16[2,16,384]{2,1,0:T(8,128)(2,1)} %get-tuple-element.58) | copy-start | bytes 73732
  164.2 20.4 %copy-start.31 = (f32[2,384]{1,0:T(2,128)S(1)}, f32[2,384]{1,0:T(2,128)}, u32[]{:S(2)}) copy-start(f32[2,384]{1,0:T(2,128)} %get-tuple-element.93) | copy-start | bytes 9220
  179.6 3.6 copy-start.17
  180.9 2.2 copy-start.7
  183.1 36.0 %copy-start.4 = (f32[256,768]{1,0:T(8,128)}, f32[256,768]{1,0:T(8,128)S(1)}, u32[]{:S(2)}) copy-start(f32[256,768]{1,0:T(8,128)S(1)} %get-tuple-element.128) | copy-start | bytes 2359300
  183.1 7.5 %copy-start.27 = (f32[256]{0:T(256)}, f32[256]{0:T(256)S(1)}, u32[]{:S(2)}) copy-start(f32[256]{0:T(256)S(1)} %get-tuple-element.126) | copy-start | bytes 3076
  183.1 7.5 %copy-start.29 = (f32[256]{0:T(256)}, f32[256]{0:T(256)S(1)}, u32[]{:S(2)}) copy-start(f32[256]{0:T(256)S(1)} %get-tuple-element.127) | copy-start | bytes 3076
  184.6 6.1 %copy-start.33 = (f32[768]{0:T(1024)S(1)}, f32[768]{0:T(1024)}, u32[]{:S(2)}) copy-start(f32[768]{0:T(1024)} %add.166) | copy-start | bytes 9220
  190.6 5.1 %copy-start.9 = (bf16[256,3072]{1,0:T(8,128)(2,1)}, bf16[256,3072]{1,0:T(8,128)(2,1)S(1)}, u32[]{:S(2)}) copy-start(bf16[256,3072]{1,0:T(8,128)(2,1)S(1)} %get-tuple-element.129) | copy-start | bytes 4718596
  198.4 9.5 %copy-start.21 = (f32[256]{0:T(256)}, f32[256]{0:T(256)S(1)}, u32[]{:S(2)}) copy-start(f32[256]{0:T(256)S(1)} %get-tuple-element.125) | copy-start | bytes 3076
  199.3 8.6 %copy-start.6 = (bf16[256,768]{1,0:T(8,128)(2,1)}, bf16[256,768]{1,0:T(8,128)(2,1)S(1)}, u32[]{:S(2)}) copy-start(bf16[256,768]{1,0:T(8,128)(2,1)S(1)} %add_convert_fusion.refs_1_) | copy-start | bytes 1179652
  202.4 1.3 copy-start.34
  204.9 0.5 copy-start.36
  208.1 3.6 copy-start.38
  209.9 7.4 %slice-start = ((s8[4718592]{0:T(1024)(128)(4,1)}), s8[4194304]{0:T(1024)(128)(4,1)S(1)}, s32[]{:S(2)}) async-start(s8[4718592]{0:T(1024)(128)(4,1)} %bitcast.130), calls=%async_computation | async-start | bytes 8388608
  211.6 5.7 %copy-start.2 = (f32[256,768]{1,0:T(8,128)}, f32[256,768]{1,0:T(8,128)S(1)}, u32[]{:S(2)}) copy-start(f32[256,768]{1,0:T(8,128)S(1)} %get-tuple-element.101) | copy-start | bytes 2359300
  211.7 5.7 %copy-start.28 = (f32[256]{0:T(256)S(1)}, f32[256]{0:T(256)}, u32[]{:S(2)}) copy-start(f32[256]{0:T(256)} %copy-done.27) | copy-start | bytes 3076
  211.7 5.7 %copy-start.30 = (f32[256]{0:T(256)S(1)}, f32[256]{0:T(256)}, u32[]{:S(2)}) copy-start(f32[256]{0:T(256)} %copy-done.29) | copy-start | bytes 3076
  211.7 5.7 %slice-start.1 = ((s8[4718592]{0:T(1024)(128)(4,1)}), s8[524288]{0:T(1024)(128)(4,1)S(1)}, s32[]{:S(2)}) async-start(s8[4718592]{0:T(1024)(128)(4,1)} %bitcast.130), calls=%async_computation.1 | async-start | bytes 1048576
  217.3 1.8 copy-start.11
  217.4 2.1 copy-start.12
  238.5 5.6 %copy-start.3 = (f32[256,768]{1,0:T(8,128)S(1)}, f32[256,768]{1,0:T(8,128)}, u32[]{:S(2)}) copy-start(f32[256,768]{1,0:T(8,128)} %copy-done.2) | copy-start | bytes 2359300
  238.5 5.5 %copy-start.10 = (bf16[256,3072]{1,0:T(8,128)(2,1)S(1)}, bf16[256,3072]{1,0:T(8,128)(2,1)}, u32[]{:S(2)}) copy-start(bf16[256,3072]{1,0:T(8,128)(2,1)} %copy-done.9) | copy-start | bytes 4718596
  244.1 3.5 copy-start.8
  267.9 6.1 %copy-start.5 = (bf16[768,1,3,1,192]{0,4,2,3,1:T(8,128)(2,1)S(1)}, bf16[768,1,3,1,192]{0,4,2,3,1:T(8,128)(2,1)}, u32[]{:S(2)}) copy-start(bf16[768,1,3,1,192]{0,4,2,3,1:T(8,128)(2,1)} %copy.68) | copy-start | bytes 2654212
  278.6 4.6 %copy-start.24 = (f32[768]{0:T(1024)S(1)}, f32[768]{0:T(1024)}, u32[]{:S(2)}) copy-start(f32[768]{0:T(1024)} %get-tuple-element.100) | copy-start | bytes 9220
  278.6 4.6 %copy-start.23 = (f32[768]{0:T(1024)S(1)}, f32[768]{0:T(1024)}, u32[]{:S(2)}) copy-start(f32[768]{0:T(1024)} %get-tuple-element.78) | copy-start | bytes 9220
  278.6 4.6 %copy-start.22 = (f32[768]{0:T(1024)S(1)}, f32[768]{0:T(1024)}, u32[]{:S(2)}) copy-start(f32[768]{0:T(1024)} %get-tuple-element.84) | copy-start | bytes 9220
  278.6 4.6 %copy-start.35 = (f32[3]{0:T(128)S(1)}, f32[3]{0:T(128)}, u32[]{:S(2)}) copy-start(f32[3]{0:T(128)} %copy-done.34) | copy-start | bytes 40
  278.6 4.6 %copy-start.37 = (f32[3]{0:T(128)S(1)}, f32[3]{0:T(128)}, u32[]{:S(2)}) copy-start(f32[3]{0:T(128)} %copy-done.36) | copy-start | bytes 40
  278.6 5.5 %copy-start.25 = (f32[768]{0:T(1024)S(1)}, f32[768]{0:T(1024)}, u32[]{:S(2)}) copy-start(f32[768]{0:T(1024)} %get-tuple-element.98) | copy-start | bytes 9220
  278.6 5.5 %copy-start.26 = (f32[768]{0:T(1024)S(1)}, f32[768]{0:T(1024)}, u32[]{:S(2)}) copy-start(f32[768]{0:T(1024)} %get-tuple-element.96) | copy-start | bytes 9220
  399.4 6.9 %copy-start.18 = (bf16[4,48,384]{2,1,0:T(8,128)(2,1)S(1)}, bf16[4,48,384]{2,1,0:T(8,128)(2,1)}, u32[]{:S(2)}) copy-start(bf16[4,48,384]{2,1,0:T(8,128)(2,1)} %get-tuple-element.75) | copy-start | bytes 442372
  399.5 9.6 %copy-start.14 = (bf16[4,48,1536]{2,1,0:T(8,128)(2,1)S(1)}, bf16[4,48,1536]{2,1,0:T(8,128)(2,1)}, u32[]{:S(2)}) copy-start(bf16[4,48,1536]{2,1,0:T(8,128)(2,1)} %get-tuple-element.76) | copy-start | bytes 1769476
  400.6 11.0 %copy-start.13 = (bf16[4,48,1536]{2,1,0:T(8,128)(2,1)S(1)}, bf16[4,48,1536]{2,1,0:T(8,128)(2,1)}, u32[]{:S(2)}) copy-start(bf16[4,48,1536]{2,1,0:T(8,128)(2,1)} %get-tuple-element.77) | copy-start | bytes 1769476
  407.1 11.1 %copy-start.15 = (bf16[512,384]{1,0:T(8,128)(2,1)S(1)}, bf16[512,384]{1,0:T(8,128)(2,1)}, u32[]{:S(2)}) copy-start(bf16[512,384]{1,0:T(8,128)(2,1)} %get-tuple-element.161) | copy-start | bytes 1179652
  409.0 9.9 %copy-start.16 = (bf16[512,384]{1,0:T(8,128)(2,1)S(1)}, bf16[512,384]{1,0:T(8,128)(2,1)}, u32[]{:S(2)}) copy-start(bf16[512,384]{1,0:T(8,128)(2,1)} %get-tuple-element.163) | copy-start | bytes 1179652
  409.0 10.7 %copy-start.1 = (bf16[768,768]{1,0:T(8,128)(2,1)S(1)}, bf16[768,768]{1,0:T(8,128)(2,1)}, u32[]{:S(2)}) copy-start(bf16[768,768]{1,0:T(8,128)(2,1)} %param.44) | copy-start | bytes 3538948

commit v2 on v1

--- a/solution.py
+++ b/solution.py
@@ -463,61 +463,93 @@
     return pl.ds(pl.multiple_of(col * width, 128), width)
 
 
-def gather_kernel(widths, x, cot, vec, *refs):
+IN_VMEM = pl.BlockSpec(memory_space=pltpu.VMEM)
+IN_PLACE = pl.BlockSpec(memory_space=pl.ANY)
+
+
+def comm_params(number):
+    return pltpu.CompilerParams(
+        collective_id=number, has_side_effects=True, vmem_limit_bytes=VMEM_BYTES
+    )
+
+
+TILE = 256
+NEAR = 3
+
+
+def nt(left, right):
+    return lax.dot_general(
+        left, right, (((1,), (1,)), ((), ())), preferred_element_type=jnp.float32
+    )
+
+
+def nn(left, right):
+    return jnp.dot(left, right, preferred_element_type=jnp.float32)
+
+
+def forward_kernel(widths, heads, x, cot, vec, wq, wk, wv, ids, *refs):
     count = len(widths)
     shards, refs = refs[:count], refs[count:]
-    x_all, cot_own, vec_all = refs[:3]
-    fulls = refs[3 : 3 + count]
-    send, recv, local = refs[3 + count :]
+    x_all, cot_own, vec_all, w_heads, q_out, k_out, kt_out, v_out, mixed_out, lse_out, context = (
+        refs[:11]
+    )
+    fulls, refs = refs[11 : 11 + count], refs[11 + count :]
+    vt_out, ids_col, packs, low_out, send, recv, local = refs
     dp, row, col = place()
     links = Links(send, recv)
-    feat = x.shape[1]
+    low = x.dtype
+    rows_dev, feat = x.shape
+    wide = heads * HEAD
     mate = (dp, row, 1 - col)
     at_row = lambda other: (dp, other, col)
     at_dp = lambda flip: (dp ^ flip, row, col)
+    home, side = row // 2, lax.rem(row, 2)
+    mine = lax.rem(row + col, 2)
+    half = rows_dev // 2
     meet([at_row(lax.rem(row + k, ROWS)) for k in (1, 2, 3)] + [at_dp(1), at_dp(2), mate])
 
-    half = x.shape[0] // 2
-    mine = lax.rem(row + col, 2)
     x_at = lambda k: x_all.at[k, :, columns(col, feat)]
+    x_mate_at = lambda k: x_all.at[k, :, columns(1 - col, feat)]
     w_at = lambda i, k, q: fulls[i].at[k, q, :, columns(col, widths[i])]
     row_at = lambda i, k: fulls[i].at[k, :, :, columns(col, widths[i])]
-    x_mate_at = lambda k: x_all.at[k, :, columns(1 - col, feat)]
     row_mate_at = lambda i, k: fulls[i].at[k, :, :, columns(1 - col, widths[i])]
 
-    line_x = links.slots(3)
+    line_x, mate_x = links.slots(3), links.slots(4)
+    line_q, first_q, second_q, mate_q = (
+        links.slots(3), links.slots(3), links.slots(6), links.slots(1),
+    )
+    mate_cot, mate_vec, swap = links.slots(1), links.slots(1), links.slots(3)
     line_w = [links.slots(3) for _ in widths]
     first_w = [links.slots(3) for _ in widths]
     second_w = [links.slots(6) for _ in widths]
-    mate_x = links.slots(4)
     mate_w = [links.slots(4) for _ in widths]
-    mate_cot, mate_vec = links.slots(1), links.slots(1)
-
-    copies = [pltpu.make_async_copy(x, x_at(row), local.at[0])]
-    copies += [
-        pltpu.make_async_copy(shards[i], row_at(i, row), local.at[1 + i]) for i in range(count)
-    ]
-    copies += [
-        pltpu.make_async_copy(
-            cot.at[pl.ds(pl.multiple_of(mine * half, 128), half)],
-            cot_own.at[:, columns(col, feat)],
-            local.at[1 + count],
-        ),
-        pltpu.make_async_copy(vec, vec_all.at[col], local.at[2 + count]),
-    ]
-
-    def relay(step):
+    steps = list(steps_of_line(row))
+    at_step = lambda step: [entry[2:] for entry in steps if entry[0] == step]
+
+    def relay(step, own, full, base):
         for way in (1, -1):
             held, onward = row - way * (step - 1), row + way
             ok = within(held) & within(onward)
             slot = 3 - step if way == 1 else step - 1
-            links.push(x if step == 1 else x_at(held), x_at(held), line_x + slot, at_row(onward), ok)
-            for i in range(count):
-                source = shards[i].at[dp] if step == 1 else w_at(i, held, dp)
-                links.push(source, w_at(i, held, dp), line_w[i] + slot, at_row(onward), ok)
-
-    relay(1)
+            links.push(own if step == 1 else full(held), full(held), base + slot, at_row(onward), ok)
+
+    relay(1, x, x_at, line_x)
     links.push(x, x_at(row), mate_x, mate)
+    for j in range(2):
+        part = slice(j * wide, (j + 1) * wide)
+        packs[j] = jnp.concatenate(
+            [wq[:, part], wk[:, part], wv[:, part]], axis=1
+        ).reshape(packs.shape[1:])
+    for j in range(2):
+        k = 2 * col + j
+        away = k != row
+        slot = lax.rem(row - k + ROWS + 3, ROWS)
+        links.push(packs.at[j, dp], w_heads.at[row, dp], line_q + slot, at_row(k), away)
+
+        @pl.when(jnp.logical_not(away))
+        def _(j=j):
+            w_heads[row] = packs[j]
+
     links.push(
         cot.at[pl.ds(pl.multiple_of((1 - mine) * half, 128), half)],
         cot_own.at[:, columns(col, feat)],
@@ -525,92 +557,254 @@
         mate,
     )
     links.push(vec, vec_all.at[col], mate_vec, mate)
+    cot_own[:, columns(col, feat)] = cot[pl.ds(pl.multiple_of(mine * half, 128), half)]
+    vec_all[col] = vec[...]
+    x_all[row, :, columns(col, feat)] = x[...]
+    copies = [
+        pltpu.make_async_copy(shards[i], row_at(i, row), local.at[i]) for i in range(count)
+    ]
+
+    at_home = home == col
+
+    def q_first():
+        for slot in range(3):
+            k = lax.rem(row + slot + 1, ROWS)
+            one = 1 + slot % 2
+            links.arrive(w_heads.at[k, dp], line_q + slot, mate, at_home)
+            links.push(
+                w_heads.at[k, dp], w_heads.at[k, dp], first_q + slot, at_dp(one), at_home
+            )
+
+    def q_second():
+        for slot in range(3):
+            k = lax.rem(row + slot + 1, ROWS)
+            one, two = 1 + slot % 2, 2 - slot % 2
+            links.arrive(w_heads.at[k, dp ^ one], first_q + slot, mate, at_home)
+            for n, q in enumerate((dp, dp ^ one)):
+                links.push(
+                    w_heads.at[k, q], w_heads.at[k, q], second_q + 2 * slot + n, at_dp(two), at_home
+                )
+
+    def q_mate():
+        for slot in range(3):
+            k = lax.rem(row + slot + 1, ROWS)
+            two = 2 - slot % 2
+            links.arrive(w_heads.at[k, dp ^ two], second_q + 2 * slot, mate, at_home)
+            links.arrive(w_heads.at[k, dp ^ 3], second_q + 2 * slot + 1, mate, at_home)
+        links.push(w_heads, w_heads, mate_q, mate, at_home)
+        links.arrive(w_heads, mate_q, mate, jnp.logical_not(at_home))
+
+    def x_step(step):
+        for slot, k, ok in at_step(step):
+            links.arrive(x_at(k), line_x + slot, mate, ok)
+        if step < 3:
+            relay(step + 1, x, x_at, line_x)
+        for slot, k, ok in at_step(step):
+            links.push(x_at(k), x_at(k), mate_x + 1 + slot, mate, ok)
+
+    turn = lambda i, slot: (1, 2) if (i + slot) % 2 == 0 else (2, 1)
+
+    def w_relay(step):
+        for i in range(count):
+            relay(step, shards[i].at[dp], lambda k, i=i: w_at(i, k, dp), line_w[i])
+
+    def w_first(step):
+        for i in range(count):
+            for slot, k, ok in at_step(step):
+                links.arrive(w_at(i, k, dp), line_w[i] + slot, mate, ok)
+        if step < 3:
+            w_relay(step + 1)
+        for i in range(count):
+            for slot, k, ok in at_step(step):
+                one, two = turn(i, slot)
+                links.push(w_at(i, k, dp), w_at(i, k, dp), first_w[i] + slot, at_dp(one), ok)
+
+    def w_second(step):
+        for i in range(count):
+            for slot, k, ok in at_step(step):
+                one, two = turn(i, slot)
+                links.arrive(w_at(i, k, dp ^ one), first_w[i] + slot, mate, ok)
+                for n, q in enumerate((dp, dp ^ one)):
+                    links.push(
+                        w_at(i, k, q), w_at(i, k, q), second_w[i] + 2 * slot + n, at_dp(two), ok
+                    )
+
+    def w_mate(step):
+        for i in range(count):
+            for slot, k, ok in at_step(step):
+                one, two = turn(i, slot)
+                links.arrive(w_at(i, k, dp ^ two), second_w[i] + 2 * slot, mate, ok)
+                links.arrive(w_at(i, k, dp ^ 3), second_w[i] + 2 * slot + 1, mate, ok)
+                links.push(row_at(i, k), row_at(i, k), mate_w[i] + 1 + slot, mate, ok)
+
+    row_tiles = ROWS * rows_dev // TILE
+    per_row = rows_dev // TILE
+
+    def split_ids(step, carry):
+        span = pl.ds(pl.multiple_of(step * TILE, TILE), TILE)
+        ids_col[span] = jnp.broadcast_to(ids[:, span], (8, TILE)).T[:, :1]
+        return carry
+
+    lax.fori_loop(0, row_tiles, split_ids, 0)
+    x_step(1)
+    q_first()
+    x_step(2)
+    q_second()
+    w_relay(1)
+    for copy in copies:
+        copy.start()
     for i in range(count):
         links.push(shards[i], row_at(i, row), mate_w[i], mate)
-    for copy in copies:
-        copy.start()
-    steps = list(steps_of_line(row))
-    turn = lambda i, slot: (1, 2) if (i + slot) % 2 == 0 else (2, 1)
-    for step in (1, 2, 3):
-        for at_step, way, slot, k, ok in steps:
-            if at_step != step:
-                continue
-            links.arrive(x_at(k), line_x + slot, mate, ok)
-            for i in range(count):
-                links.arrive(w_at(i, k, dp), line_w[i] + slot, mate, ok)
-        if step < 3:
-            relay(step + 1)
-        for at_step, way, slot, k, ok in steps:
-            if at_step != step:
-                continue
-            links.push(x_at(k), x_at(k), mate_x + 1 + slot, mate, ok)
-            for i in range(count):
-                one, two = turn(i, slot)
-                links.push(w_at(i, k, dp), w_at(i, k, dp), first_w[i] + slot, at_dp(one), ok)
+    q_mate()
+    links.arrive(vec_all.at[1 - col], mate_vec, mate)
+    bias_of = lambda n: jnp.where(
+        side == 0, vec_all[home, n : n + 1, :wide], vec_all[home, n : n + 1, wide : 2 * wide]
+    )
+    bias_q, bias_v = bias_of(0), bias_of(1)
+    weights = lambda start, stop: w_heads[:, :, :, start:stop].reshape(2 * feat, stop - start)
+
+    def project_keys(k):
+        def one_tile(step, carry):
+            here = pl.ds(pl.multiple_of(step * TILE, TILE), TILE)
+            rows = pl.ds(pl.multiple_of(k * rows_dev + step * TILE, TILE), TILE)
+            both = nn(x_all[k, here], weights(wide, 3 * wide))
+            keys = both[:, :wide]
+            values = both[:, wide:] + bias_v
+            keys_t = keys.T
+            values_t = values.T
+            for h in range(heads):
+                part = slice(h * HEAD, (h + 1) * HEAD)
+                k_out[h, rows] = keys[:, part].astype(low)
+                v_out[h, rows] = values[:, part].astype(low)
+                kt_out[h, :, rows] = keys_t[part].astype(low)
+                vt_out[h, :, rows] = values_t[part].astype(low)
+            return carry
+
+        lax.fori_loop(0, per_row, one_tile, 0)
+
+    links.arrive(x_mate_at(row), mate_x, mate)
+    project_keys(row)
+    x_step(3)
+    for slot in (0, 2, 1):
+        k = lax.rem(row + slot + 1, ROWS)
+        links.arrive(x_mate_at(k), mate_x + 1 + slot, mate)
+        project_keys(k)
+
+    def project_query(j, carry):
+        block = 2 * j + lax.rem(j + col, 2)
+        here = pl.ds(pl.multiple_of(lax.rem(block, per_row) * TILE, TILE), TILE)
+        query = nn(x_all[block // per_row, here], weights(0, wide)) + bias_q
+        query = query.astype(low) * jnp.asarray(HEAD**-0.5, low)
+        for h in range(heads):
+            q_out[h, j] = query[:, h * HEAD : (h + 1) * HEAD]
+        return carry
+
+    blocks = row_tiles // 2
+    lax.fori_loop(0, blocks, project_query, 0)
+    w_first(1)
+    for j in range(blocks):
+        block = 2 * j + lax.rem(j + col, 2)
+        rows = pl.ds(pl.multiple_of(block * TILE, TILE), TILE)
+        query_ids = ids[:, rows]
+        length = min(2 * j + NEAR, row_tiles) * TILE
+        clear = 2 * j * TILE
+
+        def one_head(h, carry, j=j, query_ids=query_ids, length=length, clear=clear):
+            scores = nt(k_out[h, :length], q_out[h, j])
+            near = jnp.where(
+                ids_col[clear:length] <= query_ids, scores[clear:], masked_score
+            )
+            top = jnp.max(near, axis=0, keepdims=True)
+            if clear:
+                top = jnp.maximum(top, jnp.max(scores[:clear], axis=0, keepdims=True))
+                weights_far = jnp.exp(scores[:clear] - top)
+            weights_near = jnp.exp(near - top)
+            mass = jnp.sum(weights_near, axis=0, keepdims=True)
+            value = nn(vt_out[h, :, clear:length], weights_near.astype(low))
+            if clear:
+                mass = mass + jnp.sum(weights_far, axis=0, keepdims=True)
+                value = value + nn(vt_out[h, :, :clear], weights_far.astype(low))
+            mixed_out[j, h] = value / mass
+            lse_out[j, h] = top + jnp.log(mass)
+            return carry
+
+        lax.fori_loop(0, heads, one_head, 0)
+        low_out[j] = (
+            jnp.concatenate([mixed_out[j, h] for h in range(heads)], axis=0).T.astype(low)
+        )
+        away = row != j
+        slot = lax.rem(row - j + ROWS + 3, ROWS)
+        links.push(low_out.at[j], context.at[row], swap + slot, at_row(j), away)
+
+        @pl.when(jnp.logical_not(away))
+        def _(j=j):
+            context[row] = low_out[j]
+
+        if j == 1:
+            w_first(2)
+            w_second(1)
+    w_first(3)
+    w_second(2)
+    w_mate(1)
+    w_second(3)
+    w_mate(2)
+    w_mate(3)
+    links.arrive(cot_own.at[:, columns(1 - col, feat)], mate_cot, mate)
     for slot in range(3):
-        k = lax.rem(row + slot + 1, ROWS)
-        for i in range(count):
-            one, two = turn(i, slot)
-            links.arrive(w_at(i, k, dp ^ one), first_w[i] + slot, mate)
-            links.push(w_at(i, k, dp), w_at(i, k, dp), second_w[i] + 2 * slot, at_dp(two))
-            links.push(
-                w_at(i, k, dp ^ one), w_at(i, k, dp ^ one), second_w[i] + 2 * slot + 1, at_dp(two)
-            )
-    for slot in range(3):
-        k = lax.rem(row + slot + 1, ROWS)
-        for i in range(count):
-            one, two = turn(i, slot)
-            links.arrive(w_at(i, k, dp ^ two), second_w[i] + 2 * slot, mate)
-            links.arrive(w_at(i, k, dp ^ 3), second_w[i] + 2 * slot + 1, mate)
-            links.push(row_at(i, k), row_at(i, k), mate_w[i] + 1 + slot, mate)
-    links.arrive(x_mate_at(row), mate_x, mate)
-    links.arrive(cot_own.at[:, columns(1 - col, feat)], mate_cot, mate)
-    links.arrive(vec_all.at[1 - col], mate_vec, mate)
+        links.arrive(context.at[lax.rem(row + slot + 1, ROWS)], swap + slot, mate)
     for i in range(count):
         links.arrive(row_mate_at(i, row), mate_w[i], mate)
-    for slot in range(3):
-        k = lax.rem(row + slot + 1, ROWS)
-        links.arrive(x_mate_at(k), mate_x + 1 + slot, mate)
-        for i in range(count):
+        for slot in range(3):
+            k = lax.rem(row + slot + 1, ROWS)
             links.arrive(row_mate_at(i, k), mate_w[i] + 1 + slot, mate)
     for copy in copies:
         copy.wait()
     links.drain()
 
 
-IN_VMEM = pl.BlockSpec(memory_space=pltpu.VMEM)
-IN_PLACE = pl.BlockSpec(memory_space=pl.ANY)
-
-
-def comm_params(number):
-    return pltpu.CompilerParams(
-        collective_id=number, has_side_effects=True, vmem_limit_bytes=VMEM_BYTES
-    )
-
-
-def gather_all(x, cot, vec, shards):
+def forward_links(x, cot, vec, wq, wk, wv, ids, shards):
     widths = [shard.shape[1] for shard in shards]
     rows, feat = x.shape
-    low = x.dtype
+    low, f32 = x.dtype, jnp.float32
     part = shards[0].shape[0] // 4
+    heads = 2 * feat // HEAD // ROWS
+    wide = heads * HEAD
+    length = ROWS * rows
+    blocks = length // TILE // 2
+    shape = jax.ShapeDtypeStruct
     shapes = [
-        jax.ShapeDtypeStruct((ROWS, rows, 2 * feat), low),
-        jax.ShapeDtypeStruct((rows // 2, 2 * feat), low),
-        jax.ShapeDtypeStruct((2,) + vec.shape, vec.dtype),
-    ] + [jax.ShapeDtypeStruct((ROWS, 4, part, 2 * width), low) for width in widths]
+        shape((ROWS, rows, 2 * feat), low),
+        shape((rows // 2, 2 * feat), low),
+        shape((2,) + vec.shape, vec.dtype),
+        shape((ROWS, 4, part, 3 * wide), low),
+        shape((heads, blocks, TILE, HEAD), low),
+        shape((heads, length, HEAD), low),
+        shape((heads, HEAD, length), low),
+        shape((heads, length, HEAD), low),
+        shape((blocks, heads, HEAD, TILE), f32),
+        shape((blocks, heads, 1, TILE), f32),
+        shape((ROWS, rows // 2, wide), low),
+    ] + [shape((ROWS, 4, part, 2 * width), low) for width in widths]
     return pl.pallas_call(
-        functools.partial(gather_kernel, widths),
+        functools.partial(forward_kernel, widths, heads),
         out_shape=shapes,
-        in_specs=[IN_VMEM] * (3 + len(shards)),
-        out_specs=[IN_PLACE] * len(shapes),
+        in_specs=[IN_VMEM] * (7 + len(shards)),
+        out_specs=[IN_VMEM] * 11 + [IN_PLACE] * len(shards),
         scratch_shapes=[
+            pltpu.VMEM((heads, HEAD, length), low),
+            pltpu.VMEM((length, 1), jnp.int32),
+            pltpu.VMEM((2, 4, part, 3 * wide), low),
+            pltpu.VMEM((blocks, TILE, wide), low),
             pltpu.SemaphoreType.DMA((160,)),
             pltpu.SemaphoreType.DMA((96,)),
-            pltpu.SemaphoreType.DMA((16,)),
+            pltpu.SemaphoreType.DMA((4,)),
         ],
         compiler_params=comm_params(1),
-        name="gather_all",
-    )(x, cot, vec, *[shard.reshape(4, part, -1) for shard in shards])
+        name="forward_links",
+    )(
+        x, cot, vec, wq, wk, wv, ids.reshape(1, -1),
+        *[shard.reshape(4, part, -1) for shard in shards],
+    )
 
 
 def swap_kernel(split, *refs):
@@ -918,109 +1112,6 @@
     )
 
 
-TILE = 256
-NEAR = 3
-
-
-def nt(left, right):
-    return lax.dot_general(
-        left, right, (((1,), (1,)), ((), ())), preferred_element_type=jnp.float32
-    )
-
-
-def nn(left, right):
-    return jnp.dot(left, right, preferred_element_type=jnp.float32)
-
-
-def attend_kernel(
-    heads, x, weights, bias_q, bias_v, ids_col, ids_row,
-    q_out, k_out, kt_out, v_out, vt_out, mixed_out, low_out, lse_out,
-):
-    width = heads * HEAD
-    row_tiles = x.shape[0] // TILE
-    col = lax.axis_index("col")
-    low = x.dtype
-
-    def project_keys(step, carry):
-        rows = pl.ds(pl.multiple_of(step * TILE, TILE), TILE)
-        both = nn(x[rows], weights[:, width:])
-        keys = both[:, :width]
-        values = both[:, width:] + bias_v[...]
-        keys_t = keys.T
-        values_t = values.T
-        for h in range(heads):
-            part = slice(h * HEAD, (h + 1) * HEAD)
-            k_out[h, rows] = keys[:, part].astype(low)
-            v_out[h, rows] = values[:, part].astype(low)
-            kt_out[h, :, rows] = keys_t[part].astype(low)
-            vt_out[h, :, rows] = values_t[part].astype(low)
-        return carry
-
-    lax.fori_loop(0, row_tiles, project_keys, 0)
-    for j in range(row_tiles // 2):
-        block = 2 * j + lax.rem(j + col, 2)
-        rows = pl.ds(pl.multiple_of(block * TILE, TILE), TILE)
-        query = nn(x[rows], weights[:, :width]) + bias_q[...]
-        query = query.astype(low) * jnp.asarray(HEAD**-0.5, low)
-        for h in range(heads):
-            q_out[h, j] = query[:, h * HEAD : (h + 1) * HEAD]
-    for j in range(row_tiles // 2):
-        block = 2 * j + lax.rem(j + col, 2)
-        rows = pl.ds(pl.multiple_of(block * TILE, TILE), TILE)
-        query_ids = ids_row[:, rows]
-        tiles = min(2 * j + NEAR, row_tiles)
-        length = tiles * TILE
-        clear = 2 * j * TILE
-
-        def one_head(h, carry, j=j, query_ids=query_ids, length=length, clear=clear):
-            scores = nt(k_out[h, :length], q_out[h, j])
-            near = jnp.where(
-                ids_col[clear:length] <= query_ids, scores[clear:], masked_score
-            )
-            top = jnp.max(near, axis=0, keepdims=True)
-            if clear:
-                top = jnp.maximum(top, jnp.max(scores[:clear], axis=0, keepdims=True))
-                weights_far = jnp.exp(scores[:clear] - top)
-            weights_near = jnp.exp(near - top)
-            mass = jnp.sum(weights_near, axis=0, keepdims=True)
-            value = nn(vt_out[h, :, clear:length], weights_near.astype(low))
-            if clear:
-                mass = mass + jnp.sum(weights_far, axis=0, keepdims=True)
-                value = value + nn(vt_out[h, :, :clear], weights_far.astype(low))
-            mixed_out[j, h] = value / mass
-            lse_out[j, h] = top + jnp.log(mass)
-            return carry
-
-        lax.fori_loop(0, heads, one_head, 0)
-        low_out[j] = (
-            jnp.concatenate([mixed_out[j, h] for h in range(heads)], axis=0).T.astype(low)
-        )
-
-
-def attend(x, weights, bias_q, bias_v, ids, heads):
-    length = x.shape[0]
-    blocks = length // TILE // 2
-    low, f32 = x.dtype, jnp.float32
-    shape = jax.ShapeDtypeStruct
-    return pl.pallas_call(
-        functools.partial(attend_kernel, heads),
-        out_shape=[
-            shape((heads, blocks, TILE, HEAD), low),
-            shape((heads, length, HEAD), low),
-            shape((heads, HEAD, length), low),
-            shape((heads, length, HEAD), low),
-            shape((heads, HEAD, length), low),
-            shape((blocks, heads, HEAD, TILE), f32),
-            shape((blocks, TILE, heads * HEAD), low),
-            shape((blocks, heads, 1, TILE), f32),
-        ],
-        in_specs=[IN_VMEM] * 6,
-        out_specs=[IN_VMEM] * 8,
-        compiler_params=pltpu.CompilerParams(vmem_limit_bytes=VMEM_BYTES),
-        name="attend",
-    )(x, weights, bias_q, bias_v, ids.reshape(-1, 1), ids.reshape(1, -1))
-
-
 def attend_back_kernel(
     heads, grad_ctx, q, k, kt, v, mixed, lse, ids_col, ids_row, grads, dk, dv
 ):
@@ -1113,40 +1204,30 @@
     own = rows // 2
     heads = features // HEAD // ROWS
     wide = heads * HEAD
-    vectors = jnp.concatenate(
-        [b_query, b_value, b_output, ln1_gain, ln1_bias, b_outer, ln2_gain, ln2_bias, b_inner]
-    )
-    count = vectors.shape[0] // feat
-    vectors = jnp.pad(vectors.reshape(count, feat), ((0, -count % 16), (0, 0)))
-    shards = [
-        jnp.concatenate([w_query, w_key, w_value], axis=1),
-        w_output.T,
-        w_inner,
-        w_outer.T,
+    vectors = [
+        b_query, b_value, b_output, ln1_gain, ln1_bias, b_outer, ln2_gain, ln2_bias, b_inner
     ]
-    x_all, cot, vec_all, w_qkv, w_o, w_1, w_2 = gather_all(
-        layer_input, cotangent, vectors, shards
+    count = sum(vector.shape[0] for vector in vectors) // feat
+    padded, at = 0.0, 0
+    full = (count + -count % 8) * feat
+    for vector in vectors:
+        size = vector.shape[0]
+        padded = padded + jnp.pad(vector.astype(f32), (at, full - at - size))
+        at += size
+    (
+        x_all, cot, vec_all, w_heads, q, k, kt, v, mixed, lse, context, w_o, w_1, w_2,
+    ) = forward_links(
+        layer_input, cotangent, padded.reshape(-1, feat), w_query, w_key, w_value, block_ids,
+        [w_output.T, w_inner, w_outer.T],
     )
     x_all = x_all.reshape(ROWS * rows, features)
-    w_qkv = w_qkv.reshape(features, 2, 3, 2, wide)
-    home, side = row // 2, lax.rem(row, 2)
-    w_heads = lax.dynamic_slice(
-        w_qkv, (0, home, 0, side, 0), (features, 1, 3, 1, wide)
-    ).reshape(features, 3 * wide)
+    w_heads = w_heads.reshape(features, 3 * wide)
     w_o = w_o.reshape(features, features)
     w_1 = w_1.reshape(features, 2 * hidden)
     w_2 = w_2.reshape(features, 2 * hidden)
-    vec_all = vec_all.astype(f32)
     take = lambda start, number=1: vec_all[:, start : start + number].reshape(1, -1)
-    bias_q = lax.dynamic_slice(take(0), (0, row * wide), (1, wide))
-    bias_v = lax.dynamic_slice(take(1), (0, row * wide), (1, wide))
     bias_o, gain_one, shift_one, bias_2, gain_two, shift_two = [take(i) for i in range(2, 8)]
     bias_1 = take(8, count - 8)
-
-    q, k, kt, v, vt, mixed, context_own, lse = attend(
-        x_all, w_heads, bias_q, bias_v, block_ids, heads
-    )
-    (context,) = swap_blocks(context_own, 2)
     context = context.transpose(1, 0, 2).reshape(own, features)
     start = row * rows + lax.rem(row + col, 2) * own
     x_own = lax.dynamic_slice_in_dim(x_all, start, own, 0).astype(f32)

time: 425 us -> 343 us (0.81)
  Pallas kernels: 286 us -> 236 us
  local copies, waits for them, and re-layouts: 62 us -> 30.4 us
    pallas_call x2 -> x1, Pallas kernels: 126 us -> 94.2 us  [forward_links(): pl.pallas_call(functools.partial(forward_kernel, widths, heads), out_shap...]
    pallas_call x2 -> x1, Pallas kernels: 32.8 us -> 15.1 us  [swap_blocks(): pl.pallas_call(functools.partial(swap_kernel, split), out_shape=shapes, i...]
    reshape x4 -> x2, local copies, waits for them, and re-layouts: 16.3 us -> 1.96 us  [the longest x1 1.35 us: attend_back(): ids.reshape(-1, 1)]
    dynamic_slice x3 -> x0, local copies, waits for them, and re-layouts: 9.1 us -> none  [the longest x2 8.46 us: fast_body(): lax.dynamic_slice(w_qkv, (0, home, 0, side, 0), (features, 1, 3, 1, wide))]
    unnamed x101 -> x89, local copies, waits for them, and re-layouts: 9.22 us -> 2.25 us
where the time goes in v2:
time: 343 us; the launch traced here: 336 us
  Pallas kernels  236 us (69%)
  matrix products  44.3 us (13%)
  local copies, waits for them, and re-layouts  30.4 us (9%)
  other arithmetic  23.4 us (7%)
    pallas_call x1, Pallas kernels, reduce_all(): pl.pallas_call(functools.partial(reduce_kernel, count), out_shape=outs, i...  107 us
    pallas_call x1, Pallas kernels, forward_links(): pl.pallas_call(functools.partial(forward_kernel, widths, heads), out_shap...  94.2 us
    pallas_call x1, Pallas kernels, attend_back(): pl.pallas_call(functools.partial(attend_back_kernel, heads), out_shape=ja...  18.8 us
    dot_general x4, matrix products, contract_first(): lax.dot_general(left, right, (((0,), (0,)), ((), ())), preferred_element_...  15.5 us
    pallas_call x1, Pallas kernels, swap_blocks(): pl.pallas_call(functools.partial(swap_kernel, split), out_shape=shapes, i...  15.1 us
    dot_general x4, matrix products, contract_last(): lax.dot_general(left, right, (((1,), (1,)), ((), ())), preferred_element_...  13.3 us
    dot_general x4, matrix products, project(): return jnp.dot(left, right, preferred_element_type=jnp.float32)  12.2 us

profile of v2, /device:TPU:0, one launch (start us, length us, event | category | flops | bytes accessed | tf_op | source)
XLA Modules:
  0.0 336.0 jit_solution(138270639614503390)
XLA Ops:
  0.7 0.9 convert_add_fusion
  2.2 94.2 %forward_links.1 = (bf16[4,512,768]{2,1,0:T(8,128)(2,1)}, bf16[256,768]{1,0:T(8,128)(2,1)}, f32[2,16,384]{2,1,0:T(8,128)}, bf16[4,4,48,576]{3,2,1,0:T(8,128)(2,1...) custom-call(bf16[512,384]{1,0:T(8,128)(2,1)} %x.23, ...), custom_call_target="tpu_custom_call" | custom-call | tf_op jit(solution)/shard_map/forward_links/pallas_call | solution.py:788
  96.5 1.6 slice_reduce_fusion.1
  98.1 1.2 copy.61
  99.3 2.1 multiply_reduce_fusion.6
  102.9 0.7 slice.138
  103.7 5.8 %multiply_convert_fusion = (bf16[256,3072]{1,0:T(8,128)(2,1)S(1)}, f32[256,3072]{1,0:T(8,128)}) fusion(f32[3072]{0:T(1024)S(1)} %add.197, bf16[768,3072]{1,0:T(8,128)(2,1)} %bitcast.116, f32[256,768]{1,0:T(8,128)S(1)} %get-tuple-element.126, f32[768]{0:T(1024)S(1)} %add.194, f32[768]{0:T(1024)S(1)} %mul.231, f32[256]{0:T(256)S(1)} %get-tuple-element.125, ...), kind=kOutput, calls=%fused_computation.12 | convolution fusion | flops 1213661184 | bytes 10244096 | tf_op jit(solution)/shard_map/dot_general | solution.py:31
  109.5 5.1 %multiply_reduce_fusion.5 = (f32[256]{0:T(256)}, f32[256]{0:T(256)}, f32[256,768]{1,0:T(8,128)S(1)}) fusion(f32[768]{0:T(1024)S(1)} %copy-done.30, bf16[256,3072]{1,0:T(8,128)(2,1)S(1)} %get-tuple-element.127, bf16[768,3072]{1,0:T(8,128)(2,1)} %bitcast.120, f32[768]{0:T(1024)S(1)} %add.194, f32[768]{0:T(1024)S(1)} %mul.231, f32[256]{0:T(256)S(1)} %get-tuple-element.124, ...), kind=kOutput, calls=%fused_computation.38 | convolution fusion | flops 1209728512 | bytes 7877632 | tf_op jit(solution)/shard_map/dot_general | solution.py:41
  114.6 1.3 add.206
  117.2 0.9 add_convert_fusion.refs_1_
  118.5 1.3 broadcast_multiply_fusion
  119.8 1.4 fusion.22
  121.2 1.3 fusion.15
  122.5 1.3 divide_subtract_fusion
  124.3 0.8 convolution_reduce_fusion.1
  125.7 1.1 convolution_reduce_fusion
  126.9 1.8 multiply_reduce_fusion.1
  128.8 1.7 fusion.18
  130.5 5.6 %convert_reduce_fusion.1 = (f32[3072]{0:T(1024)S(1)}, bf16[256,3072]{1,0:T(8,128)(2,1)S(1)}) fusion(f32[256,3072]{1,0:T(8,128)S(1)} %copy-done.36, bf16[768,3072]{1,0:T(8,128)(2,1)} %bitcast.121, f32[256,768]{1,0:T(8,128)S(1)} %get-tuple-element.101), kind=kOutput, calls=%fused_computation.11 | convolution fusion | flops 1217590272 | bytes 10235904 | tf_op jit(solution)/shard_map/dot_general | solution.py:31
  136.2 1.7 multiply_reduce_fusion.2
  138.9 1.0 copy.63
  140.0 15.1 %swap_blocks.1 = (bf16[4,256,192]{2,1,0:T(8,128)(2,1)}, bf16[512,384]{1,0:T(8,128)(2,1)}) custom-call(bf16[4,256,192]{2,1,0:T(8,128)(2,1)} %bitcast.103, bf16[256,768]{1,0:T(8,128)(2,1)} %copy-done.5), custom_call_target="tpu_custom_call" | custom-call | tf_op jit(solution)/shard_map/swap_blocks/pallas_call | solution.py:852
  155.1 5.5 %convolution_convert_fusion.1 = bf16[768,3072]{1,0:T(8,128)(2,1)} fusion(bf16[256,3072]{1,0:T(8,128)(2,1)} %copy-done.10, f32[256,768]{1,0:T(8,128)} %copy-done.4, f32[768]{0:T(1024)S(1)} %add.194, f32[768]{0:T(1024)S(1)} %mul.231, f32[256]{0:T(256)S(1)} %copy-done.29, f32[256]{0:T(256)S(1)} %copy-done.27), kind=kOutput, calls=%fused_computation.3 | convolution fusion | flops 1211301888 | bytes 7086080 | tf_op jit(solution)/shard_map/dot_general | solution.py:35
  160.6 3.6 %convolution_convert_fusion = bf16[768,3072]{1,0:T(8,128)(2,1)} fusion(bf16[256,3072]{1,0:T(8,128)(2,1)S(1)} %copy-done.9, f32[256,768]{1,0:T(8,128)S(1)} %copy-done.3), kind=kOutput, calls=%fused_computation.2 | convolution fusion | flops 1210515456 | bytes 7077888 | tf_op jit(solution)/shard_map/dot_general | solution.py:35
  164.2 1.5 convolution_convert_fusion.2
  165.8 1.3 copy.64.ids_col
  167.1 18.8 %attend_back.1 = bf16[2048,576]{1,0:T(8,128)(2,1)} custom-call(bf16[4,256,192]{2,1,0:T(8,128)(2,1)} %get-tuple-element.64.grad_ctx, bf16[3,4,256,64]{3,2,1,0:T(8,128)(2,1)} %get-tuple-element.65.q, bf16[3,2048,64]{2,1,0:T(8,128)(2,1)} %get-tuple-element.66.k, bf16[3,64,2048]{2,1,0:T(8,128)(2,1)} %get-tuple-element.67.kt, ...), custom_call_target="tpu_custom_call" | custom-call | tf_op jit(solution)/shard_map/attend_back/pallas_call | solution.py:1168
  185.9 4.8 %convolution_convert_fusion.3 = bf16[768,576]{0,1:T(8,128)(2,1)S(1)} fusion(bf16[2048,768]{1,0:T(8,128)(2,1)} %bitcast.123, bf16[2048,576]{1,0:T(8,128)(2,1)} %attend_back.1), kind=kOutput, calls=%fused_computation.15 | convolution fusion | flops 1812381696 | bytes 6389760 | tf_op jit(solution)/shard_map/dot_general | solution.py:35
  190.7 1.3 copy.65
  192.0 4.4 %fusion.23 = f32[2048,768]{1,0:T(8,128)S(1)} fusion(bf16[2048,576]{1,0:T(8,128)(2,1)} %attend_back.1, bf16[768,576]{1,0:T(8,128)(2,1)S(1)} %bitcast.124), kind=kOutput, calls=%fused_computation.115 | convolution fusion | flops 1811939328 | bytes 9535488 | tf_op jit(solution)/shard_map/dot_general | solution.py:41
  196.7 1.9 convert_element_type.140
  198.7 2.2 convert_reduce_fusion
  202.3 107.4 %reduce_all.1 = (bf16[4,48,1536]{2,1,0:T(8,128)(2,1)}, bf16[4,48,1536]{2,1,0:T(8,128)(2,1)}, bf16[4,48,384]{2,1,0:T(8,128)(2,1)}, bf16[4,2,48,576]{3,2,1,0:T(8,1...) custom-call(bf16[4,4,48,3072]{3,2,1,0:T(8,128)(2,1)} %bitcast.97, bf16[4,4,48,3072]{3,2,1,0:T(8,128)(2,1)} %bitcast.98, ...), custom_call_target="tpu_custom_call" | custom-call | tf_op jit(solution)/shard_map/reduce_all/pallas_call | solution.py:1085
  309.7 0.8 slice.146
  311.6 1.1 convert_bitcast_fusion.1
  312.7 1.0 copy.66
  313.7 1.8 reshape.299
  315.6 0.8 fusion.20
  316.7 1.0 squeeze.9
  317.7 0.8 slice_bitcast_fusion.1
  319.5 1.0 squeeze.20
  320.8 1.0 squeeze.21
  322.4 0.7 convert_bitcast_fusion.2
  325.1 1.2 bitcast_convert_fusion
  327.7 1.2 convert_bitcast_fusion
  331.4 2.1 multiply_reduce_fusion
  334.3 0.7 copy.89
  335.1 0.7 copy.90
  (146 shorter events, 16.8 us)
Async XLA Ops:
  0.7 117.5 %copy-start = (bf16[768,768]{1,0:T(8,128)(2,1)S(1)}, bf16[768,768]{1,0:T(8,128)(2,1)}, u32[]{:S(2)}) copy-start(bf16[768,768]{1,0:T(8,128)(2,1)} %param.44) | copy-start | bytes 3538948
  96.4 5.1 %copy-start.16 = (bf16[256,768]{1,0:T(8,128)(2,1)S(1)}, bf16[256,768]{1,0:T(8,128)(2,1)}, u32[]{:S(2)}) copy-start(bf16[256,768]{1,0:T(8,128)(2,1)} %get-tuple-element.62) | copy-start | bytes 1179652
  99.3 2.2 copy-start.6
  101.5 36.5 %copy-start.4 = (f32[256,768]{1,0:T(8,128)}, f32[256,768]{1,0:T(8,128)S(1)}, u32[]{:S(2)}) copy-start(f32[256,768]{1,0:T(8,128)S(1)} %get-tuple-element.126) | copy-start | bytes 2359300
  101.5 8.0 %copy-start.26 = (f32[256]{0:T(256)}, f32[256]{0:T(256)S(1)}, u32[]{:S(2)}) copy-start(f32[256]{0:T(256)S(1)} %get-tuple-element.124) | copy-start | bytes 3076
  101.5 7.9 %copy-start.28 = (f32[256]{0:T(256)}, f32[256]{0:T(256)S(1)}, u32[]{:S(2)}) copy-start(f32[256]{0:T(256)S(1)} %get-tuple-element.125) | copy-start | bytes 3076
  103.7 5.8 %copy-start.30 = (f32[768]{0:T(1024)S(1)}, f32[768]{0:T(1024)}, u32[]{:S(2)}) copy-start(f32[768]{0:T(1024)} %add.202) | copy-start | bytes 9220
  109.5 5.1 %copy-start.8 = (bf16[256,3072]{1,0:T(8,128)(2,1)}, bf16[256,3072]{1,0:T(8,128)(2,1)S(1)}, u32[]{:S(2)}) copy-start(bf16[256,3072]{1,0:T(8,128)(2,1)S(1)} %get-tuple-element.127) | copy-start | bytes 4718596
  117.2 9.6 %copy-start.19 = (f32[256]{0:T(256)}, f32[256]{0:T(256)S(1)}, u32[]{:S(2)}) copy-start(f32[256]{0:T(256)S(1)} %get-tuple-element.123) | copy-start | bytes 3076
  118.1 8.7 %copy-start.5 = (bf16[256,768]{1,0:T(8,128)(2,1)}, bf16[256,768]{1,0:T(8,128)(2,1)S(1)}, u32[]{:S(2)}) copy-start(bf16[256,768]{1,0:T(8,128)(2,1)S(1)} %add_convert_fusion.refs_1_) | copy-start | bytes 1179652
  121.2 1.3 copy-start.31
  123.8 0.5 copy-start.33
  126.9 3.6 %copy-start.36 = (f32[256,3072]{1,0:T(8,128)S(1)}, f32[256,3072]{1,0:T(8,128)}, u32[]{:S(2)}) copy-start(f32[256,3072]{1,0:T(8,128)} %get-tuple-element.128) | copy-start | bytes 9437188
  128.8 7.4 %slice-start = ((s8[4718592]{0:T(1024)(128)(4,1)}), s8[4194304]{0:T(1024)(128)(4,1)S(1)}, s32[]{:S(2)}) async-start(s8[4718592]{0:T(1024)(128)(4,1)} %bitcast.117), calls=%async_computation | async-start | bytes 8388608
  130.5 5.7 %copy-start.2 = (f32[256,768]{1,0:T(8,128)}, f32[256,768]{1,0:T(8,128)S(1)}, u32[]{:S(2)}) copy-start(f32[256,768]{1,0:T(8,128)S(1)} %get-tuple-element.101) | copy-start | bytes 2359300
  130.5 5.7 %copy-start.27 = (f32[256]{0:T(256)S(1)}, f32[256]{0:T(256)}, u32[]{:S(2)}) copy-start(f32[256]{0:T(256)} %copy-done.26) | copy-start | bytes 3076
  130.5 5.7 %copy-start.29 = (f32[256]{0:T(256)S(1)}, f32[256]{0:T(256)}, u32[]{:S(2)}) copy-start(f32[256]{0:T(256)} %copy-done.28) | copy-start | bytes 3076
  130.5 5.7 %slice-start.1 = ((s8[4718592]{0:T(1024)(128)(4,1)}), s8[524288]{0:T(1024)(128)(4,1)S(1)}, s32[]{:S(2)}) async-start(s8[4718592]{0:T(1024)(128)(4,1)} %bitcast.117), calls=%async_computation.1 | async-start | bytes 1048576
  136.1 1.8 copy-start.10
  136.2 2.0 copy-start.11
  155.1 5.5 %copy-start.3 = (f32[256,768]{1,0:T(8,128)S(1)}, f32[256,768]{1,0:T(8,128)}, u32[]{:S(2)}) copy-start(f32[256,768]{1,0:T(8,128)} %copy-done.2) | copy-start | bytes 2359300
  155.1 5.5 %copy-start.9 = (bf16[256,3072]{1,0:T(8,128)(2,1)S(1)}, bf16[256,3072]{1,0:T(8,128)(2,1)}, u32[]{:S(2)}) copy-start(bf16[256,3072]{1,0:T(8,128)(2,1)} %copy-done.8) | copy-start | bytes 4718596
  160.6 3.6 %copy-start.7 = (bf16[256,4,192]{0,2,1:T(8,128)(2,1)S(1)}, bf16[256,4,192]{0,2,1:T(8,128)(2,1)}, u32[]{:S(2)}) copy-start(bf16[256,4,192]{0,2,1:T(8,128)(2,1)} %copy-done.6) | copy-start | bytes 1179652
  160.6 5.1 %copy-start.18 = (s32[2048]{0:T(1024)S(1)}, s32[2048]{0:T(1024)}, u32[]{:S(2)}) copy-start(s32[2048]{0:T(1024)} %param.28) | copy-start | bytes 24580
  185.9 6.1 %copy-start.35 = (bf16[4,4,48,576]{3,2,1,0:T(8,128)(2,1)S(1)}, bf16[4,4,48,576]{3,2,1,0:T(8,128)(2,1)}, u32[]{:S(2)}) copy-start(bf16[4,4,48,576]{3,2,1,0:T(8,128)(2,1)} %get-tuple-element.71) | copy-start | bytes 2654212
  196.6 4.6 %copy-start.22 = (f32[768]{0:T(1024)S(1)}, f32[768]{0:T(1024)}, u32[]{:S(2)}) copy-start(f32[768]{0:T(1024)} %get-tuple-element.100) | copy-start | bytes 9220
  196.6 4.6 %copy-start.21 = (f32[768]{0:T(1024)S(1)}, f32[768]{0:T(1024)}, u32[]{:S(2)}) copy-start(f32[768]{0:T(1024)} %get-tuple-element.78) | copy-start | bytes 9220
  196.6 4.6 %copy-start.20 = (f32[768]{0:T(1024)S(1)}, f32[768]{0:T(1024)}, u32[]{:S(2)}) copy-start(f32[768]{0:T(1024)} %get-tuple-element.84) | copy-start | bytes 9220
  196.7 4.6 %copy-start.32 = (f32[3]{0:T(128)S(1)}, f32[3]{0:T(128)}, u32[]{:S(2)}) copy-start(f32[3]{0:T(128)} %copy-done.31) | copy-start | bytes 40
  196.7 4.6 %copy-start.34 = (f32[3]{0:T(128)S(1)}, f32[3]{0:T(128)}, u32[]{:S(2)}) copy-start(f32[3]{0:T(128)} %copy-done.33) | copy-start | bytes 40
  196.7 4.7 %copy-start.23 = (f32[768]{0:T(1024)S(1)}, f32[768]{0:T(1024)}, u32[]{:S(2)}) copy-start(f32[768]{0:T(1024)} %get-tuple-element.98) | copy-start | bytes 9220
  196.7 4.7 %copy-start.24 = (f32[768]{0:T(1024)S(1)}, f32[768]{0:T(1024)}, u32[]{:S(2)}) copy-start(f32[768]{0:T(1024)} %get-tuple-element.135) | copy-start | bytes 9220
  196.7 4.7 %copy-start.25 = (f32[768]{0:T(1024)S(1)}, f32[768]{0:T(1024)}, u32[]{:S(2)}) copy-start(f32[768]{0:T(1024)} %get-tuple-element.96) | copy-start | bytes 9220
  315.5 6.9 %copy-start.17 = (bf16[4,48,384]{2,1,0:T(8,128)(2,1)S(1)}, bf16[4,48,384]{2,1,0:T(8,128)(2,1)}, u32[]{:S(2)}) copy-start(bf16[4,48,384]{2,1,0:T(8,128)(2,1)} %get-tuple-element.75) | copy-start | bytes 442372
  315.5 9.6 %copy-start.13 = (bf16[4,48,1536]{2,1,0:T(8,128)(2,1)S(1)}, bf16[4,48,1536]{2,1,0:T(8,128)(2,1)}, u32[]{:S(2)}) copy-start(bf16[4,48,1536]{2,1,0:T(8,128)(2,1)} %get-tuple-element.76) | copy-start | bytes 1769476
  316.7 11.0 %copy-start.12 = (bf16[4,48,1536]{2,1,0:T(8,128)(2,1)S(1)}, bf16[4,48,1536]{2,1,0:T(8,128)(2,1)}, u32[]{:S(2)}) copy-start(bf16[4,48,1536]{2,1,0:T(8,128)(2,1)} %get-tuple-element.77) | copy-start | bytes 1769476
  323.2 11.1 %copy-start.14 = (bf16[512,384]{1,0:T(8,128)(2,1)S(1)}, bf16[512,384]{1,0:T(8,128)(2,1)}, u32[]{:S(2)}) copy-start(bf16[512,384]{1,0:T(8,128)(2,1)} %get-tuple-element.158) | copy-start | bytes 1179652
  325.1 9.9 %copy-start.15 = (bf16[512,384]{1,0:T(8,128)(2,1)S(1)}, bf16[512,384]{1,0:T(8,128)(2,1)}, u32[]{:S(2)}) copy-start(bf16[512,384]{1,0:T(8,128)(2,1)} %get-tuple-element.160) | copy-start | bytes 1179652
  325.1 10.7 %copy-start.1 = (bf16[768,768]{1,0:T(8,128)(2,1)S(1)}, bf16[768,768]{1,0:T(8,128)(2,1)}, u32[]{:S(2)}) copy-start(bf16[768,768]{1,0:T(8,128)(2,1)} %param.44) | copy-start | bytes 3538948

commit v3 on v2

--- a/solution.py
+++ b/solution.py
@@ -490,10 +490,8 @@
 def forward_kernel(widths, heads, x, cot, vec, wq, wk, wv, ids, *refs):
     count = len(widths)
     shards, refs = refs[:count], refs[count:]
-    x_all, cot_own, vec_all, w_heads, q_out, k_out, kt_out, v_out, mixed_out, lse_out, context = (
-        refs[:11]
-    )
-    fulls, refs = refs[11 : 11 + count], refs[11 + count :]
+    x_all, cot_own, vec_all, w_heads, q_out, kv_out, kt_out, mixed_out, lse_out, context = refs[:10]
+    fulls, refs = refs[10 : 10 + count], refs[10 + count :]
     vt_out, ids_col, packs, low_out, send, recv, local = refs
     dp, row, col = place()
     links = Links(send, recv)
@@ -536,10 +534,12 @@
     relay(1, x, x_at, line_x)
     links.push(x, x_at(row), mate_x, mate)
     for j in range(2):
-        part = slice(j * wide, (j + 1) * wide)
-        packs[j] = jnp.concatenate(
-            [wq[:, part], wk[:, part], wv[:, part]], axis=1
-        ).reshape(packs.shape[1:])
+        pieces = []
+        for h in range(heads):
+            part = slice(j * wide + h * HEAD, j * wide + (h + 1) * HEAD)
+            pieces += [wk[:, part], wv[:, part]]
+        pieces.append(wq[:, j * wide : (j + 1) * wide])
+        packs[j] = jnp.concatenate(pieces, axis=1).reshape(packs.shape[1:])
     for j in range(2):
         k = 2 * col + j
         away = k != row
@@ -661,23 +661,23 @@
         side == 0, vec_all[home, n : n + 1, :wide], vec_all[home, n : n + 1, wide : 2 * wide]
     )
     bias_q, bias_v = bias_of(0), bias_of(1)
+    blank = jnp.zeros((1, HEAD), jnp.float32)
+    bias_kv = jnp.concatenate(
+        sum([[blank, bias_v[:, h * HEAD : (h + 1) * HEAD]] for h in range(heads)], []), axis=1
+    )
     weights = lambda start, stop: w_heads[:, :, :, start:stop].reshape(2 * feat, stop - start)
 
     def project_keys(k):
         def one_tile(step, carry):
             here = pl.ds(pl.multiple_of(step * TILE, TILE), TILE)
             rows = pl.ds(pl.multiple_of(k * rows_dev + step * TILE, TILE), TILE)
-            both = nn(x_all[k, here], weights(wide, 3 * wide))
-            keys = both[:, :wide]
-            values = both[:, wide:] + bias_v
-            keys_t = keys.T
-            values_t = values.T
+            both = nn(x_all[k, here], weights(0, 2 * wide)) + bias_kv
+            both_t = both.T
             for h in range(heads):
-                part = slice(h * HEAD, (h + 1) * HEAD)
-                k_out[h, rows] = keys[:, part].astype(low)
-                v_out[h, rows] = values[:, part].astype(low)
-                kt_out[h, :, rows] = keys_t[part].astype(low)
-                vt_out[h, :, rows] = values_t[part].astype(low)
+                at = 2 * h * HEAD
+                kv_out[h, rows] = both[:, at : at + 2 * HEAD].astype(low)
+                kt_out[h, :, rows] = both_t[at : at + HEAD].astype(low)
+                vt_out[h, :, rows] = both_t[at + HEAD : at + 2 * HEAD].astype(low)
             return carry
 
         lax.fori_loop(0, per_row, one_tile, 0)
@@ -689,19 +689,23 @@
         k = lax.rem(row + slot + 1, ROWS)
         links.arrive(x_mate_at(k), mate_x + 1 + slot, mate)
         project_keys(k)
+        if slot == 2:
+            w_first(1)
 
     def project_query(j, carry):
         block = 2 * j + lax.rem(j + col, 2)
         here = pl.ds(pl.multiple_of(lax.rem(block, per_row) * TILE, TILE), TILE)
-        query = nn(x_all[block // per_row, here], weights(0, wide)) + bias_q
+        query = nn(x_all[block // per_row, here], weights(2 * wide, 3 * wide)) + bias_q
         query = query.astype(low) * jnp.asarray(HEAD**-0.5, low)
         for h in range(heads):
-            q_out[h, j] = query[:, h * HEAD : (h + 1) * HEAD]
+            q_out[h, j] = jnp.concatenate(
+                [query[:, h * HEAD : (h + 1) * HEAD], jnp.zeros((TILE, HEAD), low)], axis=1
+            )
         return carry
 
     blocks = row_tiles // 2
     lax.fori_loop(0, blocks, project_query, 0)
-    w_first(1)
+    w_first(2)
     for j in range(blocks):
         block = 2 * j + lax.rem(j + col, 2)
         rows = pl.ds(pl.multiple_of(block * TILE, TILE), TILE)
@@ -710,7 +714,7 @@
         clear = 2 * j * TILE
 
         def one_head(h, carry, j=j, query_ids=query_ids, length=length, clear=clear):
-            scores = nt(k_out[h, :length], q_out[h, j])
+            scores = nt(kv_out[h, :length], q_out[h, j])
             near = jnp.where(
                 ids_col[clear:length] <= query_ids, scores[clear:], masked_score
             )
@@ -740,14 +744,15 @@
         def _(j=j):
             context[row] = low_out[j]
 
+        if j == 0:
+            w_second(1)
         if j == 1:
-            w_first(2)
-            w_second(1)
-    w_first(3)
-    w_second(2)
-    w_mate(1)
-    w_second(3)
-    w_mate(2)
+            w_first(3)
+            w_second(2)
+            w_mate(1)
+        if j == 2:
+            w_second(3)
+            w_mate(2)
     w_mate(3)
     links.arrive(cot_own.at[:, columns(1 - col, feat)], mate_cot, mate)
     for slot in range(3):
@@ -777,10 +782,9 @@
         shape((rows // 2, 2 * feat), low),
         shape((2,) + vec.shape, vec.dtype),
         shape((ROWS, 4, part, 3 * wide), low),
-        shape((heads, blocks, TILE, HEAD), low),
-        shape((heads, length, HEAD), low),
+        shape((heads, blocks, TILE, 2 * HEAD), low),
+        shape((heads, length, 2 * HEAD), low),
         shape((heads, HEAD, length), low),
-        shape((heads, length, HEAD), low),
         shape((blocks, heads, HEAD, TILE), f32),
         shape((blocks, heads, 1, TILE), f32),
         shape((ROWS, rows // 2, wide), low),
@@ -789,7 +793,7 @@
         functools.partial(forward_kernel, widths, heads),
         out_shape=shapes,
         in_specs=[IN_VMEM] * (7 + len(shards)),
-        out_specs=[IN_VMEM] * 11 + [IN_PLACE] * len(shards),
+        out_specs=[IN_VMEM] * 10 + [IN_PLACE] * len(shards),
         scratch_shapes=[
             pltpu.VMEM((heads, HEAD, length), low),
             pltpu.VMEM((length, 1), jnp.int32),
@@ -807,63 +811,6 @@
     )
 
 
-def swap_kernel(split, *refs):
-    blocks, out_blocks = refs[0], refs[1 + split]
-    send, recv, local = refs[-3:]
-    dp, row, col = place()
-    links = Links(send, recv)
-    mate = (dp, row, 1 - col)
-    peers = [lax.rem(row + k, ROWS) for k in (1, 2, 3)]
-    meet([(dp, peer, col) for peer in peers] + ([mate] if split else []))
-    base = links.slots(4)
-    for number, peer in enumerate(peers):
-        links.push(blocks.at[peer], out_blocks.at[row], base + 2 - number, (dp, peer, col))
-    keep = [pltpu.make_async_copy(blocks.at[row], out_blocks.at[row], local.at[0])]
-    if split:
-        whole, halves = refs[1], refs[3]
-        half, feat = whole.shape[0], whole.shape[1] // 2
-        mine = lax.rem(row + col, 2)
-        own_rows = pl.ds(pl.multiple_of(mine * half, 128), half)
-        keep.append(
-            pltpu.make_async_copy(
-                whole.at[:, columns(col, feat)], halves.at[own_rows], local.at[1]
-            )
-        )
-        links.push(whole.at[:, columns(1 - col, feat)], halves.at[own_rows], base + 3, mate)
-        other_rows = pl.ds(pl.multiple_of((1 - mine) * half, 128), half)
-    for copy in keep:
-        copy.start()
-    for number, peer in enumerate(peers):
-        links.arrive(out_blocks.at[peer], base + number, mate)
-    if split:
-        links.arrive(halves.at[other_rows], base + 3, mate)
-    for copy in keep:
-        copy.wait()
-    links.drain()
-
-
-def swap_blocks(blocks, number, whole=None):
-    split = 0 if whole is None else 1
-    shapes = [jax.ShapeDtypeStruct(blocks.shape, blocks.dtype)]
-    if split:
-        shapes.append(
-            jax.ShapeDtypeStruct((2 * whole.shape[0], whole.shape[1] // 2), whole.dtype)
-        )
-    return pl.pallas_call(
-        functools.partial(swap_kernel, split),
-        out_shape=shapes,
-        in_specs=[IN_VMEM] * (1 + split),
-        out_specs=[IN_VMEM] * (1 + split),
-        scratch_shapes=[
-            pltpu.SemaphoreType.DMA((4,)),
-            pltpu.SemaphoreType.DMA((4,)),
-            pltpu.SemaphoreType.DMA((2,)),
-        ],
-        compiler_params=comm_params(number),
-        name="swap_blocks",
-    )(blocks, *([whole] if split else []))
-
-
 def add_into(total, *others):
     def one(step, carry):
         value = total[step].astype(jnp.float32)
@@ -875,305 +822,669 @@
     lax.fori_loop(0, total.shape[0], one, 0)
 
 
-def reduce_kernel(count, *refs):
-    grads, refs = refs[:count], refs[count:]
-    gq, dx, vec = refs[:3]
-    outs, refs = refs[3 : 3 + count], refs[3 + count :]
-    out_q, out_x, out_vec = refs[:3]
-    refs = refs[3:]
-    sums, refs = refs[:count], refs[count:]
-    first, refs = refs[: count + 1], refs[count + 1 :]
-    second, refs = refs[: count + 1], refs[count + 1 :]
-    lines, refs = refs[:count], refs[count:]
-    sum_q, all_q, sum_x, line_x, vec_mate, vec_line, vec_flat, send, recv = refs
+def middle_kernel(
+    heads, context_in, cot, vec_all, labels, b_pooler, w_classes, b_classes, w_pooler,
+    w_o, x_all, w_1_far, w_2_far,
+    output, late, stream_out, grad_pre_out, branch_two_out, activ_out, branch_one_out, context,
+    grad_blocks, packed, x_own, w_1, w_2, slope, total, sems,
+):
+    f32, low = jnp.float32, output.dtype
+    dp, row, col = place()
+    own, features = output.shape
+    wide = features // ROWS
+    hidden = w_1.shape[1]
+    chunk = features
+    mine = lax.rem(row + col, 2)
+    copies = [
+        pltpu.make_async_copy(
+            x_all.at[row, pl.ds(pl.multiple_of(mine * own, 128), own)], x_own, sems.at[0]
+        ),
+        pltpu.make_async_copy(w_1_far, w_1, sems.at[1]),
+        pltpu.make_async_copy(w_2_far, w_2, sems.at[2]),
+    ]
+    for copy in copies:
+        copy.start()
+    vector = lambda n: jnp.concatenate([vec_all[0, n : n + 1], vec_all[1, n : n + 1]], axis=1)
+    context[...] = jnp.concatenate([context_in[r] for r in range(ROWS)], axis=1)
+    value = nt(context[...], w_o[...])
+    copies[0].wait()
+    hidden_one = x_own[...].astype(f32) + value + vector(2)
+    gain_one, gain_two = vector(3), vector(6)
+    stream, normed_one, inv_one = norm_rows(hidden_one, gain_one, vector(4))
+    late[...] = stream
+    stream_out[...] = stream.astype(low)
+    total[...] = jnp.zeros_like(total)
+    bias_1 = [
+        jnp.concatenate(
+            [vec_all[c, 8 + 2 * n : 9 + 2 * n], vec_all[c, 9 + 2 * n : 10 + 2 * n]], axis=1
+        )
+        for c in range(2)
+        for n in range(hidden // chunk // 2)
+    ]
+    copies[1].wait()
+    copies[2].wait()
+    for n in range(hidden // chunk):
+        span = slice(n * chunk, (n + 1) * chunk)
+        pre_act = nn(stream_out[...], w_1[:, span]) + bias_1[n]
+        half = 0.5 * (1.0 + lax.erf(pre_act * root_half))
+        slope[:, span] = half + pre_act * inv_root_tau * jnp.exp(-0.5 * pre_act * pre_act)
+        activ_out[:, span] = (pre_act * half).astype(low)
+        total[...] += nt(activ_out[:, span], w_2[:, span])
+    hidden_two = late[...] + total[...] + vector(5)
+    result, normed_two, inv_two = norm_rows(hidden_two, gain_two, vector(7))
+    output[...] = result.astype(low)
+
+    classes = b_classes.shape[1]
+    first = output[:8]
+    pooled = jnp.tanh(nn(first, w_pooler[...])[:1] + b_pooler[...].astype(f32))
+    lane = lax.broadcasted_iota(jnp.int32, (1, 128), 1)
+    logits = jnp.full((1, 128), masked_score, f32)
+    rows = [w_classes[n : n + 1].astype(f32) for n in range(classes)]
+    for n in range(classes):
+        logit = jnp.sum(pooled * rows[n], axis=1, keepdims=True) + b_classes[:, n : n + 1].astype(f32)
+        logits = jnp.where(lane == n, logit, logits)
+    odds = jnp.exp(logits - jnp.max(logits, axis=1, keepdims=True))
+    odds = odds / jnp.sum(odds, axis=1, keepdims=True)
+    grad_logits = odds - (lane == labels[0, 0]).astype(f32)
+    grad_pool = jnp.zeros((1, features), f32)
+    for n in range(classes):
+        grad_pool = grad_pool + grad_logits[:, n : n + 1] * rows[n]
+    grad_pool = grad_pool * (1.0 - pooled * pooled)
+    high = grad_pool.astype(low)
+    rest = grad_pool - high.astype(f32)
+    mid = rest.astype(low)
+    last = (rest - mid.astype(f32)).astype(low)
+    split = jnp.concatenate(
+        [high.astype(f32), mid.astype(f32), last.astype(f32), jnp.zeros((5, features), f32)]
+    ).astype(low)
+    grad_first = jnp.sum(nt(split, w_pooler[...]), axis=0, keepdims=True)
+    holder = ((row == 0) & (col == 0)).astype(f32)
+    top = (lax.broadcasted_iota(jnp.int32, (own, 1), 0) == 0).astype(f32) * holder
+    grad_result = cot[...].astype(f32) + top * grad_first
+
+    tokens = lambda values: jnp.sum(values, axis=0, keepdims=True)
+    g_gain_two, g_shift_two = tokens(grad_result * normed_two), tokens(grad_result)
+    grad_two = norm_rows_back(grad_result, normed_two, inv_two, gain_two)
+    g_bias_two = tokens(grad_two)
+    late[...] = grad_two
+    branch_two_out[...] = grad_two.astype(low)
+    total[...] = jnp.zeros_like(total)
+    g_bias_one = []
+    for n in range(hidden // chunk):
+        span = slice(n * chunk, (n + 1) * chunk)
+        grad_pre = (nn(branch_two_out[...], w_2[:, span]) * slope[:, span]).astype(low)
+        grad_pre_out[:, span] = grad_pre
+        g_bias_one.append(tokens(grad_pre.astype(f32)))
+        total[...] += nt(grad_pre_out[:, span], w_1[:, span])
+    grad_stream = late[...] + total[...]
+    g_gain_one, g_shift_one = tokens(grad_stream * normed_one), tokens(grad_stream)
+    grad_one = norm_rows_back(grad_stream, normed_one, inv_one, gain_one)
+    late[...] = grad_one
+    branch_one_out[...] = grad_one.astype(low)
+    grad_context = nn(branch_one_out[...], w_o[...]).astype(low)
+    for r in range(ROWS):
+        grad_blocks[r] = grad_context[:, r * wide : (r + 1) * wide]
+
+    feat = features // 2
+    packed[...] = jnp.zeros_like(packed)
+    vectors = [tokens(grad_one), g_gain_one, g_shift_one, g_bias_two, g_gain_two, g_shift_two]
+    for n, value in enumerate(vectors):
+        for c in range(2):
+            packed[8 + 8 * c + n // 2, pl.ds((n % 2) * feat, feat)] = value[
+                0, c * feat : (c + 1) * feat
+            ]
+    for n, value in enumerate(g_bias_one):
+        packed[8 + 8 * (n // 2) + 3 + n % 2] = value[0]
+    spare = jnp.zeros((1, features - 128), f32)
+    shifted = pltpu.roll(jnp.where(lane < classes, grad_logits, 0.0), classes, 1)
+    tail = jnp.concatenate([jnp.where(lane < classes, logits, shifted), spare], axis=1)
+    for n, value in enumerate((first[:1].astype(f32), grad_pool, pooled, tail)):
+        here = lax.broadcasted_iota(jnp.int32, (4, features), 0) == dp
+        packed[24 + 4 * n : 28 + 4 * n] = jnp.where(here, value * holder, 0.0)
+
+
+def middle(
+    context, cot, vec_all, labels, b_pooler, w_classes, b_classes, w_pooler, w_o, x_all, w_1, w_2
+):
+    low, f32 = cot.dtype, jnp.float32
+    own, features = cot.shape
+    hidden = w_1.shape[1]
+    heads = features // HEAD // ROWS
+    shape = jax.ShapeDtypeStruct
+    narrow, broad = shape((own, features), low), shape((own, hidden), low)
+    return pl.pallas_call(
+        functools.partial(middle_kernel, heads),
+        out_shape=[
+            narrow, shape((own, features), f32), narrow, broad, narrow, broad, narrow, narrow,
+            shape((ROWS, own, features // ROWS), low), shape((40, features), f32),
+        ],
+        in_specs=[IN_VMEM] * 3 + [pl.BlockSpec(memory_space=pltpu.SMEM)] + [IN_VMEM] * 5
+        + [IN_PLACE] * 3,
+        out_specs=[IN_VMEM] * 10,
+        scratch_shapes=[
+            pltpu.VMEM((own, features), low),
+            pltpu.VMEM((features, hidden), low),
+            pltpu.VMEM((features, hidden), low),
+            pltpu.VMEM((own, hidden), f32),
+            pltpu.VMEM((own, features), f32),
+            pltpu.SemaphoreType.DMA((3,)),
+        ],
+        compiler_params=pltpu.CompilerParams(vmem_limit_bytes=VMEM_BYTES),
+        name="middle",
+    )(
+        context, cot, vec_all, labels.reshape(1, 1), b_pooler.reshape(1, -1), w_classes.T,
+        b_classes.reshape(1, -1), w_pooler, w_o, x_all, w_1, w_2,
+    )
+
+
+CHUNK = 384
+
+
+def backward_kernel(
+    heads, blocks_in, output, late, stream, grad_pre, branch_two, activ, branch_one, context,
+    q, kv, kt, mixed, lse, ids, x_all, w_heads, vec_in, *refs,
+):
+    out_g, refs = refs[:5], refs[5:]
+    out_q, out_x, halves, vec, refs = refs[0], refs[1], refs[2], refs[3], refs[4:]
+    pairs, refs = refs[:5], refs[5:]
+    mates, refs = refs[:5], refs[5:]
+    first, refs = refs[:6], refs[6:]
+    second, refs = refs[:6], refs[6:]
+    lines, refs = refs[:5], refs[5:]
+    (
+        grad_ctx, both, delta, dq, dkv, grads, grads_t, w_t, turned, ids_col, dx, sum_x,
+        line_x, gq, sum_q, all_q, vec_mate, vec_line, vec_flat, send, recv,
+    ) = refs
     dp, row, col = place()
     links = Links(send, recv)
+    low, f32 = q.dtype, jnp.float32
     mate = (dp, row, 1 - col)
-    peers = [lax.rem(row + k, ROWS) for k in (1, 2, 3)]
+    peers = [lax.rem(row + n, ROWS) for n in (1, 2, 3)]
     at_row = lambda other: (dp, other, col)
     at_dp = lambda flip: (dp ^ flip, row, col)
-    owner = row // 2
+    home, side = row // 2, lax.rem(row, 2)
+    mine = lax.rem(row + col, 2)
+    length = kv.shape[1]
+    wide = heads * HEAD
+    rows_dev, feat = out_x.shape
+    half = rows_dev // 2
+    row_tiles = length // TILE
+    blocks = row_tiles // 2
     meet(
         [at_row(peer) for peer in peers]
         + [at_dp(1), at_dp(2), mate]
         + [(dp, peer, 1 - col) for peer in peers]
     )
-    widths = [grad.shape[3] // 2 for grad in grads]
-    feat = dx.shape[2] // 2
-    turns = [(1, 2) if i % 2 == 0 else (2, 1) for i in range(count + 1)]
-
-    slot_x, slot_q, slot_v = links.slots(1), links.slots(1), links.slots(1)
-    slot_g = [links.slots(1) for _ in grads]
-    links.push(vec, vec_mate, slot_v, mate)
-    links.push(dx.at[:, :, columns(1 - col, feat)], sum_x, slot_x, mate)
-    links.push(gq.at[:, 1 - col], sum_q, slot_q, mate)
-    for i in range(count):
-        links.push(grads[i].at[:, :, :, columns(1 - col, widths[i])], sums[i], slot_g[i], mate)
-
-    links.arrive(vec_mate, slot_v, mate)
-    out_vec[...] = vec[...] + vec_mate[...]
-    slot_vl = links.slots(3)
+
+    swap, slot_o = links.slots(3), links.slots(1)
     for n, peer in enumerate(peers):
-        links.push(out_vec, vec_line.at[2 - n], slot_vl + 2 - n, at_row(peer))
-
-    links.arrive(sum_x, slot_x, mate)
-    tile = dx.shape[1] // 4
-
-    def add_x(step, carry):
-        rows = pl.ds(pl.multiple_of((step % 4) * tile, 128), tile)
-        sum_x[step // 4, rows] = (
-            sum_x[step // 4, rows].astype(jnp.float32)
-            + dx[step // 4, rows, columns(col, feat)].astype(jnp.float32)
-        ).astype(sum_x.dtype)
-        return carry
-
-    lax.fori_loop(0, 16, add_x, 0)
-    slot_xl = links.slots(3)
-    for n, peer in enumerate(peers):
-        links.push(sum_x.at[peer], line_x.at[2 - n], slot_xl + 2 - n, at_row(peer))
-
-    links.arrive(sum_q, slot_q, mate)
-
-    def add_q(step, carry):
-        sum_q[step] = (
-            sum_q[step].astype(jnp.float32) + gq[step, col].astype(jnp.float32)
-        ).astype(sum_q.dtype)
-        return carry
-
-    lax.fori_loop(0, 4, add_q, 0)
-    slot_ql = links.slots(4)
-    side = lax.rem(row, 2)
-    own_part = all_q.at[side, pl.ds(2 * col, 2)]
-    at_home = owner == col
-
-    def keep_own():
-        own_part[...] = sum_q[row]
-
-    pl.when(at_home)(keep_own)
-    links.push(sum_q.at[row], own_part, slot_ql + 2 * side + col, mate, jnp.logical_not(at_home))
-    for peer in peers:
-        links.push(sum_q.at[peer], own_part, slot_ql + 2 * side + col, (dp, peer, owner))
-
-    def send_first(i, total):
+        links.push(blocks_in.at[peer], grad_ctx.at[row], swap + 2 - n, at_row(peer))
+    own_rows = pl.ds(pl.multiple_of(mine * half, 128), half)
+    other_rows = pl.ds(pl.multiple_of((1 - mine) * half, 128), half)
+    links.push(output.at[:, columns(1 - col, feat)], halves.at[own_rows], slot_o, mate)
+    halves[own_rows] = output[:, columns(col, feat)]
+    grad_ctx[row] = blocks_in[row]
+
+    lefts = (stream, branch_two, branch_one)
+    for n in range(3):
+        turned[n] = lefts[n][...].astype(f32).T.astype(low)
+    feeds = [(0, grad_pre, 0), (1, activ, 0), (0, grad_pre, 1), (1, activ, 1), (2, context, 0)]
+    turns = [(1, 2), (2, 1), (1, 2), (2, 1), (1, 2), (2, 1)]
+    widths = [out.shape[2] for out in out_g]
+    slot_g = [links.slots(1) for _ in widths]
+
+    def local_grad(i):
+        left, right, part = feeds[i]
+        width = widths[i]
+        per = width // CHUNK
+
+        def one(step, carry):
+            which, n = step // per, step % per
+            core = jnp.where(which == 0, 1 - col, col)
+            start = core * (right.shape[1] // 2) + part * width + n * CHUNK
+            value = nn(turned[left], right[:, pl.ds(pl.multiple_of(start, 128), CHUNK)])
+            pairs[i][which, :, :, :, pl.ds(pl.multiple_of(n * CHUNK, 128), CHUNK)] = (
+                value.astype(low).reshape(pairs[i].shape[1:4] + (CHUNK,))
+            )
+            return carry
+
+        lax.fori_loop(0, 2 * per, one, 0)
+        links.push(pairs[i].at[0], mates[i], slot_g[i], mate)
+
+    totals = [pair.at[1] for pair in pairs] + [all_q]
+
+    def send_first(i):
         one, two = turns[i]
         base = links.slots(2)
-        links.push(total.at[:, dp ^ one], first[i].at[0], base, at_dp(one))
-        links.push(total.at[:, dp ^ 3], first[i].at[1], base + 1, at_dp(one))
+        links.push(totals[i].at[:, dp ^ 3], first[i].at[1], base + 1, at_dp(one))
+        links.push(totals[i].at[:, dp ^ one], first[i].at[0], base, at_dp(one))
         return base
 
-    def send_second(i, total, base):
+    def join(i):
+        links.arrive(mates[i], slot_g[i], mate)
+
+        def one(step, carry):
+            at, q_at = step // 4, step % 4
+            pairs[i][1, at, q_at] = (
+                pairs[i][1, at, q_at].astype(f32) + mates[i][at, q_at].astype(f32)
+            ).astype(low)
+            return carry
+
+        lax.fori_loop(0, 16, one, 0)
+        return send_first(i)
+
+    def send_second(i, base):
         one, two = turns[i]
         links.arrive(first[i].at[1], base + 1, mate)
-        add_into(total.at[:, dp ^ two], first[i].at[1])
+        add_into(totals[i].at[:, dp ^ two], first[i].at[1])
         slot = links.slots(1)
-        links.push(total.at[:, dp ^ two], second[i], slot, at_dp(two))
+        links.push(totals[i].at[:, dp ^ two], second[i], slot, at_dp(two))
         links.arrive(first[i].at[0], base, mate)
-        add_into(total.at[:, dp], first[i].at[0])
+        add_into(totals[i].at[:, dp], first[i].at[0])
         return slot
+
+    def send_line(i, slot):
+        links.arrive(second[i], slot, mate)
+        add_into(totals[i].at[:, dp], second[i])
+        base = links.slots(3)
+        for n, peer in enumerate(peers):
+            links.push(totals[i].at[peer, dp], lines[i].at[2 - n], base + 2 - n, at_row(peer))
+        return base
 
     def share(i, out):
         one, two = turns[i]
         base = links.slots(3)
         links.push(out.at[dp], out.at[dp], base, at_dp(two))
         links.push(out.at[dp], out.at[dp], base + 1, at_dp(one))
+        return base
+
+    def share_on(i, out, base):
+        one, two = turns[i]
         links.arrive(out.at[dp ^ two], base, mate)
         links.push(out.at[dp ^ two], out.at[dp ^ two], base + 2, at_dp(one))
-        return base
 
     def shared(i, out, base):
         one, two = turns[i]
         links.arrive(out.at[dp ^ one], base + 1, mate)
         links.arrive(out.at[dp ^ 3], base + 2, mate)
 
-    started = []
-    for i in range(count):
-        links.arrive(sums[i], slot_g[i], mate)
-        width = widths[i]
-
-        def add_g(step, carry, i=i, width=width):
-            k, q = step // 4, step % 4
-            sums[i][k, q] = (
-                sums[i][k, q].astype(jnp.float32)
-                + grads[i][k, q, :, columns(col, width)].astype(jnp.float32)
-            ).astype(sums[i].dtype)
+    stage = [None] * 6
+    local_grad(0)
+    local_grad(1)
+    w_t[...] = w_heads[...].reshape(2 * feat, 3 * wide).astype(f32).T.astype(low)
+
+    def split_ids(step, carry):
+        span = pl.ds(pl.multiple_of(step * TILE, TILE), TILE)
+        ids_col[span] = jnp.broadcast_to(ids[:, span], (8, TILE)).T[:, :1]
+        return carry
+
+    lax.fori_loop(0, row_tiles, split_ids, 0)
+    dkv[...] = jnp.zeros_like(dkv)
+    local_grad(2)
+    stage[0] = join(0)
+    for n, peer in enumerate(peers):
+        links.arrive(grad_ctx.at[peer], swap + n, mate)
+
+    def split_grad(j, carry):
+        grad = grad_ctx[j]
+        grad_t = grad.astype(f32).T
+        for h in range(heads):
+            part = slice(h * HEAD, (h + 1) * HEAD)
+            both[h, j, :TILE] = q[h, j]
+            both[h, j, TILE:] = jnp.concatenate(
+                [jnp.zeros((TILE, HEAD), low), grad[:, part]], axis=1
+            )
+            delta[h, j] = jnp.sum(grad_t[part] * mixed[j, h], axis=0, keepdims=True)
+        return carry
+
+    lax.fori_loop(0, blocks, split_grad, 0)
+    for j in range(blocks):
+        block = 2 * j + lax.rem(j + col, 2)
+        rows = pl.ds(pl.multiple_of(block * TILE, TILE), TILE)
+        query_ids = ids[:, rows]
+        far = 2 * j * TILE
+        spans = ([(0, far)] if far else []) + [(far, min(2 * j + NEAR, row_tiles) * TILE)]
+
+        def one_head(h, carry, j=j, query_ids=query_ids, far=far, spans=spans):
+            total = jnp.zeros((HEAD, TILE), f32)
+            for start, stop in spans:
+                raw = nt(kv[h, start:stop], both[h, j])
+                probs = jnp.exp(raw[:, :TILE] - lse[j, h])
+                if start == far:
+                    probs = jnp.where(ids_col[start:stop] <= query_ids, probs, 0.0)
+                grad_scores = (probs * (raw[:, TILE:] - delta[h, j])).astype(low)
+                dkv[h, start:stop] += nn(
+                    jnp.concatenate([grad_scores, probs.astype(low)], axis=1), both[h, j]
+                )
+                total = total + nn(kt[h, :, start:stop], grad_scores)
+            dq[j, h] = total * HEAD**-0.5
             return carry
 
-        lax.fori_loop(0, 16, add_g, 0)
-        started.append(send_first(i, sums[i]))
+        lax.fori_loop(0, heads, one_head, 0)
+        if j == 0:
+            stage[1] = join(1)
+        if j == 1:
+            stage[2] = join(2)
+        if j == 2:
+            stage[0], stage[1] = send_second(0, stage[0]), send_second(1, stage[1])
+    stage[0], stage[1] = send_line(0, stage[0]), send_line(1, stage[1])
+
+    def gather_q(j, carry):
+        block = 2 * j + lax.rem(j + col, 2)
+        rows = pl.ds(pl.multiple_of(block * TILE, TILE), TILE)
+        other = pl.ds(pl.multiple_of((4 * j + 1 - block) * TILE, TILE), TILE)
+        value = jnp.concatenate([dq[j, h] for h in range(heads)], axis=0)
+        grads_t[2 * wide :, rows] = value.astype(low)
+        grads_t[2 * wide :, other] = jnp.zeros((wide, TILE), low)
+        grads[rows, 2 * wide :] = value.T.astype(low)
+        grads[other, 2 * wide :] = jnp.zeros((TILE, wide), low)
+        return carry + jnp.sum(value.T, axis=0, keepdims=True)
+
+    bias_q = lax.fori_loop(0, blocks, gather_q, jnp.zeros((1, wide), f32))
+
+    def gather_kv(step, carry):
+        rows = pl.ds(pl.multiple_of(step * TILE, TILE), TILE)
+        value = jnp.concatenate([dkv[h, rows] for h in range(heads)], axis=1)
+        grads[rows, : 2 * wide] = value.astype(low)
+        grads_t[: 2 * wide, rows] = value.T.astype(low)
+        return carry + jnp.sum(value, axis=0, keepdims=True)
+
+    bias_kv = lax.fori_loop(0, row_tiles, gather_kv, jnp.zeros((1, 2 * wide), f32))
+
+    slot_x, slot_xl = links.slots(4), links.slots(3)
+    per_row = rows_dev // TILE
+    own_block = 2 * row + mine
+
+    def token_grads(at):
+        def one(step, carry):
+            here = pl.ds(pl.multiple_of(step * TILE, TILE), TILE)
+            rows = pl.ds(pl.multiple_of((at * per_row + step) * TILE, TILE), TILE)
+            value = nn(grads[rows], w_t[...])
+            is_own = (at * per_row + step == own_block).astype(f32)
+            dx[at, here] = (value + late[...] * is_own).astype(low)
+            return carry
+
+        lax.fori_loop(0, per_row, one, 0)
+
+    for n, peer in enumerate(peers):
+        token_grads(peer)
+        links.push(
+            dx.at[peer, :, columns(1 - col, feat)], sum_x.at[peer], slot_x + n, mate
+        )
+    token_grads(row)
+    links.push(dx.at[row, :, columns(1 - col, feat)], sum_x.at[row], slot_x + 3, mate)
+
+    def join_x(at, slot):
+        links.arrive(sum_x.at[at], slot, mate)
+
+        def one(step, carry):
+            here = pl.ds(pl.multiple_of(step * 128, 128), 128)
+            sum_x[at, here] = (
+                sum_x[at, here].astype(f32) + dx[at, here, columns(col, feat)].astype(f32)
+            ).astype(low)
+            return carry
+
+        lax.fori_loop(0, rows_dev // 128, one, 0)
+
+    for n, peer in enumerate(peers):
+        join_x(peer, slot_x + n)
+        links.push(sum_x.at[peer], line_x.at[2 - n], slot_xl + 2 - n, at_row(peer))
+
+    for n in range(2):
+        span = slice(n * CHUNK, (n + 1) * CHUNK)
+        value = nn(grads_t[...], x_all[:, :, span].reshape(length, CHUNK)).T
+        gq[2 * n : 2 * n + 2] = value.astype(low).reshape((2,) + gq.shape[1:])
+    slot_q, slot_ql = links.slots(1), links.slots(4)
+    links.push(gq.at[:, 1 - col], sum_q, slot_q, mate)
+    here = lax.broadcasted_iota(jnp.int32, (8, 2 * feat), 0) == row
+    value = jnp.concatenate([bias_kv, bias_q, jnp.zeros((1, 2 * feat - 3 * wide), f32)], axis=1)
+    vec[8:] = vec_in[8:]
+    vec[:8] = jnp.where(here, value, 0.0)
+    slot_v = links.slots(1)
+    links.push(vec, vec_mate, slot_v, mate)
+    local_grad(3)
+    local_grad(4)
+    links.arrive(sum_q, slot_q, mate)
+
+    def add_q(step, carry):
+        sum_q[step] = (sum_q[step].astype(f32) + gq[step, col].astype(f32)).astype(low)
+        return carry
+
+    lax.fori_loop(0, ROWS, add_q, 0)
+    own_part = all_q.at[side, pl.ds(2 * col, 2)]
+    at_home = home == col
+
+    def keep_own():
+        own_part[...] = sum_q[row]
+
+    pl.when(at_home)(keep_own)
+    links.push(sum_q.at[row], own_part, slot_ql + 2 * side + col, mate, jnp.logical_not(at_home))
+    for peer in peers:
+        links.push(sum_q.at[peer], own_part, slot_ql + 2 * side + col, (dp, peer, home))
+    stage[2] = send_second(2, stage[2])
+    links.arrive(vec_mate, slot_v, mate)
+    vec_mate[...] = vec[...] + vec_mate[...]
+    slot_vl, slot_vd = links.slots(3), links.slots(2)
+    for n, peer in enumerate(peers):
+        links.push(vec_mate, vec_line.at[2 - n], slot_vl + 2 - n, at_row(peer))
+    stage[3] = join(3)
+    stage[4] = join(4)
+    stage[2] = send_line(2, stage[2])
+    join_x(row, slot_x + 3)
+    stage[3] = send_second(3, stage[3])
+    stage[4] = send_second(4, stage[4])
+    stage[3] = send_line(3, stage[3])
+    stage[4] = send_line(4, stage[4])
+
+    def finish_line(i):
+        for n in range(3):
+            links.arrive(lines[i].at[n], stage[i] + n, mate)
+        value = pairs[i][1, row, dp].astype(f32)
+        for n in range(3):
+            value = value + lines[i][n].astype(f32)
+        out_g[i][dp] = value.astype(low)
+        stage[i] = share(i, out_g[i])
+
+    finish_line(0)
+    finish_line(1)
+    for n in range(3):
+        links.arrive(line_x.at[n], slot_xl + n, mate)
+
+    def finish_x(step, carry):
+        rows = pl.ds(pl.multiple_of(step * 128, 128), 128)
+        value = sum_x[row, rows].astype(f32)
+        for n in range(3):
+            value = value + line_x[n, rows].astype(f32)
+        out_x[rows] = value.astype(low)
+        return carry
+
+    lax.fori_loop(0, rows_dev // 128, finish_x, 0)
+    share_on(0, out_g[0], stage[0])
+    share_on(1, out_g[1], stage[1])
+    finish_line(2)
+    finish_line(3)
     for j in range(2):
         for e in range(2):
             here = (row == 2 * col + j) & (col == e)
             links.arrive(
                 all_q.at[j, pl.ds(2 * e, 2)], slot_ql + 2 * j + e, mate, jnp.logical_not(here)
             )
-    started.append(send_first(count, all_q))
-
+    stage[5] = send_first(5)
     for n in range(3):
         links.arrive(vec_line.at[n], slot_vl + n, mate)
-    vec_sum = out_vec[...] + vec_line[0] + vec_line[1] + vec_line[2]
-    vec_mate[...] = vec_sum
-    slot_v1 = links.slots(2)
-    links.push(vec_mate, vec_flat.at[0], slot_v1, at_dp(1))
-
-    totals = list(sums) + [all_q]
-    started = [send_second(i, totals[i], started[i]) for i in range(count + 1)]
-    slot_z = []
-    for i in range(count + 1):
-        links.arrive(second[i], started[i], mate)
-        add_into(totals[i].at[:, dp], second[i])
-        if i < count:
-            base = links.slots(3)
-            for n, peer in enumerate(peers):
-                links.push(
-                    sums[i].at[peer, dp], lines[i].at[2 - n], base + 2 - n, at_row(peer)
-                )
-            slot_z.append(base)
-        else:
-            for j in range(2):
-                out_q[dp, j] = all_q[j, dp]
-            slot_share_q = share(count, out_q)
-
-    links.arrive(vec_flat.at[0], slot_v1, mate)
-    vec_line[0] = vec_mate[...] + vec_flat[0]
-    links.push(vec_line.at[0], vec_flat.at[1], slot_v1 + 1, at_dp(2))
-
-    for n in range(3):
-        links.arrive(line_x.at[n], slot_xl + n, mate)
-
-    def finish_x(step, carry):
-        rows = pl.ds(pl.multiple_of(step * tile, 128), tile)
-        value = sum_x[row, rows].astype(jnp.float32)
-        for n in range(3):
-            value = value + line_x[n, rows].astype(jnp.float32)
-        out_x[rows] = value.astype(out_x.dtype)
-        return carry
-
-    lax.fori_loop(0, 4, finish_x, 0)
-    shares = []
-    for i in range(count):
-        for n in range(3):
-            links.arrive(lines[i].at[n], slot_z[i] + n, mate)
-        value = sums[i][row, dp].astype(jnp.float32)
-        for n in range(3):
-            value = value + lines[i][n].astype(jnp.float32)
-        outs[i][dp] = value.astype(outs[i].dtype)
-        shares.append(share(i, outs[i]))
-    links.arrive(vec_flat.at[1], slot_v1 + 1, mate)
+    vec_sum = vec_mate[...] + vec_line[0] + vec_line[1] + vec_line[2]
+    vec_line[1] = vec_sum
+    links.push(vec_line.at[1], vec_flat.at[0], slot_vd, at_dp(1))
+    finish_line(4)
+    share_on(2, out_g[2], stage[2])
+    share_on(3, out_g[3], stage[3])
+    stage[5] = send_second(5, stage[5])
+    links.arrive(vec_flat.at[0], slot_vd, mate)
+    vec_line[0] = vec_line[1] + vec_flat[0]
+    links.push(vec_line.at[0], vec_flat.at[1], slot_vd + 1, at_dp(2))
+    share_on(4, out_g[4], stage[4])
+    links.arrive(second[5], stage[5], mate)
+    add_into(all_q.at[:, dp], second[5])
+    for j in range(2):
+        out_q[dp, j] = all_q[j, dp]
+    stage[5] = share(5, out_q)
+    share_on(5, out_q, stage[5])
+    links.arrive(vec_flat.at[1], slot_vd + 1, mate)
     vec_total = vec_line[0] + vec_flat[1]
-    for i in range(count):
-        shared(i, outs[i], shares[i])
-    shared(count, out_q, slot_share_q)
+    for i in range(5):
+        shared(i, out_g[i], stage[i])
+    shared(5, out_q, stage[5])
+    links.arrive(halves.at[other_rows], slot_o, mate)
     links.drain()
-    out_vec[...] = vec_total
-
-
-def reduce_all(grads, gq, dx, vec):
-    count = len(grads)
-    low = dx.dtype
-    depth = grads[0].shape[0]
-    part = depth // ROWS // 4
-    widths = [grad.shape[1] // 2 for grad in grads]
-    wide = gq.shape[1]
-    rows, feat = dx.shape[0] // ROWS, dx.shape[1] // 2
-    blocks = lambda lead, width: (lead, 4, part, width)
-    outs = [jax.ShapeDtypeStruct((4, part, width), low) for width in widths] + [
-        jax.ShapeDtypeStruct((4, 2, part, wide), low),
-        jax.ShapeDtypeStruct((rows, feat), low),
-        jax.ShapeDtypeStruct(vec.shape, vec.dtype),
+    vec[...] = vec_total
+
+
+def backward_links(
+    grad_blocks, output, late, stream, grad_pre, branch_two, activ, branch_one, context,
+    q, kv, kt, mixed, lse, ids, x_all, w_heads, vec,
+):
+    low, f32 = q.dtype, jnp.float32
+    heads, length = kv.shape[0], kv.shape[1]
+    wide = heads * HEAD
+    own, features = output.shape
+    hidden = activ.shape[1]
+    part = features // ROWS // 4
+    widths = [hidden // 4] * 4 + [features // 2]
+    rows, feat = 2 * own, features // 2
+    blocks = length // TILE // 2
+    shape = jax.ShapeDtypeStruct
+    outs = [shape((4, part, width), low) for width in widths] + [
+        shape((4, 2, part, 3 * wide), low),
+        shape((rows, feat), low),
+        shape((rows, feat), low),
+        shape(vec.shape, f32),
     ]
-    every = [(ROWS, width) for width in widths] + [(2, wide)]
+    every = [(ROWS, width) for width in widths] + [(2, 3 * wide)]
     return pl.pallas_call(
-        functools.partial(reduce_kernel, count),
+        functools.partial(backward_kernel, heads),
         out_shape=outs,
-        in_specs=[IN_VMEM] * (count + 3),
+        in_specs=[IN_VMEM] * 18,
         out_specs=[IN_VMEM] * len(outs),
-        scratch_shapes=[pltpu.VMEM(blocks(ROWS, width), low) for width in widths]
+        scratch_shapes=[pltpu.VMEM((2, ROWS, 4, part, width), low) for width in widths]
+        + [pltpu.VMEM((ROWS, 4, part, width), low) for width in widths]
         + [pltpu.VMEM((2, lead, part, width), low) for lead, width in every]
         + [pltpu.VMEM((lead, part, width), low) for lead, width in every]
         + [pltpu.VMEM((3, part, width), low) for width in widths]
         + [
-            pltpu.VMEM((ROWS, 2, part, wide), low),
-            pltpu.VMEM((2, 4, part, wide), low),
+            pltpu.VMEM((ROWS, own, wide), low),
+            pltpu.VMEM((heads, blocks, 2 * TILE, 2 * HEAD), low),
+            pltpu.VMEM((heads, blocks, 1, TILE), f32),
+            pltpu.VMEM((blocks, heads, HEAD, TILE), f32),
+            pltpu.VMEM((heads, length, 2 * HEAD), f32),
+            pltpu.VMEM((length, 3 * wide), low),
+            pltpu.VMEM((3 * wide, length), low),
+            pltpu.VMEM((3 * wide, features), low),
+            pltpu.VMEM((3, features, own), low),
+            pltpu.VMEM((length, 1), jnp.int32),
+            pltpu.VMEM((ROWS, rows, features), low),
             pltpu.VMEM((ROWS, rows, feat), low),
             pltpu.VMEM((3, rows, feat), low),
-            pltpu.VMEM(vec.shape, vec.dtype),
-            pltpu.VMEM((3,) + vec.shape, vec.dtype),
-            pltpu.VMEM((2,) + vec.shape, vec.dtype),
-            pltpu.SemaphoreType.DMA((96,)),
-            pltpu.SemaphoreType.DMA((96,)),
+            pltpu.VMEM((ROWS, 2, 2, part, 3 * wide), low),
+            pltpu.VMEM((ROWS, 2, part, 3 * wide), low),
+            pltpu.VMEM((2, 4, part, 3 * wide), low),
+            pltpu.VMEM(vec.shape, f32),
+            pltpu.VMEM((3,) + vec.shape, f32),
+            pltpu.VMEM((2,) + vec.shape, f32),
+            pltpu.SemaphoreType.DMA((128,)),
+            pltpu.SemaphoreType.DMA((128,)),
         ],
-        compiler_params=comm_params(4),
-        name="reduce_all",
+        compiler_params=comm_params(2),
+        name="backward_links",
     )(
-        *[grad.reshape(ROWS, 4, part, 2 * width) for grad, width in zip(grads, widths)],
-        gq.reshape(ROWS, 2, 2, part, wide),
-        dx.reshape(ROWS, rows, 2 * feat),
-        vec,
-    )
-
-
-def attend_back_kernel(
-    heads, grad_ctx, q, k, kt, v, mixed, lse, ids_col, ids_row, grads, dk, dv
+        grad_blocks, output, late, stream, grad_pre, branch_two, activ, branch_one, context,
+        q, kv, kt, mixed, lse, ids.reshape(1, -1), x_all, w_heads, vec,
+    )
+
+
+def put_lanes(target, value):
+    for n in range(target.shape[0]):
+        target[n : n + 1] = value[:, n * 128 : (n + 1) * 128]
+
+
+def finish_kernel(
+    heads, g1a, g1b, g2a, g2b, go, gq, x_in, out_in, vec,
+    out, logits, grad_x, o_q, o_bq, o_k, o_v, o_bv, o_o, o_bo, o_g1, o_s1, o_1, o_b1, o_2, o_b2,
+    o_g2, o_s2, o_p, o_bp, o_c, o_bc,
 ):
-    length = k.shape[1]
-    row_tiles = length // TILE
-    width = heads * HEAD
-    low = q.dtype
-    col = lax.axis_index("col")
-    dk[...] = jnp.zeros_like(dk)
-    dv[...] = jnp.zeros_like(dv)
-    for j in range(row_tiles // 2):
-        block = 2 * j + lax.rem(j + col, 2)
-        rows = pl.ds(pl.multiple_of(block * TILE, TILE), TILE)
-        other = pl.ds(pl.multiple_of((4 * j + 1 - block) * TILE, TILE), TILE)
-        query_ids = ids_row[:, rows]
-        tiles = min(2 * j + NEAR, row_tiles)
-        length_j = tiles * TILE
-        clear = 2 * j * TILE
-        grad_t = grad_ctx[j].astype(jnp.float32).T
-        parts = []
-        for h in range(heads):
-            part = slice(h * HEAD, (h + 1) * HEAD)
-            grad_h = grad_ctx[j, :, part]
-            delta = jnp.sum(grad_t[part] * mixed[j, h], axis=0, keepdims=True)
-            query = q[h, j]
-            dq = jnp.zeros((HEAD, TILE), jnp.float32)
-            spans = ([(0, clear)] if clear else []) + [(clear, length_j)]
-            for low_end, high_end in spans:
-                probs = jnp.exp(nt(k[h, low_end:high_end], query) - lse[j, h])
-                if low_end == clear:
-                    probs = jnp.where(ids_col[low_end:high_end] <= query_ids, probs, 0.0)
-                slope = nt(v[h, low_end:high_end], grad_h) - delta
-                grad_scores = (probs * slope).astype(low)
-                dv[h, low_end:high_end] += nn(probs.astype(low), grad_h)
-                dk[h, low_end:high_end] += nn(grad_scores, query)
-                dq = dq + nn(kt[h, :, low_end:high_end], grad_scores)
-            parts.append(dq * HEAD**-0.5)
-        grads[rows, :width] = jnp.concatenate(parts, axis=0).T.astype(low)
-        grads[other, :width] = jnp.zeros((TILE, width), low)
-
-    def write(step, carry):
-        rows = pl.ds(pl.multiple_of(step * TILE, TILE), TILE)
-        grads[rows, width:] = jnp.concatenate(
-            [dk[h, rows] for h in range(heads)] + [dv[h, rows] for h in range(heads)], axis=1
-        ).astype(low)
-        return carry
-
-    lax.fori_loop(0, row_tiles, write, 0)
-
-
-def attend_back(grad_ctx, q, k, kt, v, mixed, lse, ids, heads):
-    length = k.shape[1]
-    low, f32 = q.dtype, jnp.float32
+    dp, _, col = place()
+    f32 = jnp.float32
+    wide = heads * HEAD
+    classes = logits.shape[1]
+    depth, feat = o_q.shape
+    part = g1a.shape[2]
+    out[...] = out_in[...]
+    grad_x[...] = x_in[...]
+    flat = lambda ref: ref[...].astype(f32).reshape(depth, ref.shape[2])
+    for target, first, second in ((o_1, g1a, g1b), (o_2, g2a, g2b)):
+        target[:, :part] = flat(first)
+        target[:, part:] = flat(second)
+    o_o[...] = flat(go)
+    bias_q, bias_v = [], []
+    for j in range(2):
+        value = gq[:, j].astype(f32).reshape(depth, 3 * wide)
+        o_q[:, j * wide : (j + 1) * wide] = value[:, 2 * wide :]
+        for target, shift in ((o_k, 0), (o_v, HEAD)):
+            target[:, j * wide : (j + 1) * wide] = jnp.concatenate(
+                [value[:, 2 * h * HEAD + shift :][:, :HEAD] for h in range(heads)], axis=1
+            )
+        bias = jnp.where(col == 0, vec[j : j + 1], vec[2 + j : 3 + j])
+        bias_q.append(bias[:, 2 * wide : 3 * wide])
+        bias_v += [bias[:, 2 * h * HEAD + HEAD :][:, :HEAD] for h in range(heads)]
+    put_lanes(o_bq, jnp.concatenate(bias_q, axis=1))
+    put_lanes(o_bv, jnp.concatenate(bias_v, axis=1))
+    own = jnp.where(col == 0, vec[8:16], vec[16:24])
+    for n, target in enumerate((o_bo, o_g1, o_s1, o_b2, o_g2, o_s2)):
+        put_lanes(target, own[n // 2 : n // 2 + 1, (n % 2) * feat : (n % 2 + 1) * feat])
+    put_lanes(o_b1, jnp.concatenate([own[3:4], own[4:5]], axis=1))
+    firsts, seconds = vec[24:32], vec[32:40]
+    first_t, second_t = firsts.T, seconds.T
+    pooler = jnp.zeros(o_p.shape, f32)
+    head = jnp.zeros((o_p.shape[0], 128), f32)
+    bias = jnp.zeros((1, 2 * feat), f32)
+    tails = seconds[4:8, :128]
+    for s in range(4):
+        pooler = pooler + first_t[:, s : s + 1] * firsts[4 + s : 5 + s]
+        bias = bias + firsts[4 + s : 5 + s]
+        head = head + second_t[:, s : s + 1] * tails[s : s + 1]
+    o_p[...] = pooler
+    put_lanes(o_bp, bias)
+    o_c[...] = head[:, classes : 2 * classes]
+    o_bc[...] = jnp.sum(tails, axis=0, keepdims=True)[:, classes : 2 * classes]
+    own_tail = jnp.zeros((1, 128), f32)
+    for s in range(4):
+        own_tail = jnp.where(dp == s, tails[s : s + 1], own_tail)
+    logits[...] = own_tail[:, :classes]
+
+
+def finish(pieces, classes, heads):
+    g1a, g1b, g2a, g2b, go, gq, x_in, out_in, vec = pieces
+    f32 = jnp.float32
+    depth = go.shape[0] * go.shape[1]
+    feat, hidden = go.shape[2], 2 * g1a.shape[2]
+    features = vec.shape[1]
+    shape = jax.ShapeDtypeStruct
+    vector = lambda size: shape((size // 128, 128) if size % 128 == 0 else (1, size), f32)
+    square = shape((depth, feat), f32)
+    outs = [
+        shape(out_in.shape, out_in.dtype), vector(classes), shape(x_in.shape, x_in.dtype),
+        square, vector(feat), square, square, vector(feat), square, vector(feat), vector(feat),
+        vector(feat), shape((depth, hidden), f32), vector(hidden), shape((depth, hidden), f32),
+        vector(feat), vector(feat), vector(feat), shape((features, features), f32),
+        vector(features), shape((features, classes), f32), vector(classes),
+    ]
     return pl.pallas_call(
-        functools.partial(attend_back_kernel, heads),
-        out_shape=jax.ShapeDtypeStruct((length, 3 * heads * HEAD), low),
-        in_specs=[IN_VMEM] * 9,
-        out_specs=IN_VMEM,
-        scratch_shapes=[pltpu.VMEM((heads, length, HEAD), f32)] * 2,
+        functools.partial(finish_kernel, heads),
+        out_shape=outs,
+        in_specs=[IN_VMEM] * len(pieces),
+        out_specs=[IN_VMEM] * len(outs),
         compiler_params=pltpu.CompilerParams(vmem_limit_bytes=VMEM_BYTES),
-        name="attend_back",
-    )(grad_ctx, q, k, kt, v, mixed, lse, ids.reshape(-1, 1), ids.reshape(1, -1))
+        name="finish",
+    )(*pieces)
 
 
 def norm_rows(hidden, gain, shift):
@@ -1196,14 +1507,11 @@
     w_output, b_output, ln1_gain, ln1_bias, w_inner, b_inner, w_outer, b_outer,
     ln2_gain, ln2_bias, w_pooler, b_pooler, w_classes, b_classes,
 ):
-    f32, bf16 = jnp.float32, jnp.bfloat16
-    dp, row, col = place()
-    rows, feat = layer_input.shape
+    f32 = jnp.float32
+    feat = layer_input.shape[1]
     features = 2 * feat
     hidden = b_inner.shape[0]
-    own = rows // 2
     heads = features // HEAD // ROWS
-    wide = heads * HEAD
     vectors = [
         b_query, b_value, b_output, ln1_gain, ln1_bias, b_outer, ln2_gain, ln2_bias, b_inner
     ]
@@ -1215,122 +1523,29 @@
         padded = padded + jnp.pad(vector.astype(f32), (at, full - at - size))
         at += size
     (
-        x_all, cot, vec_all, w_heads, q, k, kt, v, mixed, lse, context, w_o, w_1, w_2,
+        x_all, cot, vec_all, w_heads, q, kv, kt, mixed, lse, context, w_o, w_1, w_2,
     ) = forward_links(
         layer_input, cotangent, padded.reshape(-1, feat), w_query, w_key, w_value, block_ids,
         [w_output.T, w_inner, w_outer.T],
     )
-    x_all = x_all.reshape(ROWS * rows, features)
-    w_heads = w_heads.reshape(features, 3 * wide)
     w_o = w_o.reshape(features, features)
     w_1 = w_1.reshape(features, 2 * hidden)
     w_2 = w_2.reshape(features, 2 * hidden)
-    take = lambda start, number=1: vec_all[:, start : start + number].reshape(1, -1)
-    bias_o, gain_one, shift_one, bias_2, gain_two, shift_two = [take(i) for i in range(2, 8)]
-    bias_1 = take(8, count - 8)
-    context = context.transpose(1, 0, 2).reshape(own, features)
-    start = row * rows + lax.rem(row + col, 2) * own
-    x_own = lax.dynamic_slice_in_dim(x_all, start, own, 0).astype(f32)
-
-    hidden_one = x_own + contract_last(context, w_o) + bias_o
-    stream, normed_one, inv_one = norm_rows(hidden_one, gain_one, shift_one)
-    stream_low = stream.astype(bf16)
-    pre_act = project(stream_low, w_1) + bias_1
-    activ = gelu_exact(pre_act).astype(bf16)
-    hidden_two = stream + contract_last(activ, w_2) + bias_2
-    result, normed_two, inv_two = norm_rows(hidden_two, gain_two, shift_two)
-    output = result.astype(bf16)
-
-    holder = ((row == 0) & (col == 0)).astype(f32)
-    first = output[0:1]
-    pooled = jnp.tanh(project(first, w_pooler) + b_pooler.astype(f32))
-    classes = w_classes.astype(f32)
-    logits_own = jnp.dot(pooled, classes, precision=highest) + b_classes.astype(f32)
-    onehot = (jnp.arange(w_classes.shape[1]) == labels[0]).astype(f32)
-    grad_logits = jax.nn.softmax(logits_own, axis=-1) - onehot[None, :]
-    grad_pre_pool = jnp.dot(grad_logits, classes.T, precision=highest) * (1.0 - pooled * pooled)
-    grad_first = jnp.dot(grad_pre_pool, w_pooler.astype(f32).T, precision=highest)
-    grad_result = cot.astype(f32).at[0].add(grad_first[0] * holder)
-
-    total = lambda values: jnp.sum(values, axis=0)
-    g_ln2_gain, g_ln2_bias = total(grad_result * normed_two), total(grad_result)
-    grad_hidden_two = norm_rows_back(grad_result, normed_two, inv_two, gain_two)
-    g_b_outer = total(grad_hidden_two)
-    branch_two = grad_hidden_two.astype(bf16)
-    g_w2 = contract_first(branch_two, activ)
-    grad_pre = (project(branch_two, w_2) * gelu_slope(pre_act)).astype(bf16)
-    g_b_inner = total(grad_pre.astype(f32))
-    g_w1 = contract_first(stream_low, grad_pre)
-    grad_stream = grad_hidden_two + contract_last(grad_pre, w_1)
-    g_ln1_gain, g_ln1_bias = total(grad_stream * normed_one), total(grad_stream)
-    grad_hidden_one = norm_rows_back(grad_stream, normed_one, inv_one, gain_one)
-    g_b_output = total(grad_hidden_one)
-    branch_one = grad_hidden_one.astype(bf16)
-    g_wo = contract_first(branch_one, context)
-    grad_context = project(branch_one, w_o).astype(bf16)
-    grad_blocks = grad_context.reshape(own, ROWS, wide).transpose(1, 0, 2)
-    grad_ctx, output = swap_blocks(grad_blocks, 3, output)
-
-    grads_low = attend_back(grad_ctx, q, k, kt, v, mixed, lse, block_ids, heads)
-    g_qkv = contract_first(x_all, grads_low).astype(bf16)
-    grad_x = contract_last(grads_low, w_heads)
-    tokens = grad_x.shape[0]
-    grad_x = lax.dynamic_update_slice_in_dim(
-        grad_x, lax.dynamic_slice_in_dim(grad_x, start, own, 0) + grad_hidden_one, start, 0
-    ).astype(bf16)
-    bias_sums = total(grads_low.astype(f32))
-    spread = lambda part: lax.dynamic_update_slice(
-        jnp.zeros((features,), f32), part, (row * wide,)
-    )
-    classes_count = w_classes.shape[1]
-    tail = jnp.pad(
-        jnp.concatenate([logits_own[0], grad_logits[0]]) * holder, (0, 128 - 2 * classes_count)
-    )
-    table = jnp.concatenate(
-        [first[0].astype(f32) * holder, grad_pre_pool[0] * holder, pooled[0] * holder, tail]
-    )
-    sequences = lax.axis_size("dp")
-    table = lax.dynamic_update_slice(
-        jnp.zeros((sequences, table.shape[0]), f32), table[None], (dp, 0)
-    )
-    pieces = [
-        spread(bias_sums[:wide]), spread(bias_sums[2 * wide :]), g_b_output, g_ln1_gain,
-        g_ln1_bias, g_b_outer, g_ln2_gain, g_ln2_bias, g_b_inner, table.reshape(-1),
-    ]
-    packed = jnp.concatenate(pieces)
-    packed = jnp.pad(packed, (0, -packed.shape[0] % 1024)).reshape(-1, 128)
-    s_w1, s_w2, s_wo, s_q, grad_input, sums = reduce_all(
-        [g.astype(bf16) for g in (g_w1, g_w2, g_wo)], g_qkv, grad_x, packed
-    )
-    depth = w_query.shape[0]
-    s_q = s_q.transpose(0, 2, 1, 3).reshape(depth, 2, 3, wide).transpose(2, 0, 1, 3)
-    s_q = s_q.reshape(3, depth, feat).astype(f32)
-    sums = sums.reshape(-1)
-    found, at = [], 0
-    for piece in pieces:
-        found.append(sums[at : at + piece.shape[0]])
-        at += piece.shape[0]
-    own_part = lambda full: lax.dynamic_slice_in_dim(
-        full, col * (full.shape[0] // 2), full.shape[0] // 2
-    )
     (
-        g_b_query, g_b_value, g_b_output, g_ln1_gain, g_ln1_bias, g_b_outer, g_ln2_gain,
-        g_ln2_bias, g_b_inner,
-    ) = [own_part(full) for full in found[:-1]]
-    table = found[-1].reshape(sequences, -1)
-    firsts, pre_pools, pools = [
-        table[:, i * features : (i + 1) * features] for i in range(3)
-    ]
-    ends = table[:, 3 * features :]
-    all_grads = ends[:, classes_count : 2 * classes_count]
-    logits = lax.dynamic_slice_in_dim(ends[:, :classes_count], dp, 1, 0)
-    outer = lambda left, right: jnp.sum(left[:, :, None] * right[:, None, :], axis=0)
-    return (
-        output, logits, grad_input, s_q[0], g_b_query, s_q[1], s_q[2], g_b_value,
-        s_wo.reshape(depth, feat).astype(f32).T, g_b_output, g_ln1_gain, g_ln1_bias,
-        s_w1.reshape(depth, hidden).astype(f32), g_b_inner,
-        s_w2.reshape(depth, hidden).astype(f32).T, g_b_outer, g_ln2_gain, g_ln2_bias,
-        outer(firsts, pre_pools), total(pre_pools), outer(pools, all_grads), total(all_grads),
+        output, late, stream, grad_pre, branch_two, activ, branch_one, context, grad_blocks, packed
+    ) = middle(
+        context, cot, vec_all, labels, b_pooler, w_classes, b_classes, w_pooler, w_o, x_all, w_1, w_2
+    )
+    s_1a, s_2a, s_1b, s_2b, s_wo, s_q, grad_input, output, sums = backward_links(
+        grad_blocks, output, late, stream, grad_pre, branch_two, activ, branch_one, context,
+        q, kv, kt, mixed, lse, block_ids, x_all, w_heads, packed,
+    )
+    outs = finish((s_1a, s_1b, s_2a, s_2b, s_wo, s_q, grad_input, output, sums), w_classes.shape[1], heads)
+    flat = (4, 7, 9, 10, 11, 13, 15, 16, 17, 19, 21)
+    turned = (8, 14)
+    return tuple(
+        out.reshape(-1) if n in flat else out.T if n in turned else out
+        for n, out in enumerate(outs)
     )
 
 

time: 343 us -> 270 us (0.79); the launches traced: 336 us -> 269 us
  matrix products: 44.3 us -> 0 us
  Pallas kernels: 236 us -> 263 us
  local copies, waits for them, and re-layouts: 30.4 us -> 3.62 us
  other arithmetic: 23.4 us -> 0.82 us
    dot_general x15 -> x0, matrix products: 44.3 us -> none  [the longest x4 15.5 us: contract_first(): lax.dot_general(left, right, (((0,), (0,)), ((), ())), preferred_element_...]
    pallas_call x3, Pallas kernels: 141 us -> 171 us  [the longest x1 149 us: backward_links(): pl.pallas_call(functools.partial(backward_kernel, heads), out_shape=outs,...]
    reduce_sum x8 -> x0, other arithmetic: 10.7 us -> none  [the longest x5 6.66 us: fast_body(): total = lambda values: jnp.sum(values, axis=0)]
    slice x11 -> x0, local copies, waits for them, and re-layouts: 6.45 us -> none  [the longest x2 2.34 us: fast_body(): vec_all[:, start:start + number].reshape(1, -1)]
    dynamic_slice x10 -> x0, local copies, waits for them, and re-layouts: 6.39 us -> none  [the longest x9 5.87 us: fast_body(): lax.dynamic_slice_in_dim(full, col * (full.shape[0] // 2), full.shape[0]...]
    convert_element_type x5 -> x0, other arithmetic: 5.15 us -> none  [the longest x1 1.93 us: fast_body(): grad_x = lax.dynamic_update_slice_in_dim(grad_x, lax.dynamic_slice_in_dim...]
    convert_element_type x4 -> x0, local copies, waits for them, and re-layouts: 4.33 us -> none  [the longest x2 2.83 us: fast_body(): s_q = s_q.reshape(3, depth, feat).astype(f32)]
where the time goes in v3:
time: 270 us; the launch traced here: 269 us
  Pallas kernels  263 us (97%)
  local copies, waits for them, and re-layouts  3.62 us (1%)
    pallas_call x1, Pallas kernels, backward_links(): pl.pallas_call(functools.partial(backward_kernel, heads), out_shape=outs,...  149 us
    pallas_call x1, Pallas kernels, forward_links(): pl.pallas_call(functools.partial(forward_kernel, widths, heads), out_shap...  92 us
    pallas_call x1, Pallas kernels, middle(): pl.pallas_call(functools.partial(middle_kernel, heads), out_shape=[narrow...  16 us
    pallas_call x1, Pallas kernels, finish(): pl.pallas_call(functools.partial(finish_kernel, heads), out_shape=outs, i...  6.23 us

profile of v3, /device:TPU:0, one launch (start us, length us, event | category | flops | bytes accessed | tf_op | source)
XLA Modules:
  0.0 269.1 jit_solution(14219028426716550710)
XLA Ops:
  1.3 1.3 reshape.117.b_pooler
  2.6 0.8 convert_add_fusion
  3.4 0.6 reshape.111.vec
  4.0 92.0 %forward_links.1 = (bf16[4,512,768]{2,1,0:T(8,128)(2,1)}, bf16[256,768]{1,0:T(8,128)(2,1)}, f32[2,16,384]{2,1,0:T(8,128)}, bf16[4,4,48,576]{3,2,1,0:T(8,128)(2,1...) custom-call(bf16[512,384]{1,0:T(8,128)(2,1)} %x.19, ...), custom_call_target="tpu_custom_call" | custom-call | tf_op jit(solution)/shard_map/forward_links/pallas_call | solution.py:792
  96.0 16.0 %middle.1 = (bf16[256,768]{1,0:T(8,128)(2,1)}, f32[256,768]{1,0:T(8,128)}, bf16[256,768]{1,0:T(8,128)(2,1)}, bf16[256,3072]{1,0:T(8,128)(2,1)}, bf16[256,768]{1,...) custom-call(bf16[4,256,192]{2,1,0:T(8,128)(2,1)} %get-tuple-element., ...), custom_call_target="tpu_custom_call" | custom-call | tf_op jit(solution)/shard_map/middle/pallas_call | solution.py:955
  112.0 149.1 %backward_links.1 = (bf16[4,48,768]{2,1,0:T(8,128)(2,1)}, bf16[4,48,768]{2,1,0:T(8,128)(2,1)}, bf16[4,48,768]{2,1,0:T(8,128)(2,1)}, bf16[4,48,768]{2,1,0:T(8,128...) custom-call(bf16[4,256,192]{2,1,0:T(8,128)(2,1)} %get-tuple-element., ...), custom_call_target="tpu_custom_call" | custom-call | tf_op jit(solution)/shard_map/backward_links/pallas_call | solution.py:1363
  261.1 6.2 %finish.1 = (bf16[512,384]{1,0:T(8,128)(2,1)}, f32[1,3]{1,0:T(1,128)}, bf16[512,384]{1,0:T(8,128)(2,1)}, f32[192,384]{1,0:T(8,128)}, f32[3,128]{1,0:T(4,128)}, /...) custom-call(bf16[4,48,768]{2,1,0:T(8,128)(2,1)} %get-tuple-element.9, ...), custom_call_target="tpu_custom_call" | custom-call | tf_op jit(solution)/shard_map/finish/pallas_call | solution.py:1480
  267.3 1.7 copy.45

commit v4 on v3

--- a/solution.py
+++ b/solution.py
@@ -487,12 +487,21 @@
     return jnp.dot(left, right, preferred_element_type=jnp.float32)
 
 
-def forward_kernel(widths, heads, x, cot, vec, wq, wk, wv, ids, *refs):
+def forward_kernel(
+    widths, heads, x, cot, vec, wq, wk, wv, ids, labels, w_classes, b_classes, w_pooler, *refs
+):
     count = len(widths)
     shards, refs = refs[:count], refs[count:]
-    x_all, cot_own, vec_all, w_heads, q_out, kv_out, kt_out, mixed_out, lse_out, context = refs[:10]
-    fulls, refs = refs[10 : 10 + count], refs[10 + count :]
-    vt_out, ids_col, packs, low_out, send, recv, local = refs
+    x_all, w_heads, q_out, kv_out, kt_out, mixed_out, lse_out = refs[:7]
+    (
+        output, late, stream_out, grad_pre_out, branch_two_out, activ_out, branch_one_out,
+        context, grad_blocks, packed,
+    ) = refs[7:17]
+    fulls, refs = refs[17 : 17 + count], refs[17 + count :]
+    (
+        cot_own, vec_all, context_in, vt_out, ids_col, packs, low_out, slope, total, send, recv,
+        local,
+    ) = refs
     dp, row, col = place()
     links = Links(send, recv)
     low = x.dtype
@@ -604,17 +613,20 @@
 
     turn = lambda i, slot: (1, 2) if (i + slot) % 2 == 0 else (2, 1)
 
-    def w_relay(step):
-        for i in range(count):
-            relay(step, shards[i].at[dp], lambda k, i=i: w_at(i, k, dp), line_w[i])
+    def w_start(at_left, at_right):
+        for way, ok in ((1, row == at_right), (-1, row == at_left)):
+            slot = 2 if way == 1 else 0
+            for i in range(count):
+                links.push(
+                    shards[i].at[dp], w_at(i, row, dp), line_w[i] + slot, at_row(row + way), ok
+                )
 
     def w_first(step):
         for i in range(count):
             for slot, k, ok in at_step(step):
                 links.arrive(w_at(i, k, dp), line_w[i] + slot, mate, ok)
-        if step < 3:
-            w_relay(step + 1)
-        for i in range(count):
+            if step < 3:
+                relay(step + 1, None, lambda k, i=i: w_at(i, k, dp), line_w[i])
             for slot, k, ok in at_step(step):
                 one, two = turn(i, slot)
                 links.push(w_at(i, k, dp), w_at(i, k, dp), first_w[i] + slot, at_dp(one), ok)
@@ -629,14 +641,22 @@
                         w_at(i, k, q), w_at(i, k, q), second_w[i] + 2 * slot + n, at_dp(two), ok
                     )
 
-    def w_mate(step):
-        for i in range(count):
+    def w_mate(step, items):
+        for i in items:
             for slot, k, ok in at_step(step):
                 one, two = turn(i, slot)
                 links.arrive(w_at(i, k, dp ^ two), second_w[i] + 2 * slot, mate, ok)
                 links.arrive(w_at(i, k, dp ^ 3), second_w[i] + 2 * slot + 1, mate, ok)
                 links.push(row_at(i, k), row_at(i, k), mate_w[i] + 1 + slot, mate, ok)
 
+    def w_ready(i):
+        w_mate(3, (i,))
+        copies[i].wait()
+        links.arrive(row_mate_at(i, row), mate_w[i], mate)
+        for slot in range(3):
+            k = lax.rem(row + slot + 1, ROWS)
+            links.arrive(row_mate_at(i, k), mate_w[i] + 1 + slot, mate)
+
     row_tiles = ROWS * rows_dev // TILE
     per_row = rows_dev // TILE
 
@@ -646,11 +666,13 @@
         return carry
 
     lax.fori_loop(0, row_tiles, split_ids, 0)
+    w_start(3, 0)
     x_step(1)
+    w_start(2, 1)
     q_first()
     x_step(2)
+    w_start(1, 2)
     q_second()
-    w_relay(1)
     for copy in copies:
         copy.start()
     for i in range(count):
@@ -738,117 +760,37 @@
         )
         away = row != j
         slot = lax.rem(row - j + ROWS + 3, ROWS)
-        links.push(low_out.at[j], context.at[row], swap + slot, at_row(j), away)
+        links.push(low_out.at[j], context_in.at[row], swap + slot, at_row(j), away)
 
         @pl.when(jnp.logical_not(away))
         def _(j=j):
-            context[row] = low_out[j]
+            context_in[row] = low_out[j]
 
         if j == 0:
             w_second(1)
         if j == 1:
             w_first(3)
             w_second(2)
-            w_mate(1)
+            w_mate(1, range(count))
         if j == 2:
             w_second(3)
-            w_mate(2)
-    w_mate(3)
+            w_mate(2, range(count))
+
+    f32 = jnp.float32
+    own, features = output.shape
+    hidden = 2 * widths[1]
+    chunk = features
+    w_o, w_1, w_2 = fulls
+    part_of = lambda full, span: full[:, :, :, span].reshape(features, span.stop - span.start)
+    vector = lambda n: jnp.concatenate([vec_all[0, n : n + 1], vec_all[1, n : n + 1]], axis=1)
     links.arrive(cot_own.at[:, columns(1 - col, feat)], mate_cot, mate)
     for slot in range(3):
-        links.arrive(context.at[lax.rem(row + slot + 1, ROWS)], swap + slot, mate)
-    for i in range(count):
-        links.arrive(row_mate_at(i, row), mate_w[i], mate)
-        for slot in range(3):
-            k = lax.rem(row + slot + 1, ROWS)
-            links.arrive(row_mate_at(i, k), mate_w[i] + 1 + slot, mate)
-    for copy in copies:
-        copy.wait()
-    links.drain()
-
-
-def forward_links(x, cot, vec, wq, wk, wv, ids, shards):
-    widths = [shard.shape[1] for shard in shards]
-    rows, feat = x.shape
-    low, f32 = x.dtype, jnp.float32
-    part = shards[0].shape[0] // 4
-    heads = 2 * feat // HEAD // ROWS
-    wide = heads * HEAD
-    length = ROWS * rows
-    blocks = length // TILE // 2
-    shape = jax.ShapeDtypeStruct
-    shapes = [
-        shape((ROWS, rows, 2 * feat), low),
-        shape((rows // 2, 2 * feat), low),
-        shape((2,) + vec.shape, vec.dtype),
-        shape((ROWS, 4, part, 3 * wide), low),
-        shape((heads, blocks, TILE, 2 * HEAD), low),
-        shape((heads, length, 2 * HEAD), low),
-        shape((heads, HEAD, length), low),
-        shape((blocks, heads, HEAD, TILE), f32),
-        shape((blocks, heads, 1, TILE), f32),
-        shape((ROWS, rows // 2, wide), low),
-    ] + [shape((ROWS, 4, part, 2 * width), low) for width in widths]
-    return pl.pallas_call(
-        functools.partial(forward_kernel, widths, heads),
-        out_shape=shapes,
-        in_specs=[IN_VMEM] * (7 + len(shards)),
-        out_specs=[IN_VMEM] * 10 + [IN_PLACE] * len(shards),
-        scratch_shapes=[
-            pltpu.VMEM((heads, HEAD, length), low),
-            pltpu.VMEM((length, 1), jnp.int32),
-            pltpu.VMEM((2, 4, part, 3 * wide), low),
-            pltpu.VMEM((blocks, TILE, wide), low),
-            pltpu.SemaphoreType.DMA((160,)),
-            pltpu.SemaphoreType.DMA((96,)),
-            pltpu.SemaphoreType.DMA((4,)),
-        ],
-        compiler_params=comm_params(1),
-        name="forward_links",
-    )(
-        x, cot, vec, wq, wk, wv, ids.reshape(1, -1),
-        *[shard.reshape(4, part, -1) for shard in shards],
-    )
-
-
-def add_into(total, *others):
-    def one(step, carry):
-        value = total[step].astype(jnp.float32)
-        for other in others:
-            value = value + other[step].astype(jnp.float32)
-        total[step] = value.astype(total.dtype)
-        return carry
-
-    lax.fori_loop(0, total.shape[0], one, 0)
-
-
-def middle_kernel(
-    heads, context_in, cot, vec_all, labels, b_pooler, w_classes, b_classes, w_pooler,
-    w_o, x_all, w_1_far, w_2_far,
-    output, late, stream_out, grad_pre_out, branch_two_out, activ_out, branch_one_out, context,
-    grad_blocks, packed, x_own, w_1, w_2, slope, total, sems,
-):
-    f32, low = jnp.float32, output.dtype
-    dp, row, col = place()
-    own, features = output.shape
-    wide = features // ROWS
-    hidden = w_1.shape[1]
-    chunk = features
-    mine = lax.rem(row + col, 2)
-    copies = [
-        pltpu.make_async_copy(
-            x_all.at[row, pl.ds(pl.multiple_of(mine * own, 128), own)], x_own, sems.at[0]
-        ),
-        pltpu.make_async_copy(w_1_far, w_1, sems.at[1]),
-        pltpu.make_async_copy(w_2_far, w_2, sems.at[2]),
-    ]
-    for copy in copies:
-        copy.start()
-    vector = lambda n: jnp.concatenate([vec_all[0, n : n + 1], vec_all[1, n : n + 1]], axis=1)
+        links.arrive(context_in.at[lax.rem(row + slot + 1, ROWS)], swap + slot, mate)
     context[...] = jnp.concatenate([context_in[r] for r in range(ROWS)], axis=1)
-    value = nt(context[...], w_o[...])
-    copies[0].wait()
-    hidden_one = x_own[...].astype(f32) + value + vector(2)
+    w_ready(0)
+    value = nt(context[...], w_o[...].reshape(features, features))
+    own_rows = pl.ds(pl.multiple_of(mine * own, 128), own)
+    hidden_one = x_all[row, own_rows].astype(f32) + value + vector(2)
     gain_one, gain_two = vector(3), vector(6)
     stream, normed_one, inv_one = norm_rows(hidden_one, gain_one, vector(4))
     late[...] = stream
@@ -861,22 +803,24 @@
         for c in range(2)
         for n in range(hidden // chunk // 2)
     ]
-    copies[1].wait()
-    copies[2].wait()
+    w_ready(1)
     for n in range(hidden // chunk):
         span = slice(n * chunk, (n + 1) * chunk)
-        pre_act = nn(stream_out[...], w_1[:, span]) + bias_1[n]
+        pre_act = nn(stream_out[...], part_of(w_1, span)) + bias_1[n]
         half = 0.5 * (1.0 + lax.erf(pre_act * root_half))
         slope[:, span] = half + pre_act * inv_root_tau * jnp.exp(-0.5 * pre_act * pre_act)
         activ_out[:, span] = (pre_act * half).astype(low)
-        total[...] += nt(activ_out[:, span], w_2[:, span])
+    w_ready(2)
+    for n in range(hidden // chunk):
+        span = slice(n * chunk, (n + 1) * chunk)
+        total[...] += nt(activ_out[:, span], part_of(w_2, span))
     hidden_two = late[...] + total[...] + vector(5)
     result, normed_two, inv_two = norm_rows(hidden_two, gain_two, vector(7))
     output[...] = result.astype(low)
 
     classes = b_classes.shape[1]
     first = output[:8]
-    pooled = jnp.tanh(nn(first, w_pooler[...])[:1] + b_pooler[...].astype(f32))
+    pooled = jnp.tanh(nn(first, w_pooler[...])[:1] + jnp.concatenate([vec_all[0, 12:13], vec_all[0, 13:14]], axis=1))
     lane = lax.broadcasted_iota(jnp.int32, (1, 128), 1)
     logits = jnp.full((1, 128), masked_score, f32)
     rows = [w_classes[n : n + 1].astype(f32) for n in range(classes)]
@@ -900,7 +844,7 @@
     grad_first = jnp.sum(nt(split, w_pooler[...]), axis=0, keepdims=True)
     holder = ((row == 0) & (col == 0)).astype(f32)
     top = (lax.broadcasted_iota(jnp.int32, (own, 1), 0) == 0).astype(f32) * holder
-    grad_result = cot[...].astype(f32) + top * grad_first
+    grad_result = cot_own[...].astype(f32) + top * grad_first
 
     tokens = lambda values: jnp.sum(values, axis=0, keepdims=True)
     g_gain_two, g_shift_two = tokens(grad_result * normed_two), tokens(grad_result)
@@ -912,20 +856,19 @@
     g_bias_one = []
     for n in range(hidden // chunk):
         span = slice(n * chunk, (n + 1) * chunk)
-        grad_pre = (nn(branch_two_out[...], w_2[:, span]) * slope[:, span]).astype(low)
+        grad_pre = (nn(branch_two_out[...], part_of(w_2, span)) * slope[:, span]).astype(low)
         grad_pre_out[:, span] = grad_pre
         g_bias_one.append(tokens(grad_pre.astype(f32)))
-        total[...] += nt(grad_pre_out[:, span], w_1[:, span])
+        total[...] += nt(grad_pre_out[:, span], part_of(w_1, span))
     grad_stream = late[...] + total[...]
     g_gain_one, g_shift_one = tokens(grad_stream * normed_one), tokens(grad_stream)
     grad_one = norm_rows_back(grad_stream, normed_one, inv_one, gain_one)
     late[...] = grad_one
     branch_one_out[...] = grad_one.astype(low)
-    grad_context = nn(branch_one_out[...], w_o[...]).astype(low)
+    grad_context = nn(branch_one_out[...], w_o[...].reshape(features, features)).astype(low)
     for r in range(ROWS):
         grad_blocks[r] = grad_context[:, r * wide : (r + 1) * wide]
 
-    feat = features // 2
     packed[...] = jnp.zeros_like(packed)
     vectors = [tokens(grad_one), g_gain_one, g_shift_one, g_bias_two, g_gain_two, g_shift_two]
     for n, value in enumerate(vectors):
@@ -939,45 +882,138 @@
     shifted = pltpu.roll(jnp.where(lane < classes, grad_logits, 0.0), classes, 1)
     tail = jnp.concatenate([jnp.where(lane < classes, logits, shifted), spare], axis=1)
     for n, value in enumerate((first[:1].astype(f32), grad_pool, pooled, tail)):
-        here = lax.broadcasted_iota(jnp.int32, (4, features), 0) == dp
-        packed[24 + 4 * n : 28 + 4 * n] = jnp.where(here, value * holder, 0.0)
-
-
-def middle(
-    context, cot, vec_all, labels, b_pooler, w_classes, b_classes, w_pooler, w_o, x_all, w_1, w_2
-):
-    low, f32 = cot.dtype, jnp.float32
-    own, features = cot.shape
-    hidden = w_1.shape[1]
+        packed[24 + n : 25 + n] = value * holder
+    links.drain()
+
+
+def forward_links(x, cot, vec, wq, wk, wv, ids, labels, w_classes, b_classes, w_pooler, shards):
+    widths = [shard.shape[1] for shard in shards]
+    rows, feat = x.shape
+    low, f32 = x.dtype, jnp.float32
+    part = shards[0].shape[0] // 4
+    features, hidden = 2 * feat, 2 * widths[1]
     heads = features // HEAD // ROWS
+    wide = heads * HEAD
+    length, own = ROWS * rows, rows // 2
+    blocks = length // TILE // 2
     shape = jax.ShapeDtypeStruct
     narrow, broad = shape((own, features), low), shape((own, hidden), low)
+    shapes = [
+        shape((ROWS, rows, features), low),
+        shape((ROWS, 4, part, 3 * wide), low),
+        shape((heads, blocks, TILE, 2 * HEAD), low),
+        shape((heads, length, 2 * HEAD), low),
+        shape((heads, HEAD, length), low),
+        shape((blocks, heads, HEAD, TILE), f32),
+        shape((blocks, heads, 1, TILE), f32),
+        narrow, shape((own, features), f32), narrow, broad, narrow, broad, narrow, narrow,
+        shape((ROWS, own, wide), low), shape((32, features), f32),
+    ]
     return pl.pallas_call(
-        functools.partial(middle_kernel, heads),
-        out_shape=[
-            narrow, shape((own, features), f32), narrow, broad, narrow, broad, narrow, narrow,
-            shape((ROWS, own, features // ROWS), low), shape((40, features), f32),
-        ],
-        in_specs=[IN_VMEM] * 3 + [pl.BlockSpec(memory_space=pltpu.SMEM)] + [IN_VMEM] * 5
-        + [IN_PLACE] * 3,
-        out_specs=[IN_VMEM] * 10,
-        scratch_shapes=[
+        functools.partial(forward_kernel, widths, heads),
+        out_shape=shapes,
+        in_specs=[IN_VMEM] * 7 + [pl.BlockSpec(memory_space=pltpu.SMEM)]
+        + [IN_VMEM] * (3 + len(shards)),
+        out_specs=[IN_VMEM] * len(shapes),
+        scratch_shapes=[pltpu.VMEM((ROWS, 4, part, 2 * width), low) for width in widths]
+        + [
             pltpu.VMEM((own, features), low),
-            pltpu.VMEM((features, hidden), low),
-            pltpu.VMEM((features, hidden), low),
+            pltpu.VMEM((2,) + vec.shape, f32),
+            pltpu.VMEM((ROWS, own, wide), low),
+            pltpu.VMEM((heads, HEAD, length), low),
+            pltpu.VMEM((length, 1), jnp.int32),
+            pltpu.VMEM((2, 4, part, 3 * wide), low),
+            pltpu.VMEM((blocks, TILE, wide), low),
             pltpu.VMEM((own, hidden), f32),
             pltpu.VMEM((own, features), f32),
-            pltpu.SemaphoreType.DMA((3,)),
+            pltpu.SemaphoreType.DMA((160,)),
+            pltpu.SemaphoreType.DMA((96,)),
+            pltpu.SemaphoreType.DMA((4,)),
         ],
-        compiler_params=pltpu.CompilerParams(vmem_limit_bytes=VMEM_BYTES),
-        name="middle",
+        compiler_params=comm_params(1),
+        name="forward_links",
     )(
-        context, cot, vec_all, labels.reshape(1, 1), b_pooler.reshape(1, -1), w_classes.T,
-        b_classes.reshape(1, -1), w_pooler, w_o, x_all, w_1, w_2,
-    )
+        x, cot, vec, wq, wk, wv, ids.reshape(1, -1), labels.reshape(1, 1), w_classes.T,
+        b_classes.reshape(1, -1), w_pooler, *[shard.reshape(4, part, -1) for shard in shards],
+    )
+
+
+def add_into(total, *others):
+    def one(step, carry):
+        value = total[step].astype(jnp.float32)
+        for other in others:
+            value = value + other[step].astype(jnp.float32)
+        total[step] = value.astype(total.dtype)
+        return carry
+
+    lax.fori_loop(0, total.shape[0], one, 0)
 
 
 CHUNK = 384
+PLAN = (
+    "g0",
+    "g1",
+    "r0",
+    "c0",
+    "g2",
+    "g3",
+    "c1",
+    "g4",
+    "d0",
+    "a0",
+    "s0",
+    "s1",
+    "c2",
+    "a1",
+    "c3",
+    "a2",
+    "l1",
+    "l0",
+    "c4",
+    "a3",
+    "h1",
+    "h0",
+    "w0",
+    "t0",
+    "s2",
+    "t1",
+    "t2",
+    "x0",
+    "s3",
+    "q0",
+    "x1",
+    "s4",
+    "t3",
+    "v0",
+    "x2",
+    "l2",
+    "l3",
+    "l4",
+    "v1",
+    "f0",
+    "f1",
+    "h2",
+    "q1",
+    "h3",
+    "h4",
+    "k0",
+    "v2",
+    "n0",
+    "n1",
+    "s5",
+    "v3",
+    "f2",
+    "f3",
+    "f4",
+    "x3",
+    "q2",
+    "n2",
+    "n3",
+    "n4",
+    "n5",
+    "k1",
+    "v4",
+)
 
 
 def backward_kernel(
@@ -993,7 +1029,7 @@
     lines, refs = refs[:5], refs[5:]
     (
         grad_ctx, both, delta, dq, dkv, grads, grads_t, w_t, turned, ids_col, dx, sum_x,
-        line_x, gq, sum_q, all_q, vec_mate, vec_line, vec_flat, send, recv,
+        line_x, gq, sum_q, all_q, vec_own, vec_mate, vec_line, vec_flat, vec_table, send, recv,
     ) = refs
     dp, row, col = place()
     links = Links(send, recv)
@@ -1071,25 +1107,32 @@
             return carry
 
         lax.fori_loop(0, 16, one, 0)
-        return send_first(i)
-
-    def send_second(i, base):
+        stage[i] = send_first(i)
+
+    def send_second(i):
         one, two = turns[i]
+        base = stage[i]
         links.arrive(first[i].at[1], base + 1, mate)
         add_into(totals[i].at[:, dp ^ two], first[i].at[1])
         slot = links.slots(1)
         links.push(totals[i].at[:, dp ^ two], second[i], slot, at_dp(two))
-        links.arrive(first[i].at[0], base, mate)
-        add_into(totals[i].at[:, dp], first[i].at[0])
-        return slot
-
-    def send_line(i, slot):
-        links.arrive(second[i], slot, mate)
-        add_into(totals[i].at[:, dp], second[i])
+        stage[i] = (base, slot)
+
+    def send_line(i):
+        links.arrive(first[i].at[0], stage[i][0], mate)
+        links.arrive(second[i], stage[i][1], mate)
+        add_into(totals[i].at[:, dp], first[i].at[0], second[i])
         base = links.slots(3)
-        for n, peer in enumerate(peers):
-            links.push(totals[i].at[peer, dp], lines[i].at[2 - n], base + 2 - n, at_row(peer))
-        return base
+        links.push(totals[i].at[row ^ 3, dp], lines[i].at[1], base + 1, at_row(row ^ 1))
+        links.push(totals[i].at[row ^ 1, dp], lines[i].at[0], base, at_row(row ^ 1))
+        stage[i] = base
+
+    def halve_line(i):
+        links.arrive(lines[i].at[1], stage[i] + 1, mate)
+        pairs[i][1, row ^ 2, dp] = (
+            pairs[i][1, row ^ 2, dp].astype(f32) + lines[i][1].astype(f32)
+        ).astype(low)
+        links.push(totals[i].at[row ^ 2, dp], lines[i].at[2], stage[i] + 2, at_row(row ^ 2))
 
     def share(i, out):
         one, two = turns[i]
@@ -1109,21 +1152,20 @@
         links.arrive(out.at[dp ^ 3], base + 2, mate)
 
     stage = [None] * 6
-    local_grad(0)
-    local_grad(1)
-    w_t[...] = w_heads[...].reshape(2 * feat, 3 * wide).astype(f32).T.astype(low)
+    slot_x, slot_xl = links.slots(4), links.slots(3)
+    slot_q, slot_ql = links.slots(1), links.slots(4)
+    slot_v, slot_vl, slot_vd = links.slots(1), links.slots(3), links.slots(5)
+    order = (row ^ 3, row ^ 1, row ^ 2, row)
+    per_row = rows_dev // TILE
+    own_block = 2 * row + mine
+    own_part = all_q.at[side, pl.ds(2 * col, 2)]
+    at_home = home == col
+    sums = {}
 
     def split_ids(step, carry):
         span = pl.ds(pl.multiple_of(step * TILE, TILE), TILE)
         ids_col[span] = jnp.broadcast_to(ids[:, span], (8, TILE)).T[:, :1]
         return carry
-
-    lax.fori_loop(0, row_tiles, split_ids, 0)
-    dkv[...] = jnp.zeros_like(dkv)
-    local_grad(2)
-    stage[0] = join(0)
-    for n, peer in enumerate(peers):
-        links.arrive(grad_ctx.at[peer], swap + n, mate)
 
     def split_grad(j, carry):
         grad = grad_ctx[j]
@@ -1137,8 +1179,17 @@
             delta[h, j] = jnp.sum(grad_t[part] * mixed[j, h], axis=0, keepdims=True)
         return carry
 
-    lax.fori_loop(0, blocks, split_grad, 0)
-    for j in range(blocks):
+    def ready():
+        w_t[...] = w_heads[...].reshape(2 * feat, 3 * wide).astype(f32).T.astype(low)
+        lax.fori_loop(0, row_tiles, split_ids, 0)
+        dkv[...] = jnp.zeros_like(dkv)
+
+    def take_context():
+        for n, peer in enumerate(peers):
+            links.arrive(grad_ctx.at[peer], swap + n, mate)
+        lax.fori_loop(0, blocks, split_grad, 0)
+
+    def attend_back(j):
         block = 2 * j + lax.rem(j + col, 2)
         rows = pl.ds(pl.multiple_of(block * TILE, TILE), TILE)
         query_ids = ids[:, rows]
@@ -1161,13 +1212,6 @@
             return carry
 
         lax.fori_loop(0, heads, one_head, 0)
-        if j == 0:
-            stage[1] = join(1)
-        if j == 1:
-            stage[2] = join(2)
-        if j == 2:
-            stage[0], stage[1] = send_second(0, stage[0]), send_second(1, stage[1])
-    stage[0], stage[1] = send_line(0, stage[0]), send_line(1, stage[1])
 
     def gather_q(j, carry):
         block = 2 * j + lax.rem(j + col, 2)
@@ -1180,8 +1224,6 @@
         grads[other, 2 * wide :] = jnp.zeros((TILE, wide), low)
         return carry + jnp.sum(value.T, axis=0, keepdims=True)
 
-    bias_q = lax.fori_loop(0, blocks, gather_q, jnp.zeros((1, wide), f32))
-
     def gather_kv(step, carry):
         rows = pl.ds(pl.multiple_of(step * TILE, TILE), TILE)
         value = jnp.concatenate([dkv[h, rows] for h in range(heads)], axis=1)
@@ -1189,11 +1231,14 @@
         grads_t[: 2 * wide, rows] = value.T.astype(low)
         return carry + jnp.sum(value, axis=0, keepdims=True)
 
-    bias_kv = lax.fori_loop(0, row_tiles, gather_kv, jnp.zeros((1, 2 * wide), f32))
-
-    slot_x, slot_xl = links.slots(4), links.slots(3)
-    per_row = rows_dev // TILE
-    own_block = 2 * row + mine
+    def weight_grads():
+        sums["q"] = lax.fori_loop(0, blocks, gather_q, jnp.zeros((1, wide), f32))
+        sums["kv"] = lax.fori_loop(0, row_tiles, gather_kv, jnp.zeros((1, 2 * wide), f32))
+        for n in range(2):
+            span = slice(n * CHUNK, (n + 1) * CHUNK)
+            value = nn(grads_t[...], x_all[:, :, span].reshape(length, CHUNK)).T
+            gq[2 * n : 2 * n + 2] = value.astype(low).reshape((2,) + gq.shape[1:])
+        links.push(gq.at[:, 1 - col], sum_q, slot_q, mate)
 
     def token_grads(at):
         def one(step, carry):
@@ -1206,13 +1251,11 @@
 
         lax.fori_loop(0, per_row, one, 0)
 
-    for n, peer in enumerate(peers):
-        token_grads(peer)
+    def send_tokens(n):
+        token_grads(order[n])
         links.push(
-            dx.at[peer, :, columns(1 - col, feat)], sum_x.at[peer], slot_x + n, mate
+            dx.at[order[n], :, columns(1 - col, feat)], sum_x.at[order[n]], slot_x + n, mate
         )
-    token_grads(row)
-    links.push(dx.at[row, :, columns(1 - col, feat)], sum_x.at[row], slot_x + 3, mate)
 
     def join_x(at, slot):
         links.arrive(sum_x.at[at], slot, mate)
@@ -1226,117 +1269,139 @@
 
         lax.fori_loop(0, rows_dev // 128, one, 0)
 
-    for n, peer in enumerate(peers):
-        join_x(peer, slot_x + n)
-        links.push(sum_x.at[peer], line_x.at[2 - n], slot_xl + 2 - n, at_row(peer))
-
-    for n in range(2):
-        span = slice(n * CHUNK, (n + 1) * CHUNK)
-        value = nn(grads_t[...], x_all[:, :, span].reshape(length, CHUNK)).T
-        gq[2 * n : 2 * n + 2] = value.astype(low).reshape((2,) + gq.shape[1:])
-    slot_q, slot_ql = links.slots(1), links.slots(4)
-    links.push(gq.at[:, 1 - col], sum_q, slot_q, mate)
-    here = lax.broadcasted_iota(jnp.int32, (8, 2 * feat), 0) == row
-    value = jnp.concatenate([bias_kv, bias_q, jnp.zeros((1, 2 * feat - 3 * wide), f32)], axis=1)
-    vec[8:] = vec_in[8:]
-    vec[:8] = jnp.where(here, value, 0.0)
-    slot_v = links.slots(1)
-    links.push(vec, vec_mate, slot_v, mate)
-    local_grad(3)
-    local_grad(4)
-    links.arrive(sum_q, slot_q, mate)
+    def line_tokens(n):
+        join_x(order[n], slot_x + n)
+        if n < 2:
+            links.push(sum_x.at[order[n]], line_x.at[1 - n], slot_xl + 1 - n, at_row(row ^ 1))
+
+    def halve_x(step, carry):
+        rows = pl.ds(pl.multiple_of(step * 128, 128), 128)
+        sum_x[row ^ 2, rows] = (
+            sum_x[row ^ 2, rows].astype(f32) + line_x[1, rows].astype(f32)
+        ).astype(low)
+        return carry
+
+    def halve_tokens():
+        links.arrive(line_x.at[1], slot_xl + 1, mate)
+        lax.fori_loop(0, rows_dev // 128, halve_x, 0)
+        links.push(sum_x.at[row ^ 2], line_x.at[2], slot_xl + 2, at_row(row ^ 2))
+
+    def finish_x(step, carry):
+        rows = pl.ds(pl.multiple_of(step * 128, 128), 128)
+        value = sum_x[row, rows].astype(f32)
+        for n in (0, 2):
+            value = value + line_x[n, rows].astype(f32)
+        out_x[rows] = value.astype(low)
+        return carry
+
+    def finish_tokens():
+        for n in (0, 2):
+            links.arrive(line_x.at[n], slot_xl + n, mate)
+        lax.fori_loop(0, rows_dev // 128, finish_x, 0)
 
     def add_q(step, carry):
         sum_q[step] = (sum_q[step].astype(f32) + gq[step, col].astype(f32)).astype(low)
         return carry
 
-    lax.fori_loop(0, ROWS, add_q, 0)
-    own_part = all_q.at[side, pl.ds(2 * col, 2)]
-    at_home = home == col
-
     def keep_own():
         own_part[...] = sum_q[row]
 
-    pl.when(at_home)(keep_own)
-    links.push(sum_q.at[row], own_part, slot_ql + 2 * side + col, mate, jnp.logical_not(at_home))
-    for peer in peers:
-        links.push(sum_q.at[peer], own_part, slot_ql + 2 * side + col, (dp, peer, home))
-    stage[2] = send_second(2, stage[2])
-    links.arrive(vec_mate, slot_v, mate)
-    vec_mate[...] = vec[...] + vec_mate[...]
-    slot_vl, slot_vd = links.slots(3), links.slots(2)
-    for n, peer in enumerate(peers):
-        links.push(vec_mate, vec_line.at[2 - n], slot_vl + 2 - n, at_row(peer))
-    stage[3] = join(3)
-    stage[4] = join(4)
-    stage[2] = send_line(2, stage[2])
-    join_x(row, slot_x + 3)
-    stage[3] = send_second(3, stage[3])
-    stage[4] = send_second(4, stage[4])
-    stage[3] = send_line(3, stage[3])
-    stage[4] = send_line(4, stage[4])
+    def line_q():
+        links.arrive(sum_q, slot_q, mate)
+        lax.fori_loop(0, ROWS, add_q, 0)
+        pl.when(at_home)(keep_own)
+        slot = slot_ql + 2 * side + col
+        links.push(sum_q.at[row], own_part, slot, mate, jnp.logical_not(at_home))
+        for peer in peers:
+            links.push(sum_q.at[peer], own_part, slot, (dp, peer, home))
+
+    def first_q():
+        for j in range(2):
+            for e in range(2):
+                here = (row == 2 * col + j) & (col == e)
+                links.arrive(
+                    all_q.at[j, pl.ds(2 * e, 2)], slot_ql + 2 * j + e, mate, jnp.logical_not(here)
+                )
+        stage[5] = send_first(5)
+
+    def finish_q():
+        links.arrive(first[5].at[0], stage[5][0], mate)
+        links.arrive(second[5], stage[5][1], mate)
+        add_into(all_q.at[:, dp], first[5].at[0], second[5])
+        for j in range(2):
+            out_q[dp, j] = all_q[j, dp]
+        stage[5] = share(5, out_q)
 
     def finish_line(i):
-        for n in range(3):
+        for n in (0, 2):
             links.arrive(lines[i].at[n], stage[i] + n, mate)
         value = pairs[i][1, row, dp].astype(f32)
-        for n in range(3):
+        for n in (0, 2):
             value = value + lines[i][n].astype(f32)
         out_g[i][dp] = value.astype(low)
         stage[i] = share(i, out_g[i])
 
-    finish_line(0)
-    finish_line(1)
-    for n in range(3):
-        links.arrive(line_x.at[n], slot_xl + n, mate)
-
-    def finish_x(step, carry):
-        rows = pl.ds(pl.multiple_of(step * 128, 128), 128)
-        value = sum_x[row, rows].astype(f32)
+    def sums_mate():
+        value = jnp.concatenate(
+            [sums["kv"], sums["q"], jnp.zeros((1, 2 * feat - 3 * wide), f32)], axis=1
+        )
+        here = lax.broadcasted_iota(jnp.int32, (8, 2 * feat), 0) == 5 + side
+        for c in range(2):
+            part = vec_in[8 + 8 * c : 16 + 8 * c] + jnp.where(here & (home == c), value, 0.0)
+            vec_own[jnp.where(col == c, 0, 1), :8] = part
+        vec_own[0, 8:] = vec_in[24:]
+        vec_own[1, 8:] = vec_in[24:]
+        links.push(vec_own.at[1], vec_mate, slot_v, mate)
+
+    def sums_line():
+        links.arrive(vec_mate, slot_v, mate)
+        vec_mate[...] = vec_own[0] + vec_mate[...]
+        for n, peer in enumerate(peers):
+            links.push(vec_mate, vec_line.at[2 - n], slot_vl + 2 - n, at_row(peer))
+
+    def sums_first():
         for n in range(3):
-            value = value + line_x[n, rows].astype(f32)
-        out_x[rows] = value.astype(low)
-        return carry
-
-    lax.fori_loop(0, rows_dev // 128, finish_x, 0)
-    share_on(0, out_g[0], stage[0])
-    share_on(1, out_g[1], stage[1])
-    finish_line(2)
-    finish_line(3)
-    for j in range(2):
-        for e in range(2):
-            here = (row == 2 * col + j) & (col == e)
-            links.arrive(
-                all_q.at[j, pl.ds(2 * e, 2)], slot_ql + 2 * j + e, mate, jnp.logical_not(here)
-            )
-    stage[5] = send_first(5)
-    for n in range(3):
-        links.arrive(vec_line.at[n], slot_vl + n, mate)
-    vec_sum = vec_mate[...] + vec_line[0] + vec_line[1] + vec_line[2]
-    vec_line[1] = vec_sum
-    links.push(vec_line.at[1], vec_flat.at[0], slot_vd, at_dp(1))
-    finish_line(4)
-    share_on(2, out_g[2], stage[2])
-    share_on(3, out_g[3], stage[3])
-    stage[5] = send_second(5, stage[5])
-    links.arrive(vec_flat.at[0], slot_vd, mate)
-    vec_line[0] = vec_line[1] + vec_flat[0]
-    links.push(vec_line.at[0], vec_flat.at[1], slot_vd + 1, at_dp(2))
-    share_on(4, out_g[4], stage[4])
-    links.arrive(second[5], stage[5], mate)
-    add_into(all_q.at[:, dp], second[5])
-    for j in range(2):
-        out_q[dp, j] = all_q[j, dp]
-    stage[5] = share(5, out_q)
-    share_on(5, out_q, stage[5])
-    links.arrive(vec_flat.at[1], slot_vd + 1, mate)
-    vec_total = vec_line[0] + vec_flat[1]
-    for i in range(5):
-        shared(i, out_g[i], stage[i])
-    shared(5, out_q, stage[5])
+            links.arrive(vec_line.at[n], slot_vl + n, mate)
+        vec_sum = vec_mate[...] + vec_line[0] + vec_line[1] + vec_line[2]
+        vec_flat[2] = vec_sum[:8]
+        vec_table[dp] = vec_sum[8:]
+        links.push(vec_flat.at[2], vec_flat.at[0], slot_vd, at_dp(1))
+        links.push(vec_table.at[dp], vec_table.at[dp], slot_vd + 1, at_dp(1))
+        links.push(vec_table.at[dp], vec_table.at[dp], slot_vd + 2, at_dp(2))
+
+    def sums_second():
+        links.arrive(vec_flat.at[0], slot_vd, mate)
+        vec_flat[3] = vec_flat[2] + vec_flat[0]
+        links.push(vec_flat.at[3], vec_flat.at[1], slot_vd + 3, at_dp(2))
+        links.arrive(vec_table.at[dp ^ 1], slot_vd + 1, mate)
+        links.push(vec_table.at[dp ^ 1], vec_table.at[dp ^ 1], slot_vd + 4, at_dp(2))
+
+    def sums_last():
+        links.arrive(vec_flat.at[1], slot_vd + 3, mate)
+        links.arrive(vec_table.at[dp ^ 2], slot_vd + 2, mate)
+        links.arrive(vec_table.at[dp ^ 3], slot_vd + 4, mate)
+        vec[:8] = vec_flat[3] + vec_flat[1]
+        for n in range(4):
+            vec[8 + 8 * n : 16 + 8 * n] = vec_table[n]
+
+    def out_of(i):
+        return out_q if i == 5 else out_g[i]
+
+    work = {
+        "g": local_grad, "c": join, "s": send_second, "l": send_line, "h": halve_line,
+        "f": finish_line, "n": lambda i: share_on(i, out_of(i), stage[i]),
+        "r": lambda _: ready(), "d": lambda _: take_context(), "a": attend_back,
+        "w": lambda _: weight_grads(), "t": send_tokens, "x": line_tokens,
+        "k": lambda n: (halve_tokens, finish_tokens)[n](),
+        "q": lambda n: (line_q, first_q, finish_q)[n](),
+        "v": lambda n: (sums_mate, sums_line, sums_first, sums_second, sums_last)[n](),
+    }
+    for entry in PLAN:
+        work[entry[0]](int(entry[1]))
+    for i in range(6):
+        shared(i, out_of(i), stage[i])
     links.arrive(halves.at[other_rows], slot_o, mate)
     links.drain()
-    vec[...] = vec_total
 
 
 def backward_links(
@@ -1357,7 +1422,7 @@
         shape((4, 2, part, 3 * wide), low),
         shape((rows, feat), low),
         shape((rows, feat), low),
-        shape(vec.shape, f32),
+        shape((40, features), f32),
     ]
     every = [(ROWS, width) for width in widths] + [(2, 3 * wide)]
     return pl.pallas_call(
@@ -1387,9 +1452,11 @@
             pltpu.VMEM((ROWS, 2, 2, part, 3 * wide), low),
             pltpu.VMEM((ROWS, 2, part, 3 * wide), low),
             pltpu.VMEM((2, 4, part, 3 * wide), low),
-            pltpu.VMEM(vec.shape, f32),
-            pltpu.VMEM((3,) + vec.shape, f32),
-            pltpu.VMEM((2,) + vec.shape, f32),
+            pltpu.VMEM((2, 16, features), f32),
+            pltpu.VMEM((16, features), f32),
+            pltpu.VMEM((3, 16, features), f32),
+            pltpu.VMEM((4, 8, features), f32),
+            pltpu.VMEM((4, 8, features), f32),
             pltpu.SemaphoreType.DMA((128,)),
             pltpu.SemaphoreType.DMA((128,)),
         ],
@@ -1411,7 +1478,7 @@
     out, logits, grad_x, o_q, o_bq, o_k, o_v, o_bv, o_o, o_bo, o_g1, o_s1, o_1, o_b1, o_2, o_b2,
     o_g2, o_s2, o_p, o_bp, o_c, o_bc,
 ):
-    dp, _, col = place()
+    dp = lax.axis_index("dp")
     f32 = jnp.float32
     wide = heads * HEAD
     classes = logits.shape[1]
@@ -1432,32 +1499,35 @@
             target[:, j * wide : (j + 1) * wide] = jnp.concatenate(
                 [value[:, 2 * h * HEAD + shift :][:, :HEAD] for h in range(heads)], axis=1
             )
-        bias = jnp.where(col == 0, vec[j : j + 1], vec[2 + j : 3 + j])
+        bias = vec[5 + j : 6 + j]
         bias_q.append(bias[:, 2 * wide : 3 * wide])
         bias_v += [bias[:, 2 * h * HEAD + HEAD :][:, :HEAD] for h in range(heads)]
     put_lanes(o_bq, jnp.concatenate(bias_q, axis=1))
     put_lanes(o_bv, jnp.concatenate(bias_v, axis=1))
-    own = jnp.where(col == 0, vec[8:16], vec[16:24])
+    own = vec[:8]
     for n, target in enumerate((o_bo, o_g1, o_s1, o_b2, o_g2, o_s2)):
         put_lanes(target, own[n // 2 : n // 2 + 1, (n % 2) * feat : (n % 2 + 1) * feat])
     put_lanes(o_b1, jnp.concatenate([own[3:4], own[4:5]], axis=1))
-    firsts, seconds = vec[24:32], vec[32:40]
-    first_t, second_t = firsts.T, seconds.T
+    table = vec[8:40]
+    table_t = table.T
     pooler = jnp.zeros(o_p.shape, f32)
-    head = jnp.zeros((o_p.shape[0], 128), f32)
+    head = [jnp.zeros((1, 2 * feat), f32) for _ in range(classes)]
     bias = jnp.zeros((1, 2 * feat), f32)
-    tails = seconds[4:8, :128]
+    ends = jnp.zeros((1, 128), f32)
+    own_tail = jnp.zeros((1, 128), f32)
     for s in range(4):
-        pooler = pooler + first_t[:, s : s + 1] * firsts[4 + s : 5 + s]
-        bias = bias + firsts[4 + s : 5 + s]
-        head = head + second_t[:, s : s + 1] * tails[s : s + 1]
+        at = 8 * s
+        slope, tail = table[at + 1 : at + 2], table[at + 3 : at + 4, :128]
+        pooler = pooler + table_t[:, at : at + 1] * slope
+        bias = bias + slope
+        for n in range(classes):
+            head[n] = head[n] + table[at + 2 : at + 3] * tail[:, classes + n : classes + n + 1]
+        ends = ends + tail
+        own_tail = jnp.where(dp == s, tail, own_tail)
     o_p[...] = pooler
     put_lanes(o_bp, bias)
-    o_c[...] = head[:, classes : 2 * classes]
-    o_bc[...] = jnp.sum(tails, axis=0, keepdims=True)[:, classes : 2 * classes]
-    own_tail = jnp.zeros((1, 128), f32)
-    for s in range(4):
-        own_tail = jnp.where(dp == s, tails[s : s + 1], own_tail)
+    o_c[...] = jnp.concatenate(head, axis=0)
+    o_bc[...] = ends[:, classes : 2 * classes]
     logits[...] = own_tail[:, :classes]
 
 
@@ -1475,7 +1545,7 @@
         square, vector(feat), square, square, vector(feat), square, vector(feat), vector(feat),
         vector(feat), shape((depth, hidden), f32), vector(hidden), shape((depth, hidden), f32),
         vector(feat), vector(feat), vector(feat), shape((features, features), f32),
-        vector(features), shape((features, classes), f32), vector(classes),
+        vector(features), shape((classes, features), f32), vector(classes),
     ]
     return pl.pallas_call(
         functools.partial(finish_kernel, heads),
@@ -1509,11 +1579,10 @@
 ):
     f32 = jnp.float32
     feat = layer_input.shape[1]
-    features = 2 * feat
-    hidden = b_inner.shape[0]
-    heads = features // HEAD // ROWS
+    heads = 2 * feat // HEAD // ROWS
     vectors = [
-        b_query, b_value, b_output, ln1_gain, ln1_bias, b_outer, ln2_gain, ln2_bias, b_inner
+        b_query, b_value, b_output, ln1_gain, ln1_bias, b_outer, ln2_gain, ln2_bias, b_inner,
+        b_pooler,
     ]
     count = sum(vector.shape[0] for vector in vectors) // feat
     padded, at = 0.0, 0
@@ -1523,18 +1592,11 @@
         padded = padded + jnp.pad(vector.astype(f32), (at, full - at - size))
         at += size
     (
-        x_all, cot, vec_all, w_heads, q, kv, kt, mixed, lse, context, w_o, w_1, w_2,
+        x_all, w_heads, q, kv, kt, mixed, lse, output, late, stream, grad_pre, branch_two, activ,
+        branch_one, context, grad_blocks, packed,
     ) = forward_links(
-        layer_input, cotangent, padded.reshape(-1, feat), w_query, w_key, w_value, block_ids,
-        [w_output.T, w_inner, w_outer.T],
-    )
-    w_o = w_o.reshape(features, features)
-    w_1 = w_1.reshape(features, 2 * hidden)
-    w_2 = w_2.reshape(features, 2 * hidden)
-    (
-        output, late, stream, grad_pre, branch_two, activ, branch_one, context, grad_blocks, packed
-    ) = middle(
-        context, cot, vec_all, labels, b_pooler, w_classes, b_classes, w_pooler, w_o, x_all, w_1, w_2
+        layer_input, cotangent, padded.reshape(-1, feat), w_query, w_key, w_value, block_ids, labels, w_classes,
+        b_classes, w_pooler, [w_output.T, w_inner, w_outer.T],
     )
     s_1a, s_2a, s_1b, s_2b, s_wo, s_q, grad_input, output, sums = backward_links(
         grad_blocks, output, late, stream, grad_pre, branch_two, activ, branch_one, context,
@@ -1542,7 +1604,7 @@
     )
     outs = finish((s_1a, s_1b, s_2a, s_2b, s_wo, s_q, grad_input, output, sums), w_classes.shape[1], heads)
     flat = (4, 7, 9, 10, 11, 13, 15, 16, 17, 19, 21)
-    turned = (8, 14)
+    turned = (8, 14, 20)
     return tuple(
         out.reshape(-1) if n in flat else out.T if n in turned else out
         for n, out in enumerate(outs)

time: 270 us -> 232 us (0.86)
  Pallas kernels: 263 us -> 229 us
  local copies, waits for them, and re-layouts: 3.62 us -> 0.61 us
    pallas_call x1, Pallas kernels: 149 us -> 121 us  [backward_links(): pl.pallas_call(functools.partial(backward_kernel, heads), out_shape=outs,...]
    pallas_call x1 -> x0, Pallas kernels: 16 us -> none  [middle(): pl.pallas_call(functools.partial(middle_kernel, heads), out_shape=[narrow...]
    pallas_call x1, Pallas kernels: 92 us -> 103 us  [forward_links(): pl.pallas_call(functools.partial(forward_kernel, widths, heads), out_shap...]
where the time goes in v4:
time: 232 us
  Pallas kernels  229 us (99%)
    pallas_call x1, Pallas kernels, backward_links(): pl.pallas_call(functools.partial(backward_kernel, heads), out_shape=outs,...  121 us
    pallas_call x1, Pallas kernels, forward_links(): pl.pallas_call(functools.partial(forward_kernel, widths, heads), out_shap...  103 us
    pallas_call x1, Pallas kernels, finish(): pl.pallas_call(functools.partial(finish_kernel, heads), out_shape=outs, i...  5.52 us

profile of v4, /device:TPU:0, one launch (start us, length us, event | category | flops | bytes accessed | tf_op | source)
XLA Modules:
  0.0 232.0 jit_solution(11034922483543152032)
XLA Ops:
  1.3 0.8 convert_add_fusion
  2.1 0.6 reshape.99.vec
  2.8 102.9 %forward_links.1 = (bf16[4,512,768]{2,1,0:T(8,128)(2,1)}, bf16[4,4,48,576]{3,2,1,0:T(8,128)(2,1)}, bf16[3,4,256,128]{3,2,1,0:T(8,128)(2,1)}, bf16[3,2048,128]{2,...) custom-call(bf16[512,384]{1,0:T(8,128)(2,1)} %x.21, ...), custom_call_target="tpu_custom_call" | custom-call | tf_op jit(solution)/shard_map/forward_links/pallas_call | solution.py:912
  105.6 120.6 %backward_links.1 = (bf16[4,48,768]{2,1,0:T(8,128)(2,1)}, bf16[4,48,768]{2,1,0:T(8,128)(2,1)}, bf16[4,48,768]{2,1,0:T(8,128)(2,1)}, bf16[4,48,768]{2,1,0:T(8,128...) custom-call(bf16[4,256,192]{2,1,0:T(8,128)(2,1)} %get-tuple-element., ...), custom_call_target="tpu_custom_call" | custom-call | tf_op jit(solution)/shard_map/backward_links/pallas_call | solution.py:1428
  226.3 5.5 %finish.1 = (bf16[512,384]{1,0:T(8,128)(2,1)}, f32[1,3]{1,0:T(1,128)}, bf16[512,384]{1,0:T(8,128)(2,1)}, f32[192,384]{1,0:T(8,128)}, f32[3,128]{1,0:T(4,128)}, /...) custom-call(bf16[4,48,768]{2,1,0:T(8,128)(2,1)} %get-tuple-element.8, ...), custom_call_target="tpu_custom_call" | custom-call | tf_op jit(solution)/shard_map/finish/pallas_call | solution.py:1550

commit v5 on v4

--- a/solution.py
+++ b/solution.py
@@ -488,20 +488,25 @@
 
 
 def forward_kernel(
-    widths, heads, x, cot, vec, wq, wk, wv, ids, labels, w_classes, b_classes, w_pooler, *refs
+    widths, heads, x, cot, vec, wq, wk, wv, ids, labels, w_classes, b_classes, pooler_far, *refs
 ):
     count = len(widths)
     shards, refs = refs[:count], refs[count:]
-    x_all, w_heads, q_out, kv_out, kt_out, mixed_out, lse_out = refs[:7]
+    far_outs = refs[:7] + refs[12:13] + refs[10:11]
     (
-        output, late, stream_out, grad_pre_out, branch_two_out, activ_out, branch_one_out,
-        context, grad_blocks, packed,
+        output, late, stream_out, _, branch_two_out, _, branch_one_out, context,
+        grad_blocks, packed,
     ) = refs[7:17]
     fulls, refs = refs[17 : 17 + count], refs[17 + count :]
     (
-        cot_own, vec_all, context_in, vt_out, ids_col, packs, low_out, slope, total, send, recv,
-        local,
+        x_all, w_heads, q_out, kv_out, kt_out, mixed_out, lse_out, activ_out, grad_pre_out,
+        cot_own, vec_all, context_in, vt_out, ids_col, packs, low_out, slope, total, w_pooler, send, recv, local,
     ) = refs
+    near_outs = (x_all, w_heads, q_out, kv_out, kt_out, mixed_out, lse_out, activ_out, grad_pre_out)
+    write_out = [
+        pltpu.make_async_copy(near, far, local.at[count + 11 + n])
+        for n, (near, far) in enumerate(zip(near_outs, far_outs))
+    ]
     dp, row, col = place()
     links = Links(send, recv)
     low = x.dtype
@@ -566,9 +571,18 @@
         mate,
     )
     links.push(vec, vec_all.at[col], mate_vec, mate)
-    cot_own[:, columns(col, feat)] = cot[pl.ds(pl.multiple_of(mine * half, 128), half)]
     vec_all[col] = vec[...]
-    x_all[row, :, columns(col, feat)] = x[...]
+    read_in = [
+        pltpu.make_async_copy(x, x_at(row), local.at[count + 8]),
+        pltpu.make_async_copy(
+            cot.at[pl.ds(pl.multiple_of(mine * half, 128), half)],
+            cot_own.at[:, columns(col, feat)],
+            local.at[count + 9],
+        ),
+        pltpu.make_async_copy(pooler_far, w_pooler, local.at[count + 10]),
+    ]
+    for copy in read_in:
+        copy.start()
     copies = [
         pltpu.make_async_copy(shards[i], row_at(i, row), local.at[i]) for i in range(count)
     ]
@@ -705,14 +719,14 @@
         lax.fori_loop(0, per_row, one_tile, 0)
 
     links.arrive(x_mate_at(row), mate_x, mate)
+    read_in[0].wait()
     project_keys(row)
+    w_first(1)
     x_step(3)
     for slot in (0, 2, 1):
         k = lax.rem(row + slot + 1, ROWS)
         links.arrive(x_mate_at(k), mate_x + 1 + slot, mate)
         project_keys(k)
-        if slot == 2:
-            w_first(1)
 
     def project_query(j, carry):
         block = 2 * j + lax.rem(j + col, 2)
@@ -727,6 +741,8 @@
 
     blocks = row_tiles // 2
     lax.fori_loop(0, blocks, project_query, 0)
+    for copy in write_out[:5]:
+        copy.start()
     w_first(2)
     for j in range(blocks):
         block = 2 * j + lax.rem(j + col, 2)
@@ -776,6 +792,8 @@
             w_second(3)
             w_mate(2, range(count))
 
+    for copy in write_out[5:7]:
+        copy.start()
     f32 = jnp.float32
     own, features = output.shape
     hidden = 2 * widths[1]
@@ -784,6 +802,8 @@
     part_of = lambda full, span: full[:, :, :, span].reshape(features, span.stop - span.start)
     vector = lambda n: jnp.concatenate([vec_all[0, n : n + 1], vec_all[1, n : n + 1]], axis=1)
     links.arrive(cot_own.at[:, columns(1 - col, feat)], mate_cot, mate)
+    read_in[1].wait()
+    read_in[2].wait()
     for slot in range(3):
         links.arrive(context_in.at[lax.rem(row + slot + 1, ROWS)], swap + slot, mate)
     context[...] = jnp.concatenate([context_in[r] for r in range(ROWS)], axis=1)
@@ -810,6 +830,7 @@
         half = 0.5 * (1.0 + lax.erf(pre_act * root_half))
         slope[:, span] = half + pre_act * inv_root_tau * jnp.exp(-0.5 * pre_act * pre_act)
         activ_out[:, span] = (pre_act * half).astype(low)
+    write_out[7].start()
     w_ready(2)
     for n in range(hidden // chunk):
         span = slice(n * chunk, (n + 1) * chunk)
@@ -860,6 +881,7 @@
         grad_pre_out[:, span] = grad_pre
         g_bias_one.append(tokens(grad_pre.astype(f32)))
         total[...] += nt(grad_pre_out[:, span], part_of(w_1, span))
+    write_out[8].start()
     grad_stream = late[...] + total[...]
     g_gain_one, g_shift_one = tokens(grad_stream * normed_one), tokens(grad_stream)
     grad_one = norm_rows_back(grad_stream, normed_one, inv_one, gain_one)
@@ -883,6 +905,8 @@
     tail = jnp.concatenate([jnp.where(lane < classes, logits, shifted), spare], axis=1)
     for n, value in enumerate((first[:1].astype(f32), grad_pool, pooled, tail)):
         packed[24 + n : 25 + n] = value * holder
+    for copy in write_out:
+        copy.wait()
     links.drain()
 
 
@@ -912,10 +936,11 @@
     return pl.pallas_call(
         functools.partial(forward_kernel, widths, heads),
         out_shape=shapes,
-        in_specs=[IN_VMEM] * 7 + [pl.BlockSpec(memory_space=pltpu.SMEM)]
-        + [IN_VMEM] * (3 + len(shards)),
-        out_specs=[IN_VMEM] * len(shapes),
+        in_specs=[IN_PLACE] * 2 + [IN_VMEM] * 5 + [pl.BlockSpec(memory_space=pltpu.SMEM)]
+        + [IN_VMEM] * 2 + [IN_PLACE] * (1 + len(shards)),
+        out_specs=[IN_PLACE] * 7 + [IN_VMEM] * 3 + [IN_PLACE, IN_VMEM, IN_PLACE] + [IN_VMEM] * 4,
         scratch_shapes=[pltpu.VMEM((ROWS, 4, part, 2 * width), low) for width in widths]
+        + [pltpu.VMEM(out.shape, out.dtype) for out in shapes[:7] + [broad, broad]]
         + [
             pltpu.VMEM((own, features), low),
             pltpu.VMEM((2,) + vec.shape, f32),
@@ -926,9 +951,10 @@
             pltpu.VMEM((blocks, TILE, wide), low),
             pltpu.VMEM((own, hidden), f32),
             pltpu.VMEM((own, features), f32),
+            pltpu.VMEM(w_pooler.shape, low),
             pltpu.SemaphoreType.DMA((160,)),
             pltpu.SemaphoreType.DMA((96,)),
-            pltpu.SemaphoreType.DMA((4,)),
+            pltpu.SemaphoreType.DMA((24,)),
         ],
         compiler_params=comm_params(1),
         name="forward_links",
@@ -974,32 +1000,32 @@
     "h1",
     "h0",
     "w0",
-    "t0",
     "s2",
-    "t1",
-    "t2",
-    "x0",
     "s3",
     "q0",
+    "t0",
+    "t1",
+    "x0",
+    "s4",
+    "t2",
+    "l2",
     "x1",
-    "s4",
+    "l3",
     "t3",
-    "v0",
-    "x2",
-    "l2",
-    "l3",
-    "l4",
-    "v1",
     "f0",
     "f1",
+    "v0",
+    "l4",
+    "x2",
+    "n0",
+    "n1",
+    "v1",
     "h2",
     "q1",
     "h3",
     "h4",
     "k0",
     "v2",
-    "n0",
-    "n1",
     "s5",
     "v3",
     "f2",
@@ -1017,8 +1043,8 @@
 
 
 def backward_kernel(
-    heads, blocks_in, output, late, stream, grad_pre, branch_two, activ, branch_one, context,
-    q, kv, kt, mixed, lse, ids, x_all, w_heads, vec_in, *refs,
+    heads, blocks_in, output, late_far, stream, pre_far, branch_two, activ_far, branch_one, context,
+    q_far, kv_far, kt_far, mixed_far, lse_far, ids, x_far, w_far, vec_in, *refs,
 ):
     out_g, refs = refs[:5], refs[5:]
     out_q, out_x, halves, vec, refs = refs[0], refs[1], refs[2], refs[3], refs[4:]
@@ -1029,8 +1055,16 @@
     lines, refs = refs[:5], refs[5:]
     (
         grad_ctx, both, delta, dq, dkv, grads, grads_t, w_t, turned, ids_col, dx, sum_x,
-        line_x, gq, sum_q, all_q, vec_own, vec_mate, vec_line, vec_flat, vec_table, send, recv,
+        line_x, gq, sum_q, all_q, vec_own, vec_mate, vec_line, vec_flat, vec_table,
+        w_heads, q, kv, kt, mixed, lse, x_all, grad_pre, activ, late, send, recv, local,
     ) = refs
+    nears = (w_heads, q, kv, kt, mixed, lse, x_all, grad_pre, activ, late)
+    fars = (w_far, q_far, kv_far, kt_far, mixed_far, lse_far, x_far, pre_far, activ_far, late_far)
+    reads = [
+        pltpu.make_async_copy(far, near, local.at[n]) for n, (far, near) in enumerate(zip(fars, nears))
+    ]
+    for n in (7, 8, 0, 1, 2, 3, 4, 5, 6, 9):
+        reads[n].start()
     dp, row, col = place()
     links = Links(send, recv)
     low, f32 = q.dtype, jnp.float32
@@ -1058,8 +1092,12 @@
     own_rows = pl.ds(pl.multiple_of(mine * half, 128), half)
     other_rows = pl.ds(pl.multiple_of((1 - mine) * half, 128), half)
     links.push(output.at[:, columns(1 - col, feat)], halves.at[own_rows], slot_o, mate)
-    halves[own_rows] = output[:, columns(col, feat)]
-    grad_ctx[row] = blocks_in[row]
+    reads += [
+        pltpu.make_async_copy(output.at[:, columns(col, feat)], halves.at[own_rows], local.at[10]),
+        pltpu.make_async_copy(blocks_in.at[row], grad_ctx.at[row], local.at[11]),
+    ]
+    reads[10].start()
+    reads[11].start()
 
     lefts = (stream, branch_two, branch_one)
     for n in range(3):
@@ -1070,6 +1108,8 @@
     slot_g = [links.slots(1) for _ in widths]
 
     def local_grad(i):
+        if i < 2:
+            reads[7 + i].wait()
         left, right, part = feeds[i]
         width = widths[i]
         per = width // CHUNK
@@ -1180,6 +1220,7 @@
         return carry
 
     def ready():
+        reads[0].wait()
         w_t[...] = w_heads[...].reshape(2 * feat, 3 * wide).astype(f32).T.astype(low)
         lax.fori_loop(0, row_tiles, split_ids, 0)
         dkv[...] = jnp.zeros_like(dkv)
@@ -1187,6 +1228,8 @@
     def take_context():
         for n, peer in enumerate(peers):
             links.arrive(grad_ctx.at[peer], swap + n, mate)
+        for copy in reads[1:6] + reads[11:]:
+            copy.wait()
         lax.fori_loop(0, blocks, split_grad, 0)
 
     def attend_back(j):
@@ -1232,6 +1275,9 @@
         return carry + jnp.sum(value, axis=0, keepdims=True)
 
     def weight_grads():
+        reads[6].wait()
+        reads[9].wait()
+        reads[10].wait()
         sums["q"] = lax.fori_loop(0, blocks, gather_q, jnp.zeros((1, wide), f32))
         sums["kv"] = lax.fori_loop(0, row_tiles, gather_kv, jnp.zeros((1, 2 * wide), f32))
         for n in range(2):
@@ -1428,7 +1474,8 @@
     return pl.pallas_call(
         functools.partial(backward_kernel, heads),
         out_shape=outs,
-        in_specs=[IN_VMEM] * 18,
+        in_specs=[IN_PLACE] * 3 + [IN_VMEM, IN_PLACE] * 2 + [IN_VMEM] * 2 + [IN_PLACE] * 5
+        + [IN_VMEM] + [IN_PLACE] * 2 + [IN_VMEM],
         out_specs=[IN_VMEM] * len(outs),
         scratch_shapes=[pltpu.VMEM((2, ROWS, 4, part, width), low) for width in widths]
         + [pltpu.VMEM((ROWS, 4, part, width), low) for width in widths]
@@ -1457,8 +1504,13 @@
             pltpu.VMEM((3, 16, features), f32),
             pltpu.VMEM((4, 8, features), f32),
             pltpu.VMEM((4, 8, features), f32),
+        ]
+        + [pltpu.VMEM(far.shape, far.dtype)
+            for far in (w_heads, q, kv, kt, mixed, lse, x_all, grad_pre, activ, late)]
+        + [
             pltpu.SemaphoreType.DMA((128,)),
             pltpu.SemaphoreType.DMA((128,)),
+            pltpu.SemaphoreType.DMA((12,)),
         ],
         compiler_params=comm_params(2),
         name="backward_links",
@@ -1475,8 +1527,8 @@
 
 def finish_kernel(
     heads, g1a, g1b, g2a, g2b, go, gq, x_in, out_in, vec,
-    out, logits, grad_x, o_q, o_bq, o_k, o_v, o_bv, o_o, o_bo, o_g1, o_s1, o_1, o_b1, o_2, o_b2,
-    o_g2, o_s2, o_p, o_bp, o_c, o_bc,
+    out, logits, grad_x, o_q, o_bq, o_k, o_v, o_bv, o_o, o_bo, o_g1, o_s1, far_1, o_b1, far_2, o_b2,
+    o_g2, o_s2, far_p, o_bp, o_c, o_bc, o_1, o_2, o_p, sems,
 ):
     dp = lax.axis_index("dp")
     f32 = jnp.float32
@@ -1484,12 +1536,35 @@
     classes = logits.shape[1]
     depth, feat = o_q.shape
     part = g1a.shape[2]
-    out[...] = out_in[...]
-    grad_x[...] = x_in[...]
+    write_out = [
+        pltpu.make_async_copy(near, far, sems.at[n])
+        for n, (near, far) in enumerate(((o_p, far_p), (o_1, far_1), (o_2, far_2)))
+    ]
+    table = vec[8:40]
+    table_t = table.T
+    pooler = jnp.zeros(o_p.shape, f32)
+    head = [jnp.zeros((1, 2 * feat), f32) for _ in range(classes)]
+    total = jnp.zeros((1, 2 * feat), f32)
+    ends = jnp.zeros((1, 128), f32)
+    own_tail = jnp.zeros((1, 128), f32)
+    for s in range(4):
+        at = 8 * s
+        slope, tail = table[at + 1 : at + 2], table[at + 3 : at + 4, :128]
+        pooler = pooler + table_t[:, at : at + 1] * slope
+        total = total + slope
+        for n in range(classes):
+            head[n] = head[n] + table[at + 2 : at + 3] * tail[:, classes + n : classes + n + 1]
+        ends = ends + tail
+        own_tail = jnp.where(dp == s, tail, own_tail)
+    o_p[...] = pooler
+    write_out[0].start()
     flat = lambda ref: ref[...].astype(f32).reshape(depth, ref.shape[2])
     for target, first, second in ((o_1, g1a, g1b), (o_2, g2a, g2b)):
         target[:, :part] = flat(first)
         target[:, part:] = flat(second)
+        write_out[1 if target is o_1 else 2].start()
+    out[...] = out_in[...]
+    grad_x[...] = x_in[...]
     o_o[...] = flat(go)
     bias_q, bias_v = [], []
     for j in range(2):
@@ -1508,27 +1583,12 @@
     for n, target in enumerate((o_bo, o_g1, o_s1, o_b2, o_g2, o_s2)):
         put_lanes(target, own[n // 2 : n // 2 + 1, (n % 2) * feat : (n % 2 + 1) * feat])
     put_lanes(o_b1, jnp.concatenate([own[3:4], own[4:5]], axis=1))
-    table = vec[8:40]
-    table_t = table.T
-    pooler = jnp.zeros(o_p.shape, f32)
-    head = [jnp.zeros((1, 2 * feat), f32) for _ in range(classes)]
-    bias = jnp.zeros((1, 2 * feat), f32)
-    ends = jnp.zeros((1, 128), f32)
-    own_tail = jnp.zeros((1, 128), f32)
-    for s in range(4):
-        at = 8 * s
-        slope, tail = table[at + 1 : at + 2], table[at + 3 : at + 4, :128]
-        pooler = pooler + table_t[:, at : at + 1] * slope
-        bias = bias + slope
-        for n in range(classes):
-            head[n] = head[n] + table[at + 2 : at + 3] * tail[:, classes + n : classes + n + 1]
-        ends = ends + tail
-        own_tail = jnp.where(dp == s, tail, own_tail)
-    o_p[...] = pooler
-    put_lanes(o_bp, bias)
+    put_lanes(o_bp, total)
     o_c[...] = jnp.concatenate(head, axis=0)
     o_bc[...] = ends[:, classes : 2 * classes]
     logits[...] = own_tail[:, :classes]
+    for copy in write_out:
+        copy.wait()
 
 
 def finish(pieces, classes, heads):
@@ -1551,7 +1611,9 @@
         functools.partial(finish_kernel, heads),
         out_shape=outs,
         in_specs=[IN_VMEM] * len(pieces),
-        out_specs=[IN_VMEM] * len(outs),
+        out_specs=[IN_PLACE if n in (12, 14, 18) else IN_VMEM for n in range(len(outs))],
+        scratch_shapes=[pltpu.VMEM(outs[n].shape, f32) for n in (12, 14, 18)]
+        + [pltpu.SemaphoreType.DMA((3,))],
         compiler_params=pltpu.CompilerParams(vmem_limit_bytes=VMEM_BYTES),
         name="finish",
     )(*pieces)

time: 232 us -> 223 us (0.961)
  Pallas kernels: 229 us -> 220 us
    pallas_call x1, Pallas kernels: 121 us -> 114 us  [backward_links(): pl.pallas_call(functools.partial(backward_kernel, heads), out_shape=outs,...]
    pallas_call x1, Pallas kernels: 103 us -> 99.3 us  [forward_links(): pl.pallas_call(functools.partial(forward_kernel, widths, heads), out_shap...]
where the time goes in v5:
time: 223 us; the launch traced here: 222 us
  Pallas kernels  220 us (99%)
    pallas_call x1, Pallas kernels, backward_links(): pl.pallas_call(functools.partial(backward_kernel, heads), out_shape=outs,...  114 us
    pallas_call x1, Pallas kernels, forward_links(): pl.pallas_call(functools.partial(forward_kernel, widths, heads), out_shap...  99.3 us
    pallas_call x1, Pallas kernels, finish(): pl.pallas_call(functools.partial(finish_kernel, heads), out_shape=outs, i...  6.29 us

profile of v5, /device:TPU:0, one launch (start us, length us, event | category | flops | bytes accessed | tf_op | source)
XLA Modules:
  0.0 222.5 jit_solution(8456057512247421628)
XLA Ops:
  1.3 0.8 convert_add_fusion
  2.1 0.6 reshape.99.vec
  2.8 99.3 %forward_links.1 = (bf16[4,512,768]{2,1,0:T(8,128)(2,1)}, bf16[4,4,48,576]{3,2,1,0:T(8,128)(2,1)}, bf16[3,4,256,128]{3,2,1,0:T(8,128)(2,1)}, bf16[3,2048,128]{2,...) custom-call(bf16[512,384]{1,0:T(8,128)(2,1)} %x.21, ...), custom_call_target="tpu_custom_call" | custom-call | tf_op jit(solution)/shard_map/forward_links/pallas_call | solution.py:936
  102.0 114.0 %backward_links.1 = (bf16[4,48,768]{2,1,0:T(8,128)(2,1)}, bf16[4,48,768]{2,1,0:T(8,128)(2,1)}, bf16[4,48,768]{2,1,0:T(8,128)(2,1)}, bf16[4,48,768]{2,1,0:T(8,128...) custom-call(bf16[4,256,192]{2,1,0:T(8,128)(2,1)} %get-tuple-element., ...), custom_call_target="tpu_custom_call" | custom-call | tf_op jit(solution)/shard_map/backward_links/pallas_call | solution.py:1474
  216.0 6.3 %finish.1 = (bf16[512,384]{1,0:T(8,128)(2,1)}, f32[1,3]{1,0:T(1,128)}, bf16[512,384]{1,0:T(8,128)(2,1)}, f32[192,384]{1,0:T(8,128)}, f32[3,128]{1,0:T(4,128)}, /...) custom-call(bf16[4,48,768]{2,1,0:T(8,128)(2,1)} %get-tuple-element.8, ...), custom_call_target="tpu_custom_call" | custom-call | tf_op jit(solution)/shard_map/finish/pallas_call | solution.py:1610

commit v6 on v5

--- a/solution.py
+++ b/solution.py
@@ -538,10 +538,10 @@
     steps = list(steps_of_line(row))
     at_step = lambda step: [entry[2:] for entry in steps if entry[0] == step]
 
-    def relay(step, own, full, base):
+    def relay(step, own, full, base, group=True):
         for way in (1, -1):
             held, onward = row - way * (step - 1), row + way
-            ok = within(held) & within(onward)
+            ok = within(held) & within(onward) & group
             slot = 3 - step if way == 1 else step - 1
             links.push(own if step == 1 else full(held), full(held), base + slot, at_row(onward), ok)
 
@@ -635,36 +635,57 @@
                     shards[i].at[dp], w_at(i, row, dp), line_w[i] + slot, at_row(row + way), ok
                 )
 
-    def w_first(step):
+    inner = (row == 1) | (row == 2)
+    groups = {"i": inner, "o": jnp.logical_not(inner)}
+
+    def w_first(step, group):
         for i in range(count):
             for slot, k, ok in at_step(step):
-                links.arrive(w_at(i, k, dp), line_w[i] + slot, mate, ok)
+                links.arrive(w_at(i, k, dp), line_w[i] + slot, mate, ok & group)
             if step < 3:
-                relay(step + 1, None, lambda k, i=i: w_at(i, k, dp), line_w[i])
+                relay(step + 1, None, lambda k, i=i: w_at(i, k, dp), line_w[i], group)
             for slot, k, ok in at_step(step):
                 one, two = turn(i, slot)
-                links.push(w_at(i, k, dp), w_at(i, k, dp), first_w[i] + slot, at_dp(one), ok)
-
-    def w_second(step):
+                links.push(
+                    w_at(i, k, dp), w_at(i, k, dp), first_w[i] + slot, at_dp(one), ok & group
+                )
+
+    def w_second(step, group):
         for i in range(count):
             for slot, k, ok in at_step(step):
                 one, two = turn(i, slot)
-                links.arrive(w_at(i, k, dp ^ one), first_w[i] + slot, mate, ok)
+                links.arrive(w_at(i, k, dp ^ one), first_w[i] + slot, mate, ok & group)
                 for n, q in enumerate((dp, dp ^ one)):
                     links.push(
-                        w_at(i, k, q), w_at(i, k, q), second_w[i] + 2 * slot + n, at_dp(two), ok
+                        w_at(i, k, q), w_at(i, k, q), second_w[i] + 2 * slot + n, at_dp(two),
+                        ok & group,
                     )
 
-    def w_mate(step, items):
+    def w_mate(step, group, items):
         for i in items:
             for slot, k, ok in at_step(step):
                 one, two = turn(i, slot)
-                links.arrive(w_at(i, k, dp ^ two), second_w[i] + 2 * slot, mate, ok)
-                links.arrive(w_at(i, k, dp ^ 3), second_w[i] + 2 * slot + 1, mate, ok)
-                links.push(row_at(i, k), row_at(i, k), mate_w[i] + 1 + slot, mate, ok)
+                links.arrive(
+                    w_at(i, k, dp ^ two), second_w[i] + 2 * slot, mate, ok & group
+                )
+                links.arrive(
+                    w_at(i, k, dp ^ 3), second_w[i] + 2 * slot + 1, mate, ok & group
+                )
+                links.push(row_at(i, k), row_at(i, k), mate_w[i] + 1 + slot, mate, ok & group)
+
+    def advance(point):
+        for entry in FLOW[point]:
+            step, group = int(entry[1]), groups[entry[2]]
+            if entry[0] == "f":
+                w_first(step, group)
+            elif entry[0] == "s":
+                w_second(step, group)
+            else:
+                w_mate(step, group, range(count))
 
     def w_ready(i):
-        w_mate(3, (i,))
+        for entry in FLOW["end"]:
+            w_mate(int(entry[1]), groups[entry[2]], (i,))
         copies[i].wait()
         links.arrive(row_mate_at(i, row), mate_w[i], mate)
         for slot in range(3):
@@ -721,7 +742,7 @@
     links.arrive(x_mate_at(row), mate_x, mate)
     read_in[0].wait()
     project_keys(row)
-    w_first(1)
+    advance("x2")
     x_step(3)
     for slot in (0, 2, 1):
         k = lax.rem(row + slot + 1, ROWS)
@@ -743,7 +764,7 @@
     lax.fori_loop(0, blocks, project_query, 0)
     for copy in write_out[:5]:
         copy.start()
-    w_first(2)
+    advance("pq")
     for j in range(blocks):
         block = 2 * j + lax.rem(j + col, 2)
         rows = pl.ds(pl.multiple_of(block * TILE, TILE), TILE)
@@ -782,15 +803,7 @@
         def _(j=j):
             context_in[row] = low_out[j]
 
-        if j == 0:
-            w_second(1)
-        if j == 1:
-            w_first(3)
-            w_second(2)
-            w_mate(1, range(count))
-        if j == 2:
-            w_second(3)
-            w_mate(2, range(count))
+        advance("a%d" % j)
 
     for copy in write_out[5:7]:
         copy.start()
@@ -952,7 +965,7 @@
             pltpu.VMEM((own, hidden), f32),
             pltpu.VMEM((own, features), f32),
             pltpu.VMEM(w_pooler.shape, low),
-            pltpu.SemaphoreType.DMA((160,)),
+            pltpu.SemaphoreType.DMA((256,)),
             pltpu.SemaphoreType.DMA((96,)),
             pltpu.SemaphoreType.DMA((24,)),
         ],
@@ -976,6 +989,15 @@
 
 
 CHUNK = 384
+FLOW = {
+    "x2": ("f1i",),
+    "pq": ("f2i",),
+    "a0": ("s1i",),
+    "a1": ("s2i", "m1i", "f1o",),
+    "a2": ("m2i", "f2o", "s1o",),
+    "a3": ("f3o", "s2o", "m1o", "s3o", "m2o",),
+    "end": ("m3o",),
+}
 PLAN = (
     "g0",
     "g1",

time: 223 us -> 219 us (0.982)
  Pallas kernels: 220 us -> 216 us
    pallas_call x1, Pallas kernels: 114 us -> 109 us  [backward_links(): pl.pallas_call(functools.partial(backward_kernel, heads), out_shape=outs,...]
where the time goes in v6:
time: 219 us
  Pallas kernels  216 us (99%)
    pallas_call x1, Pallas kernels, backward_links(): pl.pallas_call(functools.partial(backward_kernel, heads), out_shape=outs,...  109 us
    pallas_call x1, Pallas kernels, forward_links(): pl.pallas_call(functools.partial(forward_kernel, widths, heads), out_shap...  100 us
    pallas_call x1, Pallas kernels, finish(): pl.pallas_call(functools.partial(finish_kernel, heads), out_shape=outs, i...  6.29 us

profile of v6, /device:TPU:0, one launch (start us, length us, event | category | flops | bytes accessed | tf_op | source)
XLA Modules:
  0.0 218.9 jit_solution(16153257166429825572)
XLA Ops:
  1.3 0.8 convert_add_fusion
  2.1 0.6 reshape.99.vec
  2.8 100.3 %forward_links.1 = (bf16[4,512,768]{2,1,0:T(8,128)(2,1)}, bf16[4,4,48,576]{3,2,1,0:T(8,128)(2,1)}, bf16[3,4,256,128]{3,2,1,0:T(8,128)(2,1)}, bf16[3,2048,128]{2,...) custom-call(bf16[512,384]{1,0:T(8,128)(2,1)} %x.21, ...), custom_call_target="tpu_custom_call" | custom-call | tf_op jit(solution)/shard_map/forward_links/pallas_call | solution.py:949
  103.1 109.3 %backward_links.1 = (bf16[4,48,768]{2,1,0:T(8,128)(2,1)}, bf16[4,48,768]{2,1,0:T(8,128)(2,1)}, bf16[4,48,768]{2,1,0:T(8,128)(2,1)}, bf16[4,48,768]{2,1,0:T(8,128...) custom-call(bf16[4,256,192]{2,1,0:T(8,128)(2,1)} %get-tuple-element., ...), custom_call_target="tpu_custom_call" | custom-call | tf_op jit(solution)/shard_map/backward_links/pallas_call | solution.py:1496
  212.4 6.3 %finish.1 = (bf16[512,384]{1,0:T(8,128)(2,1)}, f32[1,3]{1,0:T(1,128)}, bf16[512,384]{1,0:T(8,128)(2,1)}, f32[192,384]{1,0:T(8,128)}, f32[3,128]{1,0:T(4,128)}, /...) custom-call(bf16[4,48,768]{2,1,0:T(8,128)(2,1)} %get-tuple-element.8, ...), custom_call_target="tpu_custom_call" | custom-call | tf_op jit(solution)/shard_map/finish/pallas_call | solution.py:1632

commit v7 on v6

--- a/solution.py
+++ b/solution.py
@@ -991,9 +991,9 @@
 CHUNK = 384
 FLOW = {
     "x2": ("f1i",),
-    "pq": ("f2i",),
-    "a0": ("s1i",),
-    "a1": ("s2i", "m1i", "f1o",),
+    "pq": ("f2i", "s1i",),
+    "a0": ("s2i",),
+    "a1": ("m1i", "f1o",),
     "a2": ("m2i", "f2o", "s1o",),
     "a3": ("f3o", "s2o", "m1o", "s3o", "m2o",),
     "end": ("m3o",),
@@ -1015,13 +1015,13 @@
     "a1",
     "c3",
     "a2",
+    "c4",
+    "a3",
     "l1",
     "l0",
-    "c4",
-    "a3",
+    "w0",
     "h1",
     "h0",
-    "w0",
     "s2",
     "s3",
     "q0",

time: 219 us -> 219 us (level)
  no operation moved by 1% of the time
where the time goes in v7:
time: 219 us
  Pallas kernels  216 us (99%)
    pallas_call x1, Pallas kernels, backward_links(): pl.pallas_call(functools.partial(backward_kernel, heads), out_shape=outs,...  109 us
    pallas_call x1, Pallas kernels, forward_links(): pl.pallas_call(functools.partial(forward_kernel, widths, heads), out_shap...  100 us
    pallas_call x1, Pallas kernels, finish(): pl.pallas_call(functools.partial(finish_kernel, heads), out_shape=outs, i...  6.29 us

profile of v7, /device:TPU:0, one launch (start us, length us, event | category | flops | bytes accessed | tf_op | source)
XLA Modules:
  0.0 218.9 jit_solution(17620414171568361249)
XLA Ops:
  1.3 0.8 convert_add_fusion
  2.1 0.6 reshape.99.vec
  2.8 100.3 %forward_links.1 = (bf16[4,512,768]{2,1,0:T(8,128)(2,1)}, bf16[4,4,48,576]{3,2,1,0:T(8,128)(2,1)}, bf16[3,4,256,128]{3,2,1,0:T(8,128)(2,1)}, bf16[3,2048,128]{2,...) custom-call(bf16[512,384]{1,0:T(8,128)(2,1)} %x.21, ...), custom_call_target="tpu_custom_call" | custom-call | tf_op jit(solution)/shard_map/forward_links/pallas_call | solution.py:949
  103.1 109.3 %backward_links.1 = (bf16[4,48,768]{2,1,0:T(8,128)(2,1)}, bf16[4,48,768]{2,1,0:T(8,128)(2,1)}, bf16[4,48,768]{2,1,0:T(8,128)(2,1)}, bf16[4,48,768]{2,1,0:T(8,128...) custom-call(bf16[4,256,192]{2,1,0:T(8,128)(2,1)} %get-tuple-element., ...), custom_call_target="tpu_custom_call" | custom-call | tf_op jit(solution)/shard_map/backward_links/pallas_call | solution.py:1496
  212.4 6.3 %finish.1 = (bf16[512,384]{1,0:T(8,128)(2,1)}, f32[1,3]{1,0:T(1,128)}, bf16[512,384]{1,0:T(8,128)(2,1)}, f32[192,384]{1,0:T(8,128)}, f32[3,128]{1,0:T(4,128)}, /...) custom-call(bf16[4,48,768]{2,1,0:T(8,128)(2,1)} %get-tuple-element.8, ...), custom_call_target="tpu_custom_call" | custom-call | tf_op jit(solution)/shard_map/finish/pallas_call | solution.py:1632
